TPU v7x, 32 devices: a whole 2x2x4 slice. The times are simulated.
32 devices in a mesh: dp: 2 (over x), fsdp: 16 (over z, y, core).
Axes of the slice: x: 2, y: 2, z: 4, core: 2. Of those that a mesh axis runs over, the one named last changes fastest.
Arguments:
- image_tokens: bfloat16 [1024, 50, 768], P(('dp', 'fsdp')), may hold values from -6 to 6
- text_tokens: bfloat16 [1024, 16, 768], P(('dp', 'fsdp')), may hold values from -6 to 6
- image_qkv: bfloat16 [768, 2304], replicated, may hold values from -0.21875 to 0.21875
- image_out: bfloat16 [768, 768], replicated, may hold values from -1.25 to 1.25
- image_up: bfloat16 [768, 3072], replicated, may hold values from -0.21875 to 0.21875
- image_down: bfloat16 [3072, 768], replicated, may hold values from -0.109375 to 0.109375
- image_vectors: bfloat16 [8, 768], replicated, may hold values from -1.2 to 1.5
- image_up_bias: bfloat16 [3072], replicated, may hold values from -2 to 2
- text_qkv: bfloat16 [768, 2304], P('fsdp', 'dp'), may hold values from -0.21875 to 0.21875
- text_out: bfloat16 [768, 768], P('fsdp', 'dp'), may hold values from -0.875 to 0.875
- text_up: bfloat16 [768, 3072], P('fsdp', 'dp'), may hold values from -0.21875 to 0.21875
- text_down: bfloat16 [3072, 768], P('fsdp', 'dp'), may hold values from -0.109375 to 0.109375
- text_vectors: bfloat16 [8, 768], P(None, 'fsdp'), may hold values from -1.2 to 1.5
- text_up_bias: bfloat16 [3072], P('fsdp'), may hold values from -2 to 2
- pair_counts: int32 [32], replicated, may hold values from 8 to 32, as said below
- pair_groups: int32 [1024], replicated, may hold values from 0 to 511
Outputs:
- loss_value: float32 [], replicated
- grad_text_tokens: float32 [1024, 16, 768], P(('dp', 'fsdp'))
- grad_text_qkv: float32 [768, 2304], P('fsdp', 'dp')
- grad_text_out: float32 [768, 768], P('fsdp', 'dp')
- grad_text_up: float32 [768, 3072], P('fsdp', 'dp')
- grad_text_down: float32 [3072, 768], P('fsdp', 'dp')
- grad_text_vectors: float32 [8, 768], P(None, 'fsdp')
- grad_text_up_bias: float32 [3072], P('fsdp')
Inputs may be any that keep to these rules, and one draw needn't show every extreme that they name: Device d (index over dp+fsdp, dp slowest) has its first pair_counts[d] of its 32 pair slots live; some device is full.
All inputs are finite; a program needn't handle non-finite values.
Results may differ from a plain program's by a relative error of at most 0.024.
Values may be sent and summed in bfloat16 or wider, within the bound.
No kernel may reach another device: no remote copies, remote signals or barrier semaphores. Data moves between devices by JAX's collectives and lax.ppermute only.
A program may use at most 192 MiB of HBM per device.

v0:
```python
import functools

import jax
import jax.numpy as jnp
from jax import lax
from jax.experimental import pallas as pl
from jax.experimental.pallas import tpu as pltpu
from jax.sharding import PartitionSpec as P

HEAD_DIM = 64
LOGIT_SCALE = 50.0
LOSS_WEIGHT = 32768.0
BF = jnp.bfloat16
F32 = jnp.float32
AXES = ("dp", "fsdp")
PX, PF = 2, 16
VMEM_LIMIT = 62 * 1024 * 1024

ANY = pl.BlockSpec(memory_space=pl.ANY)
WHOLE = pl.BlockSpec(memory_space=pltpu.VMEM)


def params(**more):
    return pltpu.CompilerParams(vmem_limit_bytes=VMEM_LIMIT, **more)


def dot(a, b, ca=1, cb=0):
    return lax.dot_general(a, b, (((ca,), (cb,)), ((), ())), preferred_element_type=F32)


def repeat(count, step, together=1):
    def turn(j, _):
        for k in range(together):
            step(j * together + k)
        return 0

    if together >= count:
        for i in range(count):
            step(i)
    else:
        lax.fori_loop(0, count // together, turn, 0)


def normalize(values):
    centered = values - jnp.mean(values, axis=-1, keepdims=True)
    inverse = lax.rsqrt(jnp.mean(centered * centered, axis=-1, keepdims=True) + 1e-05)
    return centered * inverse, inverse


def norm_back(grad, hat, inverse, gain):
    scaled = grad * gain
    return inverse * (
        scaled
        - jnp.mean(scaled, axis=-1, keepdims=True)
        - hat * jnp.mean(scaled * hat, axis=-1, keepdims=True)
    )


def gauss_tail(u):
    size = jnp.abs(u)
    t = 1.0 / (1.0 + (0.3275911 * 0.7071067811865476) * size)
    bell = jnp.exp(-0.5 * (u * u))
    poly = 0.5 * 1.061405429 * t - 0.5 * 1.453152027
    poly = poly * t + 0.5 * 1.421413741
    poly = poly * t - 0.5 * 0.284496736
    poly = poly * t + 0.5 * 0.254829592
    return poly * t * bell, bell, size


def head_pair(block, low_lane):
    zero = jnp.zeros_like(block)
    return jnp.concatenate(
        [jnp.where(low_lane, block, zero), jnp.where(low_lane, zero, block)], axis=0
    )


def softmax_half(scores, bias):
    scores = scores + bias
    top = jnp.max(scores, axis=-1, keepdims=True)
    powers = jnp.exp(scores - top)
    return powers * (1.0 / jnp.sum(powers, axis=-1, keepdims=True))


def unit_rows(pooled):
    return pooled * lax.rsqrt(jnp.sum(pooled * pooled, axis=-1, keepdims=True) + 1e-06)


def mean_down(total, count, down):
    mean = total * (1.0 / count)
    high = mean.astype(BF)
    low = (mean - high.astype(F32)).astype(BF)
    both = dot(jnp.concatenate([high, low], axis=0), down)
    return both[: mean.shape[0]] + both[mean.shape[0] :]


def image_kernel(
    tok, wq_h, wo_h, wu_h, wd_h, vec, ub, out, wq, wo, wu, wd, x, h, qkv, att, act_sum, r1_sum, bias_row, stage, sem
):
    step, steps = pl.program_id(0), pl.num_programs(0)
    length, group, width = tok.shape
    rows = group * length
    hidden = wu.shape[1]
    copies = [
        pltpu.make_async_copy(src, dst, sem.at[i])
        for i, (src, dst) in enumerate(((wq_h, wq), (wo_h, wo), (wu_h, wu), (wd_h, wd)))
    ]

    @pl.when(step == 0)
    def _():
        for copy in copies:
            copy.start()

    def arrived(i):
        @pl.when(step == 0)
        def _():
            copies[i].wait()

    v = vec[...].astype(F32)
    bias_row[:, :width] = v[2:3]
    bias_row[:, width : 2 * width] = jnp.zeros((1, width), F32)
    bias_row[:, 2 * width :] = v[3:4]
    for k in range(width // 128):
        stage[k] = tok[:, :, k * 128 : (k + 1) * 128].astype(F32).reshape(rows, 128)
        for i in range(group):
            x[pl.ds(i * length, length), k * 128 : (k + 1) * 128] = stage[k, pl.ds(i, length, stride=group), :]

    def norm_rows(gain, shift):
        blk = 80

        def one(i):
            at = pl.ds(pl.multiple_of(i * blk, blk), blk)
            hat, _ = normalize(x[at, :])
            h[at, :] = (hat * gain + shift).astype(BF)

        repeat(rows // blk, one, 5)

    norm_rows(v[0:1], v[1:2])
    arrived(0)

    def project(i):
        at = pl.ds(pl.multiple_of(i * 256, 256), 256)
        qkv[:, at] = (dot(h[...], wq[:, at]) + bias_row[:, at]).astype(BF)

    repeat(3 * width // 256, project, 3)

    wins = rows // (2 * length)
    q_len = 112
    low_lane = lax.broadcasted_iota(jnp.int32, (128, 128), 1) < HEAD_DIM
    cols = range(0, width, 128)

    def window(w):
        q_at = pl.multiple_of((2 * length * w) // 16 * 16, 16)
        k_at = pl.multiple_of(jnp.minimum(q_at, rows - 128), 16)
        lo, mid, hi = 2 * w * length, (2 * w + 1) * length, (2 * w + 2) * length
        qi = q_at + lax.broadcasted_iota(jnp.int32, (q_len, 128), 0)
        ki = k_at + lax.broadcasted_iota(jnp.int32, (q_len, 128), 1)
        first = (qi >= lo) & (qi < mid) & (ki >= lo) & (ki < mid)
        second = (qi >= mid) & (qi < hi) & (ki >= mid) & (ki < hi)
        bias = jnp.where(first | second, 0.0, -1e30)
        q_rows, k_rows = pl.ds(q_at, q_len), pl.ds(k_at, 128)
        q2 = [qkv[q_rows, c : c + 128] * 0.125 for c in cols]
        k2 = [head_pair(qkv[k_rows, width + c : width + c + 128], low_lane) for c in cols]
        v2 = [head_pair(qkv[k_rows, 2 * width + c : 2 * width + c + 128], low_lane) for c in cols]
        scores = [dot(q, k, 1, 1) for q, k in zip(q2, k2)]
        probs = [
            jnp.concatenate(
                [softmax_half(s[:, :128], bias).astype(BF), softmax_half(s[:, 128:], bias).astype(BF)],
                axis=1,
            )
            for s in scores
        ]
        mine = (q_at + lax.broadcasted_iota(jnp.int32, (16, 128), 0)) >= lo
        for c, p, values in zip(cols, probs, v2):
            mixed = dot(p, values)
            old = att[pl.ds(q_at, 16), c : c + 128].astype(F32)
            att[pl.ds(q_at, 16), c : c + 128] = jnp.where(mine, mixed[:16], old).astype(BF)
            att[pl.ds(q_at + 16, q_len - 16), c : c + 128] = mixed[16:].astype(BF)

    repeat(wins, window, 2)

    arrived(1)
    for c in range(0, width, 256):
        x[:, c : c + 256] = x[:, c : c + 256] + (dot(att[...], wo[:, c : c + 256]) + v[4:5, c : c + 256])
    norm_rows(v[5:6], v[6:7])

    def image_sums(values):
        sums = []
        for i in range(group):
            lo, hi = i * length, (i + 1) * length
            a, b = lo // 8 * 8, -(-hi // 8) * 8
            part = values[a:b]
            row = a + lax.broadcasted_iota(jnp.int32, (b - a, 1), 0)
            if lo % 8 or hi % 8:
                part = jnp.where((row >= lo) & (row < hi), part, 0.0)
            sums.append(jnp.sum(part, axis=0, keepdims=True))
        return jnp.concatenate(sums, axis=0)

    place = pl.ds(pl.multiple_of(step * group, group), group)
    for c in range(0, width, 256):
        r1_sum[place, c : c + 256] = image_sums(x[:, c : c + 256])
    arrived(2)

    def expand(i):
        at = pl.ds(pl.multiple_of(i * 256, 256), 256)
        u = dot(h[...], wu[:, at]) + ub[:, at].astype(F32)
        tail, _, size = gauss_tail(u)
        act_sum[place, at] = image_sums(jnp.maximum(u, 0.0) - size * tail)

    repeat(hidden // 256, expand, 3)
    arrived(3)

    @pl.when(step == steps - 1)
    def _():
        pooled = r1_sum[...] * (1.0 / length) + mean_down(act_sum[...], length, wd[...]) + v[7:8]
        out[...] = unit_rows(pooled).astype(BF)


def image_forward(tokens, wq, wo, wu, wd, vec, ub):
    pairs, length, width = tokens.shape
    hidden = wu.shape[1]
    group = 16
    rows = group * length
    return pl.pallas_call(
        image_kernel,
        name="image_forward",
        grid=(pairs // group,),
        in_specs=[
            pl.BlockSpec((length, group, width), lambda i: (0, i, 0)),
            ANY,
            ANY,
            ANY,
            ANY,
            pl.BlockSpec((8, width), lambda i: (0, 0)),
            pl.BlockSpec((1, hidden), lambda i: (0, 0)),
        ],
        out_specs=pl.BlockSpec((pairs, width), lambda i: (0, 0)),
        out_shape=jax.ShapeDtypeStruct((pairs, width), BF),
        scratch_shapes=[
            pltpu.VMEM((width, 3 * width), BF),
            pltpu.VMEM((width, width), BF),
            pltpu.VMEM((width, hidden), BF),
            pltpu.VMEM((hidden, width), BF),
            pltpu.VMEM((rows, width), F32),
            pltpu.VMEM((rows, width), BF),
            pltpu.VMEM((rows, 3 * width), BF),
            pltpu.VMEM((rows, width), BF),
            pltpu.VMEM((pairs, hidden), F32),
            pltpu.VMEM((pairs, width), F32),
            pltpu.VMEM((1, 3 * width), F32),
            pltpu.VMEM((width // 128, rows, 128), F32),
            pltpu.SemaphoreType.DMA((4,)),
        ],
        compiler_params=params(),
        cost_estimate=pl.CostEstimate(
            flops=2 * pairs * length * width * (4 * width + hidden),
            bytes_accessed=2 * (4 * width * width + 2 * width * hidden + pairs * length * width),
            transcendentals=pairs * length * hidden,
        ),
    )(jnp.swapaxes(tokens, 0, 1), wq, wo, wu, wd, vec, ub.reshape(1, hidden))


def pack_rows(width, hidden):
    piece, rows = width // PX, width // PF
    return piece, rows, hidden // PF


def weight_copies(packed, which, dst, sem, base, width, hidden):
    piece, rows, frows = pack_rows(width, hidden)
    q_pieces, u_pieces = 3, hidden // width
    spans = {
        "qkv": (0, q_pieces, rows),
        "out": (q_pieces * rows, 1, rows),
        "up": ((q_pieces + 1) * rows, u_pieces, rows),
        "down": ((q_pieces + 1 + u_pieces) * rows, 1, frows),
    }
    start, count, tall = spans[which]
    copies = []
    for x in range(PX):
        for p in range(count):
            copies.append(
                pltpu.make_async_copy(
                    packed.at[pl.ds(x * PF, PF), pl.ds(start + p * tall, tall), :],
                    dst.at[:, :, pl.ds((x * count + p) * piece, piece)],
                    sem.at[base + len(copies)],
                )
            )
    return copies


def natural(ref):
    blocks, rows, cols = ref.shape
    return ref[...].reshape(blocks * rows, cols)


def weight_scratch(which, width, hidden):
    rows, frows = width // PF, hidden // PF
    shape = {
        "qkv": (PF, rows, 3 * width),
        "out": (PF, rows, width),
        "up": (PF, rows, hidden),
        "down": (PF, frows, width),
    }[which]
    return pltpu.VMEM(shape, BF)


def text_mask(size, length):
    row = lax.broadcasted_iota(jnp.int32, (size, size), 0) // length
    col = lax.broadcasted_iota(jnp.int32, (size, size), 1) // length
    return jnp.where(row == col, 0.0, -1e30)


def text_forward_kernel(
    length, tok, packed, vec, ub, h1, qkv, att, r1, h2, slope, acts, pooled_out, low, wq, wo, wu, wd, total,
    bias_row, sem
):
    rows, width = tok.shape
    hidden = slope.shape[1]
    texts = rows // length
    load = {}
    base = 0
    for which, dst in (("qkv", wq), ("out", wo), ("up", wu), ("down", wd)):
        load[which] = weight_copies(packed, which, dst, sem, base, width, hidden)
        base += len(load[which])
        for copy in load[which]:
            copy.start()
    v = vec[...].astype(F32)
    bias_row[:, :width] = v[2:3]
    bias_row[:, width : 2 * width] = jnp.zeros((1, width), F32)
    bias_row[:, 2 * width :] = v[3:4]
    blk = 128

    def norm_rows(src, dst, gain, shift):
        def one(i):
            at = pl.ds(pl.multiple_of(i * blk, blk), blk)
            hat, _ = normalize(src[at, :].astype(F32))
            dst[at, :] = (hat * gain + shift).astype(BF)

        repeat(rows // blk, one, 2)

    norm_rows(tok, h1, v[0:1], v[1:2])
    for copy in load["qkv"]:
        copy.wait()

    def project(i):
        at = pl.ds(pl.multiple_of(i * 256, 256), 256)
        qkv[:, at] = (dot(h1[...], wq[:, :, at].reshape(width, 256)) + bias_row[:, at]).astype(BF)

    repeat(3 * width // 256, project, 3)
    low_lane = lax.broadcasted_iota(jnp.int32, (blk, 128), 1) < HEAD_DIM
    bias = text_mask(blk, length)
    cols = range(0, width, 128)

    def attend(i):
        at = pl.ds(pl.multiple_of(i * blk, blk), blk)
        q2 = [qkv[at, c : c + 128] * 0.125 for c in cols]
        k2 = [head_pair(qkv[at, width + c : width + c + 128], low_lane) for c in cols]
        v2 = [head_pair(qkv[at, 2 * width + c : 2 * width + c + 128], low_lane) for c in cols]
        scores = [dot(q, k, 1, 1) for q, k in zip(q2, k2)]
        probs = [
            jnp.concatenate(
                [softmax_half(s[:, :blk], bias).astype(BF), softmax_half(s[:, blk:], bias).astype(BF)],
                axis=1,
            )
            for s in scores
        ]
        for c, p, values in zip(cols, probs, v2):
            att[at, c : c + 128] = dot(p, values).astype(BF)

    repeat(rows // blk, attend, 2)
    for copy in load["out"]:
        copy.wait()
    for c in range(0, width, 256):
        r1[:, c : c + 256] = tok[:, c : c + 256].astype(F32) + (
            dot(att[...], wo[:, :, c : c + 256].reshape(width, 256)) + v[4:5, c : c + 256]
        )
    norm_rows(r1, h2, v[5:6], v[6:7])
    for copy in load["up"]:
        copy.wait()

    def expand(i):
        at = pl.ds(pl.multiple_of(i * 256, 256), 256)
        u = dot(h2[...], wu[:, :, at].reshape(width, 256)) + ub[:, at].astype(F32)
        tail, bell, size = gauss_tail(u)
        act = jnp.maximum(u, 0.0) - size * tail
        phi = jnp.where(u >= 0.0, 1.0 - tail, tail)
        slope[:, at] = (phi + u * (bell * 0.3989422804014327)).astype(BF)
        sums = jnp.sum(act.reshape(texts, length, 256), axis=1)
        total[:, at] = sums
        acts[:, at] = sums.astype(BF)

    repeat(hidden // 256, expand, 3)
    for copy in load["down"]:
        copy.wait()
    mean_r1 = jnp.sum(r1[...].reshape(texts, length, width), axis=1) * (1.0 / length)
    pooled = mean_r1 + mean_down(total[...], length, natural(wd)) + v[7:8]
    pooled_out[...] = pooled
    low[...] = unit_rows(pooled).astype(BF)


def text_forward(tokens, packed, vec, ub, length, hidden):
    rows, width = tokens.shape
    texts = rows // length
    shape = jax.ShapeDtypeStruct
    copies = PX * (3 + 1 + hidden // width + 1)
    return pl.pallas_call(
        functools.partial(text_forward_kernel, length),
        name="text_forward",
        in_specs=[WHOLE, ANY, WHOLE, WHOLE],
        out_specs=[WHOLE] * 9,
        out_shape=[
            shape((rows, width), BF),
            shape((rows, 3 * width), BF),
            shape((rows, width), BF),
            shape((rows, width), F32),
            shape((rows, width), BF),
            shape((rows, hidden), BF),
            shape((texts, hidden), BF),
            shape((texts, width), F32),
            shape((texts, width), BF),
        ],
        scratch_shapes=[weight_scratch(w, width, hidden) for w in ("qkv", "out", "up", "down")]
        + [
            pltpu.VMEM((texts, hidden), F32),
            pltpu.VMEM((1, 3 * width), F32),
            pltpu.SemaphoreType.DMA((copies,)),
        ],
        compiler_params=params(),
        cost_estimate=pl.CostEstimate(
            flops=2 * rows * width * (4 * width + hidden),
            bytes_accessed=2 * (4 * width * width + 2 * width * hidden + 12 * rows * width),
            transcendentals=rows * hidden,
        ),
    )(tokens, packed, vec, ub)


def contrast_kernel(low, images, live, same, groups, own, own_group, power, row_part, col_sum, loss_part):
    scores = LOGIT_SCALE * dot(low[...], images[...], 1, 1)
    exps = jnp.exp(scores)
    live_own, same_own = own[:, 0:1], own[:, 1:2]
    power[...] = exps
    rows = jnp.sum(exps * live_own, axis=0, keepdims=True)
    for k in range(row_part.shape[0]):
        row_part[k : k + 1, :] = rows[:, k * 128 : (k + 1) * 128]
    cols = jnp.sum(exps * live[...], axis=1, keepdims=True)
    col_sum[...] = cols
    pair = jnp.where(own_group[...] == groups[...], live_own * live[...], 0.0)
    linear = pair * scores * (1.0 / same_own + 1.0 / same[...])
    losses = live_own * jnp.log(cols) - jnp.sum(linear, axis=1, keepdims=True)
    loss_part[...] = jnp.broadcast_to(jnp.sum(losses, axis=0, keepdims=True), loss_part.shape)


def contrast(low, images, live, same, groups, own, own_group):
    texts = low.shape[0]
    pairs = images.shape[0]
    shape = jax.ShapeDtypeStruct
    return pl.pallas_call(
        contrast_kernel,
        name="contrast",
        in_specs=[WHOLE] * 7,
        out_specs=[WHOLE] * 4,
        out_shape=[
            shape((texts, pairs), F32),
            shape((pairs // 128, 128), F32),
            shape((texts, 1), F32),
            shape((8, 128), F32),
        ],
        compiler_params=params(),
    )(low, images, live, same, groups, own, own_group)


def relative_kernel(where, h1, h2, att, h1_t, h2_t, att_t):
    width = h1.shape[1]
    block = width // PF
    my, mz, mc = where[1], where[2], where[3]
    for src, dst in ((h2, h2_t), (h1, h1_t), (att, att_t)):
        turned = src[...].T
        for z in range(4):
            for y in range(2):
                for c in range(2):
                    f = (z * 2 + y) * 2 + c
                    place = (((c ^ mc) * 2 + (y ^ my)) * 4 + (z ^ mz)) * block
                    dst[pl.ds(pl.multiple_of(place, block), block), :] = turned[
                        f * block : (f + 1) * block
                    ]


SMEM = pl.BlockSpec(memory_space=pltpu.SMEM)


def relative_rows(where, h1, h2, att):
    rows, width = h1.shape
    return pl.pallas_call(
        relative_kernel,
        name="relative_rows",
        in_specs=[SMEM, WHOLE, WHOLE, WHOLE],
        out_specs=[WHOLE] * 3,
        out_shape=[jax.ShapeDtypeStruct((width, rows), BF)] * 3,
        compiler_params=params(),
        cost_estimate=pl.CostEstimate(flops=0, bytes_accessed=12 * rows * width, transcendentals=0),
    )(where, h1, h2, att)


def grad_shapes(width):
    block, half = width // PF, width
    return [jax.ShapeDtypeStruct((2, 2, 4, block, half), BF)] * 4


def put_grad(values, outs, x_rel, at, second):
    width, cols = values.shape
    block = width // PF
    low = values.astype(BF)
    for c in range(2):
        for y in range(2):
            piece = low[(c * 2 + y) * 4 * block : (c * 2 + y + 1) * 4 * block].reshape(4, block, cols)
            if second:
                outs[2 + c][y, x_rel, :, :, pl.ds(at, cols)] = piece
            else:
                outs[c][x_rel, y, :, :, pl.ds(at, cols)] = piece


def back_first_kernel(
    length,
    where, power, row_all, col_sum, images, live, same, groups, own, own_group, factor, pooled, packed, slope,
    h2_t, dy_out, dm_out, du, keep_a, send_a, keep_b, send_b, bias_up, down_bias, wd, dact, sem,
):
    rows, hidden = slope.shape
    texts = rows // length
    width = h2_t.shape[0]
    loads = weight_copies(packed, "down", wd, sem, 0, width, hidden)
    for copy in loads:
        copy.start()
    sums = row_all[...]
    if sums.ndim == 3:
        sums = jnp.sum(sums, axis=0)
    row_sum = jnp.concatenate([sums[k : k + 1] for k in range(sums.shape[0])], axis=1)
    live_own, same_own = own[:, 0:1], own[:, 1:2]
    pair = factor[0:1, 0:1] * live_own * live[...]
    match = jnp.where(own_group[...] == groups[...], 1.0 / same_own + 1.0 / same[...], 0.0)
    grad_scores = pair * (power[...] * (1.0 / row_sum + 1.0 / col_sum[...]) - match)
    grad_low = LOGIT_SCALE * dot(grad_scores.astype(BF), images[...])
    pool = pooled[...]
    inverse = lax.rsqrt(jnp.sum(pool * pool, axis=-1, keepdims=True) + 1e-06)
    along = jnp.sum(pool * grad_low, axis=-1, keepdims=True)
    dy = inverse * (grad_low - pool * (inverse * inverse * along)) * (1.0 / length)
    dm = dy.astype(BF)
    dy_out[...] = dy
    dm_out[...] = dm
    down_bias[...] = length * jnp.sum(dm.astype(F32), axis=0, keepdims=True)
    for copy in loads:
        copy.wait()
    dact[...] = dot(dm, natural(wd), 1, 1)

    def slopes(i):
        at = pl.ds(pl.multiple_of(i * 256, 256), 256)
        spread = jnp.broadcast_to(dact[:, at].reshape(texts, 1, 256), (texts, length, 256))
        part = (spread.reshape(rows, 256) * slope[:, at].astype(F32)).astype(BF)
        du[:, at] = part
        bias_up[:, at] = jnp.sum(part.astype(F32), axis=0, keepdims=True)

    repeat(hidden // 256, slopes, 3)
    half = hidden // PX

    def grads(i):
        x, c = i // (width // 256), pl.multiple_of(i % (width // 256) * 256, 256)
        first = (x ^ where[0]) * half + c
        for second in range(2):
            part = du[:, pl.ds(pl.multiple_of(first + second * width, 256), 256)]
            put_grad(dot(h2_t[...], part), (keep_a, send_a, keep_b, send_b), x, c, second)

    repeat(PX * width // 256, grads, 2)


def back_first(
    where, power, row_all, col_sum, images, live, same, groups, own, own_group, factor, pooled, packed, slope,
    h2_t, length,
):
    rows, hidden = slope.shape
    width = h2_t.shape[0]
    texts = rows // length
    shape = jax.ShapeDtypeStruct
    return pl.pallas_call(
        functools.partial(back_first_kernel, length),
        name="back_first",
        in_specs=[SMEM] + [WHOLE] * 11 + [ANY, WHOLE, WHOLE],
        out_specs=[WHOLE] * 9,
        out_shape=[
            shape((texts, width), F32),
            shape((texts, width), BF),
            shape((rows, hidden), BF),
            *grad_shapes(width),
            shape((1, hidden), F32),
            shape((1, width), F32),
        ],
        scratch_shapes=[
            weight_scratch("down", width, hidden),
            pltpu.VMEM((texts, hidden), F32),
            pltpu.SemaphoreType.DMA((PX,)),
        ],
        compiler_params=params(),
        cost_estimate=pl.CostEstimate(
            flops=2 * rows * width * hidden, bytes_accessed=12 * width * hidden, transcendentals=0
        ),
    )(
        where, power, row_all, col_sum, images, live, same, groups, own, own_group, factor, pooled, packed, slope,
        h2_t,
    )


def back_norm_kernel(length, dy, du, r1, packed, vec, dr1, dz_s, da_s, sums, wu, wo, sem):
    rows, width = r1.shape
    hidden = du.shape[1]
    up = weight_copies(packed, "up", wu, sem, 0, width, hidden)
    out = weight_copies(packed, "out", wo, sem, len(up), width, hidden)
    for copy in up + out:
        copy.start()
    v = vec[...].astype(F32)
    blk = 128
    for copy in up:
        copy.wait()
    half = rows // 2

    def product(i):
        at = pl.ds(pl.multiple_of(i * half, half), half)
        dr1[at, :] = dot(du[at, :], natural(wu), 1, 1)

    repeat(2, product)
    sums[...] = jnp.zeros((8, width), F32)
    some = blk // length

    def back(i):
        at = pl.ds(pl.multiple_of(i * blk, blk), blk)
        hat, inverse = normalize(r1[at, :])
        grad = dr1[at, :]
        sums[1:2, :] += jnp.sum(grad * hat, axis=0, keepdims=True)
        sums[2:3, :] += jnp.sum(grad, axis=0, keepdims=True)
        spread = jnp.broadcast_to(
            dy[pl.ds(pl.multiple_of(i * some, some), some), :].reshape(some, 1, width), (some, length, width)
        ).reshape(blk, width)
        grad = spread + norm_back(grad, hat, inverse, v[5:6])
        dr1[at, :] = grad
        low = grad.astype(BF)
        dz_s[at, :] = low
        sums[0:1, :] += jnp.sum(low.astype(F32), axis=0, keepdims=True)

    repeat(rows // blk, back, 2)
    for copy in out:
        copy.wait()
    da_s[...] = dot(dz_s[...], natural(wo), 1, 1).astype(BF)


def back_norm(dy, du, r1, packed, vec, length):
    rows, width = r1.shape
    hidden = du.shape[1]
    shape = jax.ShapeDtypeStruct
    return pl.pallas_call(
        functools.partial(back_norm_kernel, length),
        name="back_norm",
        in_specs=[WHOLE] * 3 + [ANY, WHOLE],
        out_specs=[WHOLE] * 4,
        out_shape=[
            shape((rows, width), F32),
            shape((rows, width), BF),
            shape((rows, width), BF),
            shape((8, width), F32),
        ],
        scratch_shapes=[
            weight_scratch("up", width, hidden),
            weight_scratch("out", width, hidden),
            pltpu.SemaphoreType.DMA((PX * (1 + hidden // width),)),
        ],
        compiler_params=params(),
        cost_estimate=pl.CostEstimate(
            flops=2 * rows * width * (hidden + width), bytes_accessed=6 * width * hidden, transcendentals=0
        ),
    )(dy, du, r1, packed, vec)


def back_attention_kernel(length, qkv, da_s, dqkv, sums):
    rows, width = da_s.shape
    blk = 128
    low_lane = lax.broadcasted_iota(jnp.int32, (blk, 128), 1) < HEAD_DIM
    bias = text_mask(blk, length)
    cols = range(0, width, 128)
    def group(i):
        at = pl.ds(pl.multiple_of(i * blk, blk), blk)
        take = lambda base, c: qkv[at, base + c : base + c + 128]
        q2 = [take(0, c) * 0.125 for c in cols]
        k2 = [head_pair(take(width, c), low_lane) for c in cols]
        v2 = [head_pair(take(2 * width, c), low_lane) for c in cols]
        da = [da_s[at, c : c + 128] for c in cols]
        scores = [dot(k, q, 1, 1) for k, q in zip(k2, q2)]
        grads = [dot(v, d, 1, 1) for v, d in zip(v2, da)]
        probs, deltas = [], []
        for score, grad in zip(scores, grads):
            p_low, d_low = [], []
            for half in range(2):
                s = score[half * blk : (half + 1) * blk] + bias
                g = grad[half * blk : (half + 1) * blk]
                powers = jnp.exp(s - jnp.max(s, axis=0, keepdims=True))
                soft = powers * (1.0 / jnp.sum(powers, axis=0, keepdims=True))
                p_low.append(soft.astype(BF))
                d_low.append((soft * (g - jnp.sum(g * soft, axis=0, keepdims=True))).astype(BF))
            probs.append(jnp.concatenate(p_low, axis=0))
            deltas.append(jnp.concatenate(d_low, axis=0))
        for n, c in enumerate(cols):
            dq = dot(deltas[n], k2[n], 0, 0) * 0.125
            dk = dot(deltas[n], q2[n])
            dv = dot(probs[n], da[n])
            dqkv[at, c : c + 128] = dq.astype(BF)
            dqkv[at, width + c : width + c + 128] = jnp.where(
                low_lane, dk[:blk], dk[blk:]
            ).astype(BF)
            dqkv[at, 2 * width + c : 2 * width + c + 128] = jnp.where(
                low_lane, dv[:blk], dv[blk:]
            ).astype(BF)

    repeat(rows // blk, group, 2)
    sums[0:1, :] = jnp.sum(dqkv[:, :width].astype(F32), axis=0, keepdims=True)
    sums[1:2, :] = jnp.sum(dqkv[:, 2 * width :].astype(F32), axis=0, keepdims=True)
    sums[2:8, :] = jnp.zeros((6, width), F32)


def back_attention(qkv, da, length):
    rows, width = da.shape
    shape = jax.ShapeDtypeStruct
    return pl.pallas_call(
        functools.partial(back_attention_kernel, length),
        name="back_attention",
        in_specs=[WHOLE] * 2,
        out_specs=[WHOLE] * 2,
        out_shape=[shape((rows, 3 * width), BF), shape((8, width), F32)],
        compiler_params=params(),
        cost_estimate=pl.CostEstimate(
            flops=2 * rows * width * 1280, bytes_accessed=20 * rows * width, transcendentals=rows * width
        ),
    )(qkv, da)


def attention_grads_kernel(where, h1_t, att_t, dqkv, dz, keep_a, send_a, keep_b, send_b):
    width = h1_t.shape[0]
    piece = width // PX
    outs = (keep_a, send_a, keep_b, send_b)

    def part_of(x):
        other = x ^ where[0]
        first = other * (3 * piece)

        def chunk(i):
            c = pl.multiple_of(i * 256, 256)
            part = dqkv[:, pl.ds(pl.multiple_of(first + c, 128), 256)]
            put_grad(dot(h1_t[...], part), outs, x, c, 0)

        repeat(width // 256, chunk, 3)
        part = dqkv[:, pl.ds(pl.multiple_of(first + width, 128), piece)]
        put_grad(dot(h1_t[...], part), outs, x, 0, 1)
        part = dz[:, pl.ds(pl.multiple_of(other * piece, 128), piece)]
        put_grad(dot(att_t[...], part), outs, x, piece, 1)

    repeat(PX, part_of)


def attention_grads(where, h1_t, att_t, dqkv, dz):
    width, rows = h1_t.shape
    return pl.pallas_call(
        attention_grads_kernel,
        name="attention_grads",
        in_specs=[SMEM] + [WHOLE] * 4,
        out_specs=[WHOLE] * 4,
        out_shape=grad_shapes(width),
        compiler_params=params(),
        cost_estimate=pl.CostEstimate(
            flops=8 * rows * width * width, bytes_accessed=8 * width * width + 12 * rows * width, transcendentals=0
        ),
    )(where, h1_t, att_t, dqkv, dz)


def back_third_kernel(dr1, dqkv, tok, packed, vec, sums, bias_sums, down_bias, dx, all_sums, wq, sem):
    rows, width = tok.shape
    loads = weight_copies(packed, "qkv", wq, sem, 0, width, width)
    for copy in loads:
        copy.start()
    v = vec[...].astype(F32)
    for copy in loads:
        copy.wait()
    half = rows // 2

    def product(i):
        at = pl.ds(pl.multiple_of(i * half, half), half)
        dx[at, :] = dot(dqkv[at, :], natural(wq), 1, 1)

    repeat(2, product)
    all_sums[0:2, :] = jnp.zeros((2, width), F32)
    blk = 128

    def back(i):
        at = pl.ds(pl.multiple_of(i * blk, blk), blk)
        hat, inverse = normalize(tok[at, :].astype(F32))
        grad = dx[at, :]
        all_sums[0:1, :] += jnp.sum(grad * hat, axis=0, keepdims=True)
        all_sums[1:2, :] += jnp.sum(grad, axis=0, keepdims=True)
        dx[at, :] = dr1[at, :] + norm_back(grad, hat, inverse, v[0:1])

    repeat(rows // blk, back, 2)
    all_sums[2:4, :] = bias_sums[0:2, :]
    all_sums[4:7, :] = sums[0:3, :]
    all_sums[7:8, :] = down_bias[...]


def back_third(dr1, dqkv, tok, packed, vec, sums, bias_sums, down_bias):
    rows, width = tok.shape
    shape = jax.ShapeDtypeStruct
    return pl.pallas_call(
        back_third_kernel,
        name="back_third",
        in_specs=[WHOLE, WHOLE, WHOLE, ANY, WHOLE, WHOLE, WHOLE, WHOLE],
        out_specs=[WHOLE] * 2,
        out_shape=[shape((rows, width), F32), shape((8, width), F32)],
        scratch_shapes=[
            weight_scratch("qkv", width, width),
            pltpu.SemaphoreType.DMA((PX * 3,)),
        ],
        compiler_params=params(),
        cost_estimate=pl.CostEstimate(
            flops=6 * rows * width * width, bytes_accessed=14 * width * width, transcendentals=0
        ),
    )(dr1, dqkv, tok, packed, vec, sums, bias_sums, down_bias)


def fold_kernel(a_own, a_new, b_own, b_new, a_keep, a_send, b_keep, b_send):
    for own, new, keep, send in ((a_own, a_new, a_keep, a_send), (b_own, b_new, b_keep, b_send)):
        total = own[...].astype(F32) + new[...].astype(F32)
        keep[...] = total[0].astype(BF)
        send[...] = total[1].astype(BF)


def fold(a_own, a_new, b_own, b_new):
    shape = a_own.shape
    rest = 1
    for n in shape[1:-2]:
        rest *= n
    rows, cols = shape[-2:]
    view = lambda a: a.reshape(2, rest, rows, cols)
    steps = 2 if rest > 4 else 1
    pair = pl.BlockSpec((2, rest // steps, rows, cols), lambda i: (0, i, 0, 0))
    one = pl.BlockSpec((rest // steps, rows, cols), lambda i: (i, 0, 0))
    outs = pl.pallas_call(
        fold_kernel,
        name="fold",
        grid=(steps,),
        in_specs=[pair] * 4,
        out_specs=[one] * 4,
        out_shape=[jax.ShapeDtypeStruct((rest, rows, cols), BF)] * 4,
        compiler_params=params(),
        cost_estimate=pl.CostEstimate(
            flops=4 * rest * rows * cols, bytes_accessed=24 * rest * rows * cols, transcendentals=0
        ),
    )(*(view(a) for a in (a_own, a_new, b_own, b_new)))
    return [o.reshape(shape[1:]) for o in outs]


def join_kernel(a_own, a_new, b_own, b_new, stay, one, two, three):
    half = a_own.shape[-1]
    for at, own, new in ((0, a_own, a_new), (half, b_own, b_new)):
        total = own[...].astype(F32) + new[...].astype(F32)
        for k, dst in enumerate((stay, one, two, three)):
            dst[:, at : at + half] = total[k].astype(dst.dtype)


def join(a_own, a_new, b_own, b_new):
    blocks, rows, cols = a_own.shape
    shape = jax.ShapeDtypeStruct
    return pl.pallas_call(
        join_kernel,
        name="join",
        in_specs=[WHOLE] * 4,
        out_specs=[WHOLE] * 4,
        out_shape=[shape((rows, 2 * cols), F32)] + [shape((rows, 2 * cols), BF)] * 3,
        compiler_params=params(),
        cost_estimate=pl.CostEstimate(
            flops=16 * rows * cols, bytes_accessed=40 * rows * cols, transcendentals=0
        ),
    )(a_own, a_new, b_own, b_new)


def shifted(x, y, z, core):
    change = x * 16 + z * 4 + y * 2 + core
    return [(i, i ^ change) for i in range(32)]


def hop(array, x=0, y=0, z=0, core=0):
    return lax.ppermute(array, AXES, shifted(x, y, z, core))


def after(values, *others):
    return lax.optimization_barrier((tuple(values), others))[0]


def core_step(parts, *wait):
    keep_a, send_a, keep_b, send_b = parts
    new_a, new_b = hop(send_a, core=1), hop(send_b, core=1)
    keep_a, keep_b = after((keep_a, keep_b), *wait)
    return fold(keep_a, new_a, keep_b, new_b)


def first_step(parts, *wait):
    keep_a, send_a, keep_b, send_b = parts
    new_a, new_b = hop(send_a, x=1), hop(send_b, y=1)
    keep_a, keep_b = after((keep_a, keep_b), *wait)
    return fold(keep_a, new_a, keep_b, new_b)


def second_step(parts, *wait):
    keep_a, send_a, keep_b, send_b = parts
    new_a, new_b = hop(send_a, y=1), hop(send_b, x=1)
    keep_a, keep_b = after((keep_a, keep_b), *wait)
    return join(keep_a, new_a, keep_b, new_b)


def third_step(parts):
    stay, one, two, three = parts
    others = [hop(one, z=1), hop(two, z=2), hop(three, z=3)]
    return stay + sum(o.astype(F32) for o in others)


def natural_grad(keep_a, send_a, keep_b, send_b):
    first = jnp.stack([keep_a, send_a])
    second = jnp.swapaxes(jnp.stack([keep_b, send_b]), 1, 2)
    whole = jnp.concatenate([first, second], axis=-1)
    core, x, y, z, rows, cols = whole.shape
    return whole.transpose(1, 3, 2, 0, 4, 5).reshape(x, z * y * core * rows, cols)


def pack_kernel(qkv, out, up, down, packed):
    rows, piece = out.shape
    at = 0
    for ref in (qkv, out, up, down):
        for c in range(0, ref.shape[1], piece):
            packed[at : at + ref.shape[0], :] = ref[:, c : c + piece]
            at += ref.shape[0]


def pack_block(qkv, out, up, down):
    piece = out.shape[1]
    total = sum(w.shape[0] * w.shape[1] for w in (qkv, out, up, down)) // piece
    return pl.pallas_call(
        pack_kernel,
        name="pack_block",
        in_specs=[WHOLE] * 4,
        out_specs=WHOLE,
        out_shape=jax.ShapeDtypeStruct((total, piece), BF),
        compiler_params=params(),
    )(qkv, out, up, down)


def gather_packed(qkv, out, up, down, dp, fsdp):
    if (dp, fsdp) == (PX, PF):
        return lax.all_gather(pack_block(qkv, out, up, down), AXES, axis=0)
    full = [
        lax.all_gather(lax.all_gather(w, "dp", axis=1, tiled=True), "fsdp", axis=0, tiled=True)
        for w in (qkv, out, up, down)
    ]
    blocks = []
    for x in range(PX):
        for f in range(PF):
            some = []
            for w in full:
                rows, cols = w.shape[0] // PF, w.shape[1] // PX
                some.append(w[f * rows : (f + 1) * rows, x * cols : (x + 1) * cols])
            blocks.append(pack_block(*some))
    return jnp.stack(blocks)


def scatter_columns(grad, dp, fsdp):
    parts, rows, cols = grad.shape
    if dp != parts:
        grad = jnp.swapaxes(grad, 0, 1).reshape(rows, dp, parts * cols // dp)
        grad = jnp.swapaxes(grad, 0, 1)
    return lax.psum_scatter(
        grad.reshape(dp * rows, -1), AXES, scatter_dimension=0, tiled=True
    ).astype(F32)


def body(
    image_tokens,
    text_tokens,
    image_qkv,
    image_out,
    image_up,
    image_down,
    image_vectors,
    image_up_bias,
    text_qkv,
    text_out,
    text_up,
    text_down,
    text_vectors,
    text_up_bias,
    pair_counts,
    pair_groups,
):
    dp, fsdp = lax.axis_size("dp"), lax.axis_size("fsdp")
    devices = dp * fsdp
    cap, length, width = text_tokens.shape
    hidden = image_up.shape[1]
    pairs = pair_groups.shape[0]
    me = lax.axis_index("dp") * fsdp + lax.axis_index("fsdp")

    grid_mesh = (dp, fsdp) == (PX, PF)
    packed = gather_packed(text_qkv, text_out, text_up, text_down, dp, fsdp)
    part = width // fsdp
    small = jnp.concatenate([text_vectors, text_up_bias.reshape(8, -1)], axis=1)
    if grid_mesh:
        small = jnp.broadcast_to(small[None], (fsdp,) + small.shape)
        small = lax.all_to_all(small, "fsdp", 0, 0, tiled=True)
    else:
        small = lax.all_gather(small, "fsdp", axis=0)
    vec = jnp.swapaxes(small[:, :, :part], 0, 1).reshape(8, width)
    ub = small[:, :, part:].reshape(1, hidden)
    bits = [lax.shift_right_logical(me, k) & 1 for k in range(5)]
    where = jnp.stack([bits[4], bits[1], 2 * bits[3] + bits[2], bits[0]])
    where = where if grid_mesh else jnp.zeros_like(where)

    image_low = image_forward(
        image_tokens, image_qkv, image_out, image_up, image_down, image_vectors, image_up_bias
    )
    if grid_mesh:
        images = image_low
        for change in (dict(z=1), dict(z=2), dict(x=1), dict(y=1), dict(core=1)):
            images = jnp.concatenate([images, hop(images, **change)], axis=0)
        far = jnp.arange(devices, dtype=jnp.int32) ^ me
        bit = lambda k: lax.shift_right_logical(far, k) & 1
        order = bit(2) + 2 * bit(3) + 4 * bit(4) + 8 * bit(1) + 16 * bit(0)
        images = jnp.take(images.reshape(devices, cap, width), order, axis=0).reshape(pairs, width)
    else:
        images = lax.all_gather(image_low, AXES, axis=0, tiled=True)

    slots = jnp.arange(cap, dtype=jnp.int32)
    live = (slots[None, :] < pair_counts[:, None]).reshape(pairs).astype(F32)
    same = jnp.maximum(
        jnp.sum(jnp.where(pair_groups[:, None] == pair_groups[None, :], live[None, :], 0.0), axis=1), 1.0
    )
    own_of = lambda array: lax.dynamic_slice_in_dim(array, me * cap, cap)
    own = jnp.stack([own_of(live), own_of(same)], axis=1)
    own_group = own_of(pair_groups).reshape(cap, 1)
    live_row, same_row, group_row = (a.reshape(1, pairs) for a in (live, same, pair_groups))
    live_total = jnp.sum(pair_counts).astype(F32)
    factor = jnp.broadcast_to(LOSS_WEIGHT / (2.0 * live_total), (1, 128))

    tokens = text_tokens.reshape(cap * length, width)
    h1, qkv, att, r1, h2, slope, acts, pooled, low = text_forward(tokens, packed, vec, ub, length, hidden)
    power, row_part, col_sum, loss_part = contrast(
        low, images, live_row, same_row, group_row, own, own_group
    )
    if devices <= 32:
        row_all = lax.all_to_all(
            jnp.broadcast_to(row_part[None], (devices,) + row_part.shape), AXES, 0, 0, tiled=True
        )
        row_sum = jnp.sum(row_all, axis=0)
    else:
        row_all = lax.psum(row_part, AXES)
        row_sum = row_all
    h1_t, h2_t, att_t = relative_rows(where, h1, h2, att)
    dy, dm, du, *up_parts, bias_up, down_bias = back_first(
        where, power, row_all, col_sum, images, live_row, same_row, group_row, own, own_group, factor, pooled,
        packed, slope, h2_t, length,
    )
    dr1, dz, da, sums = back_norm(dy, du, r1, packed, vec, length)
    if grid_mesh:
        up_parts = core_step(up_parts, da)
        (da,) = after((da,), *up_parts)
    dqkv, bias_sums = back_attention(qkv, da, length)
    att_parts = attention_grads(where, h1_t, att_t, dqkv, dz)
    if grid_mesh:
        up_parts = first_step(up_parts, *att_parts)
        dqkv, *att_parts = after((dqkv, *att_parts), *up_parts)
    dx, vec_grads = back_third(dr1, dqkv, tokens, packed, vec, sums, bias_sums, down_bias)
    rows_of = hidden // fsdp
    cols_of = width // dp
    left = jnp.swapaxes(acts.reshape(cap, fsdp, rows_of), 0, 1)
    left = jnp.broadcast_to(left[None], (dp, fsdp, cap, rows_of)).reshape(devices, cap, rows_of)
    right = jnp.swapaxes(dm.reshape(cap, dp, cols_of), 0, 1)
    right = jnp.broadcast_to(right[:, None], (dp, fsdp, cap, cols_of)).reshape(devices, cap, cols_of)
    both = lax.all_to_all(jnp.concatenate([left, right], axis=2), AXES, 0, 0, tiled=True)
    both = both.reshape(pairs, rows_of + cols_of)
    grad_down = dot(both[:, :rows_of], both[:, rows_of:], 0, 0)

    if grid_mesh:
        att_parts = core_step(att_parts, dx)
        up_parts = second_step(up_parts, *att_parts)
        att_parts = first_step(att_parts, grad_down, *up_parts)
        (vec_grads,) = after((vec_grads,), *att_parts)
        grad_up = third_step(up_parts)
        grad_attn = third_step(second_step(att_parts))
        grad_qkv, grad_out = grad_attn[:, : 3 * width // dp], grad_attn[:, 3 * width // dp :]
    else:
        grad_attn = natural_grad(*att_parts)
        grad_up = scatter_columns(natural_grad(*up_parts), dp, fsdp)
        grad_qkv = scatter_columns(grad_attn[:, :, : 3 * width // PX], dp, fsdp)
        grad_out = scatter_columns(grad_attn[:, :, 3 * width // PX :], dp, fsdp)

    share = jnp.concatenate(
        [
            jnp.swapaxes(vec_grads.reshape(8, fsdp, part), 0, 1).reshape(fsdp, 8 * part),
            bias_up.reshape(fsdp, rows_of),
            jnp.broadcast_to(loss_part[0, 0].reshape(1, 1), (fsdp, 1)),
        ],
        axis=1,
    )
    used = share.shape[1]
    padded = -(-used // 128) * 128
    share = jnp.pad(share, ((0, 0), (0, padded - used))).reshape(fsdp, padded // 128, 128)
    share = jnp.broadcast_to(share[None], (dp,) + share.shape).reshape(devices, padded // 128, 128)
    share = jnp.sum(lax.all_to_all(share, AXES, 0, 0, tiled=True), axis=0).reshape(padded)
    grad_vec = share[: 8 * part].reshape(8, part)
    grad_bias = share[8 * part : 8 * part + rows_of]
    loss = (share[used - 1] + jnp.sum(live * jnp.log(row_sum.reshape(pairs)))) / (2.0 * live_total)

    return (
        loss,
        dx.reshape(text_tokens.shape),
        grad_qkv,
        grad_out,
        grad_up,
        grad_down,
        grad_vec,
        grad_bias,
    )


def solution(mesh):
    return jax.shard_map(
        body,
        mesh=mesh,
        in_specs=(
            P(AXES, None, None),
            P(AXES, None, None),
            P(),
            P(),
            P(),
            P(),
            P(),
            P(),
            P("fsdp", "dp"),
            P("fsdp", "dp"),
            P("fsdp", "dp"),
            P("fsdp", "dp"),
            P(None, "fsdp"),
            P("fsdp"),
            P(),
            P(),
        ),
        out_specs=(
            P(),
            P(AXES, None, None),
            P("fsdp", "dp"),
            P("fsdp", "dp"),
            P("fsdp", "dp"),
            P("fsdp", "dp"),
            P(None, "fsdp"),
            P("fsdp"),
        ),
        check_vma=False,
    )
```

profile of v0, /device:TPU:0, one launch (start us, length us, event | category | flops | bytes accessed | tf_op | source)
XLA Modules:
  0.0 304.7 jit_solution(9182533748370344450)
XLA Ops:
  7.2 1.9 pack_block.1
  9.1 1.3 reshape.271.ub
  10.4 50.3 %image_forward.1 = bf16[32,768]{1,0:T(8,128)(2,1)} custom-call(bf16[50,32,768]{2,1,0:T(8,128)(2,1)} %bitcast.80, bf16[768,2304]{1,0:T(8,128)(2,1)} %wq_h.1, bf16[768,768]{1,0:T(8,128)(2,1)} %wo_h.1, bf16[768,3072]{1,0:T(8,128)(2,1)} %wu_h.1, bf16[3072,768]{1,0:T(8,128)(2,1)} %wd_h.1, bf16[8,768]{1,0:T(8,128)(2,1)} %vec.1, bf16[1,3072]{1,0:T(2,128)(2,1)} %reshape.271.ub), custom_call_target="tpu_custom_call" | custom-call | flops 15099494400 | bytes 16613376 | tf_op jit(solution)/shard_map/image_forward/pallas_call | solution.py:223
  60.8 3.1 %collective-permute-start = (bf16[32,768]{1,0:T(8,128)(2,1)}, bf16[32,768]{1,0:T(8,128)(2,1)S(1)}, u32[]{:S(2)}, u32[]{:S(2)}) collective-permute-start(bf16[32,768]{1,0:T(8,128)(2,1)} %image_forward.1), channel_id=1, source_target_pairs={{0,4},{1,5},{2,6},{3,7},{4,0},{5,1},{6,2},{7,3},{8,12},{9,13},{10,... | collective-permute-start | bytes 147464 | tf_op jit(solution)/shard_map/ppermute | solution.py:891
  64.6 4.9 %all-to-all-start = ((bf16[16,8,72]{2,1,0:T(8,128)(2,1)}), bf16[16,8,72]{2,1,0:T(8,128)(2,1)S(1)}, u32[]{:S(2)}, u32[]{:S(2)}) async-start(bf16[16,8,72]{2,1,0:T(8,128)(2,1)} %broadcast_in_dim.74), calls=%async_computation | async-start | bytes 65536 | tf_op jit(solution)/shard_map/all_to_all | solution.py:1014
  70.3 0.8 pad_maximum_fusion.3
  71.1 2.8 collective-permute-start.1
  73.9 1.4 constant_dynamic-update-slice_fusion.4
  75.4 10.8 %collective-permute-done.1 = bf16[64,768]{1,0:T(8,128)(2,1)S(1)} collective-permute-done((bf16[64,768]{1,0:T(8,128)(2,1)S(1)}, bf16[64,768]{1,0:T(8,128)(2,1)S(1)}, u32[]{:S(2)}, u32[]{:S(2)}) %collective-permute-start.1) | collective-permute-done | bytes 98336 | tf_op jit(solution)/shard_map/ppermute | solution.py:891
  86.2 0.8 pad_maximum_fusion.2
  87.0 1.6 collective-permute-start.2
  88.6 10.1 %collective-permute-done.2 = bf16[128,768]{1,0:T(8,128)(2,1)S(1)} collective-permute-done((bf16[128,768]{1,0:T(8,128)(2,1)S(1)}, bf16[128,768]{1,0:T(8,128)(2,1)S(1)}, u32[]{:S(2)}, u32[]{:S(2)}) %collective-permute-start.2) | collective-permute-done | bytes 196640 | tf_op jit(solution)/shard_map/ppermute | solution.py:891
  98.7 0.8 pad_maximum_fusion.1
  99.5 1.6 collective-permute-start.3
  103.1 6.7 %collective-permute-done.3 = bf16[256,768]{1,0:T(8,128)(2,1)S(1)} collective-permute-done((bf16[256,768]{1,0:T(8,128)(2,1)S(1)}, bf16[256,768]{1,0:T(8,128)(2,1)S(1)}, u32[]{:S(2)}, u32[]{:S(2)}) %collective-permute-start.3) | collective-permute-done | bytes 393248 | tf_op jit(solution)/shard_map/ppermute | solution.py:891
  109.8 0.8 constant_dynamic-update-slice_fusion
  113.8 0.7 reshape.270.ub
  115.2 1.5 bitcast_select_fusion.images
  116.7 4.9 %all-gather.3.cloned.1.call-done = bf16[18432,384]{1,0:T(8,128)(2,1)} async-done(((bf16[576,384]{1,0:T(8,128)(2,1)}), bf16[18432,384]{1,0:T(8,128)(2,1)}) %all-gather.3.cloned.1.call-update) | async-done | bytes 14155792 | tf_op jit(solution)/shard_map/all_gather | solution.py:957
  121.6 23.2 %text_forward.1 = (bf16[512,768]{1,0:T(8,128)(2,1)}, bf16[512,2304]{1,0:T(8,128)(2,1)}, bf16[512,768]{1,0:T(8,128)(2,1)}, f32[512,768]{1,0:T(8,128)}, bf16[512,7...) custom-call(bf16[512,768]{1,0:T(8,128)(2,1)} %bitcast.66, ...), custom_call_target="tpu_custom_call" | custom-call | flops 4831838208 | bytes 23592960 | tf_op jit(solution)/shard_map/text_forward/pallas_call | solution.py:405
  144.8 2.8 contrast.1
  147.6 1.3 broadcast_in_dim.82
  148.9 2.7 all-to-all-start.1
  153.6 3.5 %relative_rows.1 = (bf16[768,512]{1,0:T(8,128)(2,1)}, bf16[768,512]{1,0:T(8,128)(2,1)}, bf16[768,512]{1,0:T(8,128)(2,1)}) custom-call(s32[4]{0:T(128)} %pad_add_fusion.where, bf16[512,768]{1,0:T(8,128)(2,1)} %get-tuple-element.94.h1, bf16[512,768]{1,0:T(8,128)(2,1)} %get-tuple-element.95.h2, bf16[512,768]{1,0:T(8,128)(2,1)} %get-tuple-element.96.att), custom_call_target="tpu_custom_call" | custom-call | bytes 4718592 | tf_op jit(solution)/shard_map/relative_rows/pallas_call | solution.py:492
  157.1 2.8 all-to-all-done.1.row_all
  160.5 14.8 %back_first.1 = (f32[32,768]{1,0:T(8,128)}, bf16[32,768]{1,0:T(8,128)(2,1)}, bf16[512,3072]{1,0:T(8,128)(2,1)}, bf16[2,2,4,48,768]{4,3,2,1,0:T(8,128)(2,1)}, bf1...) custom-call(s32[4]{0:T(128)} %pad_add_fusion.where, ...), custom_call_target="tpu_custom_call" | custom-call | flops 2415919104 | bytes 28311552 | tf_op jit(solution)/shard_map/back_first/pallas_call | solution.py:581
  176.3 0.8 reshape.290
  177.3 1.7 pad_maximum_fusion
  179.0 3.3 %all-to-all-start.2 = ((bf16[32,32,576]{2,1,0:T(8,128)(2,1)}), bf16[32,32,576]{2,1,0:T(8,128)(2,1)S(1)}, u32[]{:S(2)}, u32[]{:S(2)}) async-start(bf16[32,32,576]{2,1,0:T(8,128)(2,1)} %pad_maximum_fusion), calls=%async_computation.2 | async-start | bytes 2621440 | tf_op jit(solution)/shard_map/all_to_all | solution.py:1083
  182.3 10.8 %back_norm.1 = (f32[512,768]{1,0:T(8,128)}, bf16[512,768]{1,0:T(8,128)(2,1)}, bf16[512,768]{1,0:T(8,128)(2,1)}, f32[8,768]{1,0:T(8,128)}) custom-call(f32[32,768]{1,0:T(8,128)} %get-tuple-element.98.dy, bf16[512,3072]{1,0:T(8,128)(2,1)} %get-tuple-element.99.du, f32[512,768]{1,0:T(8,128)} %get-tuple-element.100.r1, bf16[32,576,384]{2,1,0:T(8,128)(2,1)} %bitcast.55, ...), custom_call_target="tpu_custom_call" | custom-call | flops 3019898880 | bytes 14155776 | tf_op jit(solution)/shard_map/back_norm/pallas_call | solution.py:655
  193.1 3.6 %fold.4 = (bf16[8,48,768]{2,1,0:T(8,128)(2,1)}, bf16[8,48,768]{2,1,0:T(8,128)(2,1)}, bf16[8,48,768]{2,1,0:T(8,128)(2,1)}, bf16[8,48,768]{2,1,0:T(8,128)(2,1)}) custom-call(bf16[2,8,48,768]{3,2,1,0:T(8,128)(2,1)} %bitcast.61, bf16[2,8,48,768]{3,2,1,0:T(8,128)(2,1)} %bitcast.17.a_new, bf16[2,8,48,768]{3,2,1,0:T(8,128)(2,1)} %bitcast.62, ...), custom_call_target="tpu_custom_call" | custom-call | flops 1179648 | bytes 7077888 | tf_op jit(solution)/shard_map/fold/pallas_call | solution.py:846
  196.7 1.6 collective-permute-start.7
  198.3 1.5 collective-permute-start.8
  199.7 6.7 %back_attention.1 = (bf16[512,2304]{1,0:T(8,128)(2,1)}, f32[8,768]{1,0:T(8,128)}) custom-call(bf16[512,2304]{1,0:T(8,128)(2,1)} %get-tuple-element.102.qkv, bf16[512,768]{1,0:T(8,128)(2,1)} %get-tuple-element.114.da_s), custom_call_target="tpu_custom_call" | custom-call | flops 1006632960 | bytes 7864320 | tf_op jit(solution)/shard_map/back_attention/pallas_call | solution.py:726
  206.4 6.8 %attention_grads.1 = (bf16[2,2,4,48,768]{4,3,2,1,0:T(8,128)(2,1)}, bf16[2,2,4,48,768]{4,3,2,1,0:T(8,128)(2,1)}, bf16[2,2,4,48,768]{4,3,2,1,0:T(8,128)(2,1)}, bf16[2,2,4,48,768]{4,3,2,1,0:T(8,128)(2,1)}) custom-call(s32[4]{0:T(128)} %pad_add_fusion.where, bf16[768,512]{1,0:T(8,128)(2,1)} %get-tuple-element.116.h1_t, ...), custom_call_target="tpu_custom_call" | custom-call | flops 2415919104 | bytes 9437184 | tf_op jit(solution)/shard_map/attention_grads/pallas_call | solution.py:764
  213.3 2.6 collective-permute-done.7.a_new
  215.9 2.0 collective-permute-done.8.b_new
  217.9 2.7 fold.5
  221.1 8.9 %back_third.1 = (f32[512,768]{1,0:T(8,128)}, f32[8,768]{1,0:T(8,128)}) custom-call(f32[512,768]{1,0:T(8,128)} %get-tuple-element.101.dr1, bf16[512,2304]{1,0:T(8,128)(2,1)} %get-tuple-element.129.dqkv, bf16[512,768]{1,0:T(8,128)(2,1)} %bitcast.67, bf16[32,576,384]{2,1,0:T(8,128)(2,1)} %bitcast.56, bf16[8,768]{1,0:T(8,128)(2,1)} %reshape.269.vec, ...), custom_call_target="tpu_custom_call" | custom-call | flops 1811939328 | bytes 8257536 | tf_op jit(solution)/shard_map/back_third/pallas_call | solution.py:812
  230.1 3.6 %fold.6 = (bf16[8,48,768]{2,1,0:T(8,128)(2,1)}, bf16[8,48,768]{2,1,0:T(8,128)(2,1)}, bf16[8,48,768]{2,1,0:T(8,128)(2,1)}, bf16[8,48,768]{2,1,0:T(8,128)(2,1)}) custom-call(bf16[2,8,48,768]{3,2,1,0:T(8,128)(2,1)} %bitcast.63, bf16[2,8,48,768]{3,2,1,0:T(8,128)(2,1)} %bitcast.25.a_new, bf16[2,8,48,768]{3,2,1,0:T(8,128)(2,1)} %bitcast.64, ...), custom_call_target="tpu_custom_call" | custom-call | flops 1179648 | bytes 7077888 | tf_op jit(solution)/shard_map/fold/pallas_call | solution.py:846
  234.1 1.6 collective-permute-start.14
  236.2 1.6 collective-permute-start.12
  237.7 0.7 lt.73
  239.8 1.2 slice.35
  241.0 1.3 pad.7.clone
  242.8 1.4 reduce.7
  245.5 1.3 fusion
  246.8 8.9 %collective-permute-done.11.a_new = bf16[4,48,768]{2,1,0:T(8,128)(2,1)} collective-permute-done((bf16[4,48,768]{2,1,0:T(8,128)(2,1)}, bf16[4,48,768]{2,1,0:T(8,128)(2,1)}, u32[]{:S(2)}, u32[]{:S(2)}) %collective-permute-start.11) | collective-permute-done | bytes 294944 | tf_op jit(solution)/shard_map/ppermute | solution.py:891
  255.7 2.1 join.2
  257.9 0.8 copy-done.2
  258.7 2.7 fold.7
  261.4 1.6 collective-permute-start.15
  263.0 1.6 collective-permute-start.16
  265.3 1.3 collective-permute-start.20
  266.6 1.4 collective-permute-start.21
  267.9 1.7 collective-permute-start.22
  270.6 3.2 %all-to-all-start.3 = ((f32[32,5,128]{2,1,0:T(8,128)}), f32[32,5,128]{2,1,0:T(8,128)S(1)}, u32[]{:S(2)}, u32[]{:S(2)}) async-start(f32[32,5,128]{2,1,0:T(8,128)} %bitcast.39), calls=%async_computation.3 | async-start | bytes 262144 | tf_op jit(solution)/shard_map/all_to_all | solution.py:1113
  275.2 2.1 join.3
  277.4 1.8 collective-permute-start.17
  279.2 2.4 collective-permute-start.18
  281.8 0.8 add_add_fusion
  282.6 2.4 all-to-all-done.3
  288.2 6.2 %collective-permute-done.18 = bf16[48,1536]{1,0:T(8,128)(2,1)S(1)} collective-permute-done((bf16[48,1536]{1,0:T(8,128)(2,1)}, bf16[48,1536]{1,0:T(8,128)(2,1)S(1)}, u32[]{:S(2)}, u32[]{:S(2)}) %collective-permute-start.18) | collective-permute-done | bytes 147488 | tf_op jit(solution)/shard_map/ppermute | solution.py:891
  294.3 1.0 add_add_fusion.1
  (122 shorter events, 21.4 us)
Async XLA Ops:
  7.2 114.4 %all-gather.3.cloned.1.call-start = ((), (), s32[]{:S(2)}) async-start(), calls=%async_computation.4 | async-start | bytes 14598144 | tf_op jit(solution)/shard_map/all_gather | solution.py:957
  10.4 53.4 %copy-start.18 = (bf16[192]{0:T(256)(128)(2,1)S(1)}, bf16[192]{0:T(256)(128)(2,1)}, u32[]{:S(2)}) copy-start(bf16[192]{0:T(256)(128)(2,1)} %param.29) | copy-start | bytes 1156
  10.4 53.5 %copy-start.15 = (bf16[8,48]{1,0:T(8,128)(2,1)S(1)}, bf16[8,48]{1,0:T(8,128)(2,1)}, u32[]{:S(2)}) copy-start(bf16[8,48]{1,0:T(8,128)(2,1)} %param.28) | copy-start | bytes 2308
  10.4 59.2 %copy-start.16 = (s32[32]{0:T(128)S(1)}, s32[32]{0:T(128)}, u32[]{:S(2)}) copy-start(s32[32]{0:T(128)} %param.30) | copy-start | bytes 388
  10.4 59.3 %copy-start.8 = (s32[1024]{0:T(1024)S(1)}, s32[1024]{0:T(1024)}, u32[]{:S(2)}) copy-start(s32[1024]{0:T(1024)} %param.31) | copy-start | bytes 12292
  60.8 9.5 %collective-permute-start = (bf16[32,768]{1,0:T(8,128)(2,1)}, bf16[32,768]{1,0:T(8,128)(2,1)S(1)}, u32[]{:S(2)}, u32[]{:S(2)}) collective-permute-start(bf16[32,768]{1,0:T(8,128)(2,1)} %image_forward.1), channel_id=1, source_target_pairs={{0,4},{1,5},{2,6},{3,7},{4,0},{5,1},{6,2},{7,3},{8,12},{9,13},{10,... | collective-permute-start | bytes 147464 | tf_op jit(solution)/shard_map/ppermute | solution.py:891
  64.6 48.3 %all-to-all-start = ((bf16[16,8,72]{2,1,0:T(8,128)(2,1)}), bf16[16,8,72]{2,1,0:T(8,128)(2,1)S(1)}, u32[]{:S(2)}, u32[]{:S(2)}) async-start(bf16[16,8,72]{2,1,0:T(8,128)(2,1)} %broadcast_in_dim.74), calls=%async_computation | async-start | bytes 65536 | tf_op jit(solution)/shard_map/all_to_all | solution.py:1014
  71.1 15.1 %collective-permute-start.1 = (bf16[64,768]{1,0:T(8,128)(2,1)S(1)}, bf16[64,768]{1,0:T(8,128)(2,1)S(1)}, u32[]{:S(2)}, u32[]{:S(2)}) collective-permute-start(bf16[64,768]{1,0:T(8,128)(2,1)S(1)} %pad_maximum_fusion.3), channel_id=1, source_target_pairs={{0,8},{1,9},{2,10},{3,11},{4,12},{5,13},{6,14},{7,15},{8,0},{9,1},... | collective-permute-start | bytes 294920 | tf_op jit(solution)/shard_map/ppermute | solution.py:891
  87.0 11.7 %collective-permute-start.2 = (bf16[128,768]{1,0:T(8,128)(2,1)S(1)}, bf16[128,768]{1,0:T(8,128)(2,1)S(1)}, u32[]{:S(2)}, u32[]{:S(2)}) collective-permute-start(bf16[128,768]{1,0:T(8,128)(2,1)S(1)} %pad_maximum_fusion.2), channel_id=1, source_target_pairs={{0,16},{1,17},{2,18},{3,19},{4,20},{5,21},{6,22},{7,23},{8,24},{9,... | collective-permute-start | bytes 589832 | tf_op jit(solution)/shard_map/ppermute | solution.py:891
  88.6 24.4 %copy-start.10 = (f32[1024]{0:T(1024)}, f32[1024]{0:T(1024)S(1)}, u32[]{:S(2)}) copy-start(f32[1024]{0:T(1024)S(1)} %broadcast_maximum_fusion) | copy-start | bytes 12292
  99.5 10.2 %collective-permute-start.3 = (bf16[256,768]{1,0:T(8,128)(2,1)S(1)}, bf16[256,768]{1,0:T(8,128)(2,1)S(1)}, u32[]{:S(2)}, u32[]{:S(2)}) collective-permute-start(bf16[256,768]{1,0:T(8,128)(2,1)S(1)} %pad_maximum_fusion.1), channel_id=1, source_target_pairs={{0,2},{1,3},{2,0},{3,1},{4,6},{5,7},{6,4},{7,5},{8,10},{9,11},{10,... | collective-permute-start | bytes 1179656 | tf_op jit(solution)/shard_map/ppermute | solution.py:891
  110.6 3.9 %collective-permute-start.4 = (bf16[512,768]{1,0:T(8,128)(2,1)}, bf16[512,768]{1,0:T(8,128)(2,1)S(1)}, u32[]{:S(2)}, u32[]{:S(2)}) collective-permute-start(bf16[512,768]{1,0:T(8,128)(2,1)} %get-tuple-element.168), channel_id=1, source_target_pairs={{0,1},{1,0},{2,3},{3,2},{4,5},{5,4},{6,7},{7,6},{8,9},{9,8},{10,11... | collective-permute-start | bytes 2359304 | tf_op jit(solution)/shard_map/ppermute | solution.py:891
  148.9 11.0 %all-to-all-start.1 = ((f32[32,8,128]{2,1,0:T(8,128)}), f32[32,8,128]{2,1,0:T(8,128)S(1)}, u32[]{:S(2)}, u32[]{:S(2)}) async-start(f32[32,8,128]{2,1,0:T(8,128)} %broadcast_in_dim.82), calls=%async_computation.1 | async-start | bytes 262144 | tf_op jit(solution)/shard_map/all_to_all | solution.py:1055
  159.9 0.6 copy-start
  160.5 15.4 %copy-start.7 = (bf16[32,3072]{1,0:T(8,128)(2,1)S(1)}, bf16[32,3072]{1,0:T(8,128)(2,1)}, u32[]{:S(2)}) copy-start(bf16[32,3072]{1,0:T(8,128)(2,1)} %get-tuple-element.143) | copy-start | bytes 589828
  175.4 17.7 %collective-permute-start.5 = (bf16[2,2,4,48,768]{4,3,2,1,0:T(8,128)(2,1)}, bf16[2,2,4,48,768]{4,3,2,1,0:T(8,128)(2,1)}, u32[]{:S(2)}, u32[]{:S(2)}) collective-permute-start(bf16[2,2,4,48,768]{4,3,2,1,0:T(8,128)(2,1)} %get-tuple-element.107), channel_id=1, source_target_pairs={{0,1},{1,0},{2,3},{3,2},{4,5},{5,4},{6,7},{7,6},{8,9},{9,8},{10,11... | collective-permute-start | bytes 3538952 | tf_op jit(solution)/shard_map/ppermute | solution.py:891
  175.7 17.4 %collective-permute-start.6 = (bf16[2,2,4,48,768]{4,3,2,1,0:T(8,128)(2,1)}, bf16[2,2,4,48,768]{4,3,2,1,0:T(8,128)(2,1)}, u32[]{:S(2)}, u32[]{:S(2)}) collective-permute-start(bf16[2,2,4,48,768]{4,3,2,1,0:T(8,128)(2,1)} %get-tuple-element.109), channel_id=1, source_target_pairs={{0,1},{1,0},{2,3},{3,2},{4,5},{5,4},{6,7},{7,6},{8,9},{9,8},{10,11... | collective-permute-start | bytes 3538952 | tf_op jit(solution)/shard_map/ppermute | solution.py:891
  179.0 66.5 %all-to-all-start.2 = ((bf16[32,32,576]{2,1,0:T(8,128)(2,1)}), bf16[32,32,576]{2,1,0:T(8,128)(2,1)S(1)}, u32[]{:S(2)}, u32[]{:S(2)}) async-start(bf16[32,32,576]{2,1,0:T(8,128)(2,1)} %pad_maximum_fusion), calls=%async_computation.2 | async-start | bytes 2621440 | tf_op jit(solution)/shard_map/all_to_all | solution.py:1083
  196.7 19.2 %collective-permute-start.7 = (bf16[2,4,48,768]{3,2,1,0:T(8,128)(2,1)}, bf16[2,4,48,768]{3,2,1,0:T(8,128)(2,1)S(1)}, u32[]{:S(2)}, u32[]{:S(2)}) collective-permute-start(bf16[2,4,48,768]{3,2,1,0:T(8,128)(2,1)} %bitcast.85), channel_id=1, source_target_pairs={{0,16},{1,17},{2,18},{3,19},{4,20},{5,21},{6,22},{7,23},{8,24},{9,... | collective-permute-start | bytes 1769480 | tf_op jit(solution)/shard_map/ppermute | solution.py:891
  198.3 19.6 %collective-permute-start.8 = (bf16[2,4,48,768]{3,2,1,0:T(8,128)(2,1)}, bf16[2,4,48,768]{3,2,1,0:T(8,128)(2,1)}, u32[]{:S(2)}, u32[]{:S(2)}) collective-permute-start(bf16[2,4,48,768]{3,2,1,0:T(8,128)(2,1)} %bitcast.84), channel_id=1, source_target_pairs={{0,2},{1,3},{2,0},{3,1},{4,6},{5,7},{6,4},{7,5},{8,10},{9,11},{10,... | collective-permute-start | bytes 1769480 | tf_op jit(solution)/shard_map/ppermute | solution.py:891
  215.9 2.0 copy-start.3
  220.6 9.5 %collective-permute-start.9 = (bf16[2,2,4,48,768]{4,3,2,1,0:T(8,128)(2,1)}, bf16[2,2,4,48,768]{4,3,2,1,0:T(8,128)(2,1)}, u32[]{:S(2)}, u32[]{:S(2)}) collective-permute-start(bf16[2,2,4,48,768]{4,3,2,1,0:T(8,128)(2,1)} %get-tuple-element.138), channel_id=1, source_target_pairs={{0,1},{1,0},{2,3},{3,2},{4,5},{5,4},{6,7},{7,6},{8,9},{9,8},{10,11... | collective-permute-start | bytes 3538952 | tf_op jit(solution)/shard_map/ppermute | solution.py:891
  220.6 9.5 %collective-permute-start.10 = (bf16[2,2,4,48,768]{4,3,2,1,0:T(8,128)(2,1)}, bf16[2,2,4,48,768]{4,3,2,1,0:T(8,128)(2,1)}, u32[]{:S(2)}, u32[]{:S(2)}) collective-permute-start(bf16[2,2,4,48,768]{4,3,2,1,0:T(8,128)(2,1)} %get-tuple-element.140), channel_id=1, source_target_pairs={{0,1},{1,0},{2,3},{3,2},{4,5},{5,4},{6,7},{7,6},{8,9},{9,8},{10,11... | collective-permute-start | bytes 3538952 | tf_op jit(solution)/shard_map/ppermute | solution.py:891
  230.1 14.8 %copy-start.1 = (f32[32,8,128]{2,1,0:T(8,128)S(1)}, f32[32,8,128]{2,1,0:T(8,128)}, u32[]{:S(2)}) copy-start(f32[32,8,128]{2,1,0:T(8,128)} %copy-done) | copy-start | bytes 393220
  233.7 24.2 %collective-permute-start.13 = (bf16[2,4,48,768]{3,2,1,0:T(8,128)(2,1)}, bf16[2,4,48,768]{3,2,1,0:T(8,128)(2,1)S(1)}, u32[]{:S(2)}, u32[]{:S(2)}) collective-permute-start(bf16[2,4,48,768]{3,2,1,0:T(8,128)(2,1)} %bitcast.83), channel_id=1, source_target_pairs={{0,16},{1,17},{2,18},{3,19},{4,20},{5,21},{6,22},{7,23},{8,24},{9,... | collective-permute-start | bytes 1769480 | tf_op jit(solution)/shard_map/ppermute | solution.py:891
  234.1 23.8 %collective-permute-start.14 = (bf16[2,4,48,768]{3,2,1,0:T(8,128)(2,1)}, bf16[2,4,48,768]{3,2,1,0:T(8,128)(2,1)}, u32[]{:S(2)}, u32[]{:S(2)}) collective-permute-start(bf16[2,4,48,768]{3,2,1,0:T(8,128)(2,1)} %bitcast.82), channel_id=1, source_target_pairs={{0,2},{1,3},{2,0},{3,1},{4,6},{5,7},{6,4},{7,5},{8,10},{9,11},{10,... | collective-permute-start | bytes 1769480 | tf_op jit(solution)/shard_map/ppermute | solution.py:891
  235.8 19.9 %collective-permute-start.11 = (bf16[4,48,768]{2,1,0:T(8,128)(2,1)}, bf16[4,48,768]{2,1,0:T(8,128)(2,1)}, u32[]{:S(2)}, u32[]{:S(2)}) collective-permute-start(bf16[4,48,768]{2,1,0:T(8,128)(2,1)} %get-tuple-element.126), channel_id=1, source_target_pairs={{0,2},{1,3},{2,0},{3,1},{4,6},{5,7},{6,4},{7,5},{8,10},{9,11},{10,... | collective-permute-start | bytes 884744 | tf_op jit(solution)/shard_map/ppermute | solution.py:891
  236.2 19.6 %collective-permute-start.12 = (bf16[4,48,768]{2,1,0:T(8,128)(2,1)}, bf16[4,48,768]{2,1,0:T(8,128)(2,1)}, u32[]{:S(2)}, u32[]{:S(2)}) collective-permute-start(bf16[4,48,768]{2,1,0:T(8,128)(2,1)} %get-tuple-element.128), channel_id=1, source_target_pairs={{0,16},{1,17},{2,18},{3,19},{4,20},{5,21},{6,22},{7,23},{8,24},{9,... | collective-permute-start | bytes 884744 | tf_op jit(solution)/shard_map/ppermute | solution.py:891
  246.8 17.8 %copy-start.12 = (s32[8,128]{1,0:T(8,128)S(1)}, s32[8,128]{1,0:T(8,128)}, u32[]{:S(2)}) copy-start(s32[8,128]{1,0:T(8,128)} %lt.75) | copy-start | bytes 12292
  246.8 17.8 %copy-start.13 = (f32[8,128]{1,0:T(8,128)S(1)}, f32[8,128]{1,0:T(8,128)}, u32[]{:S(2)}) copy-start(f32[8,128]{1,0:T(8,128)} %reduce_sum.48) | copy-start | bytes 12292
  246.8 17.8 %copy-start.17 = (s32[128]{0:T(128)S(1)}, s32[128]{0:T(128)}, u32[]{:S(2)}) copy-start(s32[128]{0:T(128)} %lt.71) | copy-start | bytes 1540
  246.8 22.8 %copy-start.11 = (f32[8,768]{1,0:T(8,128)S(1)}, f32[8,768]{1,0:T(8,128)}, u32[]{:S(2)}) copy-start(f32[8,768]{1,0:T(8,128)} %get-tuple-element.159) | copy-start | bytes 73732
  257.9 12.0 %copy-start.9 = (f32[16,192]{1,0:T(8,128)S(1)}, f32[16,192]{1,0:T(8,128)}, u32[]{:S(2)}) copy-start(f32[16,192]{1,0:T(8,128)} %reshape.297) | copy-start | bytes 36868
  257.9 12.0 %copy-start.14 = (f32[577]{0:T(1024)S(1)}, f32[577]{0:T(1024)}, u32[]{:S(2)}) copy-start(f32[577]{0:T(1024)} %pad.7.clone) | copy-start | bytes 6928
  257.9 0.8 copy-start.2
  261.4 20.4 %copy-start.4 = (f32[48,1536]{1,0:T(8,128)S(1)}, f32[48,1536]{1,0:T(8,128)}, u32[]{:S(2)}) copy-start(f32[48,1536]{1,0:T(8,128)} %get-tuple-element.149) | copy-start | bytes 884740
  261.4 12.4 %collective-permute-start.15 = (bf16[4,48,768]{2,1,0:T(8,128)(2,1)}, bf16[4,48,768]{2,1,0:T(8,128)(2,1)S(1)}, u32[]{:S(2)}, u32[]{:S(2)}) collective-permute-start(bf16[4,48,768]{2,1,0:T(8,128)(2,1)} %get-tuple-element.156), channel_id=1, source_target_pairs={{0,2},{1,3},{2,0},{3,1},{4,6},{5,7},{6,4},{7,5},{8,10},{9,11},{10,... | collective-permute-start | bytes 884744 | tf_op jit(solution)/shard_map/ppermute | solution.py:891
  263.0 10.8 %collective-permute-start.16 = (bf16[4,48,768]{2,1,0:T(8,128)(2,1)}, bf16[4,48,768]{2,1,0:T(8,128)(2,1)S(1)}, u32[]{:S(2)}, u32[]{:S(2)}) collective-permute-start(bf16[4,48,768]{2,1,0:T(8,128)(2,1)} %get-tuple-element.158), channel_id=1, source_target_pairs={{0,16},{1,17},{2,18},{3,19},{4,20},{5,21},{6,22},{7,23},{8,24},{9,... | collective-permute-start | bytes 884744 | tf_op jit(solution)/shard_map/ppermute | solution.py:891
  265.3 16.3 %collective-permute-start.20 = (bf16[48,1536]{1,0:T(8,128)(2,1)}, bf16[48,1536]{1,0:T(8,128)(2,1)S(1)}, u32[]{:S(2)}, u32[]{:S(2)}) collective-permute-start(bf16[48,1536]{1,0:T(8,128)(2,1)} %get-tuple-element.150), channel_id=1, source_target_pairs={{0,4},{1,5},{2,6},{3,7},{4,0},{5,1},{6,2},{7,3},{8,12},{9,13},{10,... | collective-permute-start | bytes 442376 | tf_op jit(solution)/shard_map/ppermute | solution.py:891
  266.6 15.2 %collective-permute-start.21 = (bf16[48,1536]{1,0:T(8,128)(2,1)}, bf16[48,1536]{1,0:T(8,128)(2,1)S(1)}, u32[]{:S(2)}, u32[]{:S(2)}) collective-permute-start(bf16[48,1536]{1,0:T(8,128)(2,1)} %get-tuple-element.151), channel_id=1, source_target_pairs={{0,8},{1,9},{2,10},{3,11},{4,12},{5,13},{6,14},{7,15},{8,0},{9,1},... | collective-permute-start | bytes 442376 | tf_op jit(solution)/shard_map/ppermute | solution.py:891
  267.9 13.8 %collective-permute-start.22 = (bf16[48,1536]{1,0:T(8,128)(2,1)}, bf16[48,1536]{1,0:T(8,128)(2,1)S(1)}, u32[]{:S(2)}, u32[]{:S(2)}) collective-permute-start(bf16[48,1536]{1,0:T(8,128)(2,1)} %get-tuple-element.152), channel_id=1, source_target_pairs={{0,12},{1,13},{2,14},{3,15},{4,8},{5,9},{6,10},{7,11},{8,4},{9,5},... | collective-permute-start | bytes 442376 | tf_op jit(solution)/shard_map/ppermute | solution.py:891
  270.6 14.4 %all-to-all-start.3 = ((f32[32,5,128]{2,1,0:T(8,128)}), f32[32,5,128]{2,1,0:T(8,128)S(1)}, u32[]{:S(2)}, u32[]{:S(2)}) async-start(f32[32,5,128]{2,1,0:T(8,128)} %bitcast.39), calls=%async_computation.3 | async-start | bytes 262144 | tf_op jit(solution)/shard_map/all_to_all | solution.py:1113
  273.8 0.7 copy-start.5
  274.5 0.7 copy-start.6
  277.4 10.8 %collective-permute-start.17 = (bf16[48,1536]{1,0:T(8,128)(2,1)}, bf16[48,1536]{1,0:T(8,128)(2,1)S(1)}, u32[]{:S(2)}, u32[]{:S(2)}) collective-permute-start(bf16[48,1536]{1,0:T(8,128)(2,1)} %get-tuple-element.165), channel_id=1, source_target_pairs={{0,4},{1,5},{2,6},{3,7},{4,0},{5,1},{6,2},{7,3},{8,12},{9,13},{10,... | collective-permute-start | bytes 442376 | tf_op jit(solution)/shard_map/ppermute | solution.py:891
  279.2 15.2 %collective-permute-start.18 = (bf16[48,1536]{1,0:T(8,128)(2,1)}, bf16[48,1536]{1,0:T(8,128)(2,1)S(1)}, u32[]{:S(2)}, u32[]{:S(2)}) collective-permute-start(bf16[48,1536]{1,0:T(8,128)(2,1)} %get-tuple-element.166), channel_id=1, source_target_pairs={{0,8},{1,9},{2,10},{3,11},{4,12},{5,13},{6,14},{7,15},{8,0},{9,1},... | collective-permute-start | bytes 442376 | tf_op jit(solution)/shard_map/ppermute | solution.py:891
  281.6 12.8 %collective-permute-start.19 = (bf16[48,1536]{1,0:T(8,128)(2,1)}, bf16[48,1536]{1,0:T(8,128)(2,1)S(1)}, u32[]{:S(2)}, u32[]{:S(2)}) collective-permute-start(bf16[48,1536]{1,0:T(8,128)(2,1)} %get-tuple-element.167), channel_id=1, source_target_pairs={{0,12},{1,13},{2,14},{3,15},{4,8},{5,9},{6,10},{7,11},{8,4},{9,5},... | collective-permute-start | bytes 442376 | tf_op jit(solution)/shard_map/ppermute | solution.py:891
Sparse Core Ops, SparseCore 0:
  10.9 110.6 all-gather.2
where the time goes:
time: 306 us; the launch traced here: 305 us
  Pallas kernels  147 us (48%)
  waiting for transfers between devices  57.4 us (19%)
  starting transfers between devices  43.4 us (14%)
  local copies, waits for them, and re-layouts  26.2 us (9%)
  between operations  17.6 us (6%)
  other arithmetic  12.1 us (4%)
    pallas_call x1, Pallas kernels, image_forward(): pl.pallas_call(image_kernel, name='image_forward', grid=(pairs // group,)...  50.3 us
    ppermute x23, waiting for transfers between devices, hop(): return lax.ppermute(array, AXES, shifted(x, y, z, core))  47.3 us
    ppermute x23, starting transfers between devices, hop(): return lax.ppermute(array, AXES, shifted(x, y, z, core))  29.2 us
    pallas_call x1, Pallas kernels, text_forward(): pl.pallas_call(functools.partial(text_forward_kernel, length), name='text...  23.2 us
    pallas_call x1, Pallas kernels, back_first(): pl.pallas_call(functools.partial(back_first_kernel, length), name='back_f...  14.8 us
    pallas_call x4, Pallas kernels, fold(): pl.pallas_call(fold_kernel, name='fold', grid=(steps,), in_specs=[pair] *...  12.6 us
    pallas_call x1, Pallas kernels, back_norm(): pl.pallas_call(functools.partial(back_norm_kernel, length), name='back_no...  10.8 us
    pallas_call x1, Pallas kernels, back_third(): pl.pallas_call(back_third_kernel, name='back_third', in_specs=[WHOLE, WHO...  8.95 us
  transfers between devices with their start and end apart: 28, of which 10 were waited for; matrix products, arithmetic and copies ran while one was open for 11% of the time, Pallas kernels for 33%

commit v1 on v0

--- a/solution.py
+++ b/solution.py
@@ -14,14 +14,13 @@
 F32 = jnp.float32
 AXES = ("dp", "fsdp")
 PX, PF = 2, 16
-VMEM_LIMIT = 62 * 1024 * 1024
-
-ANY = pl.BlockSpec(memory_space=pl.ANY)
+
+ANY = pl.BlockSpec(memory_space=pltpu.HBM)
 WHOLE = pl.BlockSpec(memory_space=pltpu.VMEM)
 
 
-def params(**more):
-    return pltpu.CompilerParams(vmem_limit_bytes=VMEM_LIMIT, **more)
+def params(mebibytes=62):
+    return pltpu.CompilerParams(vmem_limit_bytes=mebibytes * 1024 * 1024)
 
 
 def dot(a, b, ca=1, cb=0):
@@ -39,6 +38,13 @@
             step(i)
     else:
         lax.fori_loop(0, count // together, turn, 0)
+
+
+def move(pairs, sem, base=0):
+    copies = [pltpu.make_async_copy(a, b, sem.at[base + i]) for i, (a, b) in enumerate(pairs)]
+    for copy in copies:
+        copy.start()
+    return copies
 
 
 def normalize(values):
@@ -303,6 +309,25 @@
     return pltpu.VMEM(shape, BF)
 
 
+def contrast(low, images, live, same, groups, own, own_group, power, row_part, col_sum, loss_part):
+    scores = LOGIT_SCALE * dot(low, images[...], 1, 1)
+    exps = jnp.exp(scores)
+    live_own, same_own = own[:, 0:1], own[:, 1:2]
+    power[...] = exps
+    rows = jnp.sum(exps * live_own, axis=0, keepdims=True)
+    tiled = jnp.concatenate(
+        [rows[:, k * 128 : (k + 1) * 128] for k in range(rows.shape[1] // 128)], axis=0
+    )
+    for d in range(row_part.shape[0]):
+        row_part[d] = tiled
+    cols = jnp.sum(exps * live[...], axis=1, keepdims=True)
+    col_sum[...] = cols
+    pair = jnp.where(own_group[...] == groups[...], live_own * live[...], 0.0)
+    linear = pair * scores * (1.0 / same_own + 1.0 / same[...])
+    losses = live_own * jnp.log(cols) - jnp.sum(linear, axis=1, keepdims=True)
+    loss_part[...] = jnp.broadcast_to(jnp.sum(losses, axis=0, keepdims=True), loss_part.shape)
+
+
 def text_mask(size, length):
     row = lax.broadcasted_iota(jnp.int32, (size, size), 0) // length
     col = lax.broadcasted_iota(jnp.int32, (size, size), 1) // length
@@ -310,8 +335,9 @@
 
 
 def text_forward_kernel(
-    length, tok, packed, vec, ub, h1, qkv, att, r1, h2, slope, acts, pooled_out, low, wq, wo, wu, wd, total,
-    bias_row, sem
+    length, tok, packed, vec, ub, images_i, live, same, groups, own, own_group,
+    h1_o, qkv_o, att_o, r1_o, h2_o, slope_o, acts, pooled_out, power, row_part, col_sum, loss_part,
+    wq, wo, wu, wd, total, bias_row, h1, qkv, att, r1, h2, slope, sem, images, out_sem
 ):
     rows, width = tok.shape
     hidden = slope.shape[1]
@@ -338,6 +364,8 @@
         repeat(rows // blk, one, 2)
 
     norm_rows(tok, h1, v[0:1], v[1:2])
+    saves = move([(h1, h1_o)], out_sem)
+    (gathered,) = move([(images_i, images)], out_sem, 6)
     for copy in load["qkv"]:
         copy.wait()
 
@@ -346,6 +374,7 @@
         qkv[:, at] = (dot(h1[...], wq[:, :, at].reshape(width, 256)) + bias_row[:, at]).astype(BF)
 
     repeat(3 * width // 256, project, 3)
+    saves += move([(qkv, qkv_o)], out_sem, 1)
     low_lane = lax.broadcasted_iota(jnp.int32, (blk, 128), 1) < HEAD_DIM
     bias = text_mask(blk, length)
     cols = range(0, width, 128)
@@ -367,13 +396,16 @@
             att[at, c : c + 128] = dot(p, values).astype(BF)
 
     repeat(rows // blk, attend, 2)
+    saves += move([(att, att_o)], out_sem, 2)
     for copy in load["out"]:
         copy.wait()
     for c in range(0, width, 256):
         r1[:, c : c + 256] = tok[:, c : c + 256].astype(F32) + (
             dot(att[...], wo[:, :, c : c + 256].reshape(width, 256)) + v[4:5, c : c + 256]
         )
+    saves += move([(r1, r1_o)], out_sem, 3)
     norm_rows(r1, h2, v[5:6], v[6:7])
+    saves += move([(h2, h2_o)], out_sem, 4)
     for copy in load["up"]:
         copy.wait()
 
@@ -389,24 +421,33 @@
         acts[:, at] = sums.astype(BF)
 
     repeat(hidden // 256, expand, 3)
+    saves += move([(slope, slope_o)], out_sem, 5)
     for copy in load["down"]:
         copy.wait()
     mean_r1 = jnp.sum(r1[...].reshape(texts, length, width), axis=1) * (1.0 / length)
     pooled = mean_r1 + mean_down(total[...], length, natural(wd)) + v[7:8]
     pooled_out[...] = pooled
-    low[...] = unit_rows(pooled).astype(BF)
-
-
-def text_forward(tokens, packed, vec, ub, length, hidden):
+    gathered.wait()
+    contrast(
+        unit_rows(pooled).astype(BF), images, live, same, groups, own, own_group, power, row_part, col_sum, loss_part
+    )
+    for copy in saves:
+        copy.wait()
+
+
+def text_forward(
+    tokens, packed, vec, ub, images, live, same, groups, own, own_group, length, hidden, copies_of
+):
     rows, width = tokens.shape
     texts = rows // length
+    pairs = images.shape[0]
     shape = jax.ShapeDtypeStruct
     copies = PX * (3 + 1 + hidden // width + 1)
     return pl.pallas_call(
         functools.partial(text_forward_kernel, length),
         name="text_forward",
-        in_specs=[WHOLE, ANY, WHOLE, WHOLE],
-        out_specs=[WHOLE] * 9,
+        in_specs=[WHOLE, ANY, WHOLE, WHOLE, ANY] + [WHOLE] * 5,
+        out_specs=[ANY] * 6 + [WHOLE] * 6,
         out_shape=[
             shape((rows, width), BF),
             shape((rows, 3 * width), BF),
@@ -416,13 +457,24 @@
             shape((rows, hidden), BF),
             shape((texts, hidden), BF),
             shape((texts, width), F32),
-            shape((texts, width), BF),
+            shape((texts, pairs), F32),
+            shape((copies_of, pairs // 128, 128), F32),
+            shape((texts, 1), F32),
+            shape((8, 128), F32),
         ],
         scratch_shapes=[weight_scratch(w, width, hidden) for w in ("qkv", "out", "up", "down")]
         + [
             pltpu.VMEM((texts, hidden), F32),
             pltpu.VMEM((1, 3 * width), F32),
+            pltpu.VMEM((rows, width), BF),
+            pltpu.VMEM((rows, 3 * width), BF),
+            pltpu.VMEM((rows, width), BF),
+            pltpu.VMEM((rows, width), F32),
+            pltpu.VMEM((rows, width), BF),
+            pltpu.VMEM((rows, hidden), BF),
             pltpu.SemaphoreType.DMA((copies,)),
+            pltpu.VMEM((pairs, width), BF),
+            pltpu.SemaphoreType.DMA((7,)),
         ],
         compiler_params=params(),
         cost_estimate=pl.CostEstimate(
@@ -430,49 +482,17 @@
             bytes_accessed=2 * (4 * width * width + 2 * width * hidden + 12 * rows * width),
             transcendentals=rows * hidden,
         ),
-    )(tokens, packed, vec, ub)
-
-
-def contrast_kernel(low, images, live, same, groups, own, own_group, power, row_part, col_sum, loss_part):
-    scores = LOGIT_SCALE * dot(low[...], images[...], 1, 1)
-    exps = jnp.exp(scores)
-    live_own, same_own = own[:, 0:1], own[:, 1:2]
-    power[...] = exps
-    rows = jnp.sum(exps * live_own, axis=0, keepdims=True)
-    for k in range(row_part.shape[0]):
-        row_part[k : k + 1, :] = rows[:, k * 128 : (k + 1) * 128]
-    cols = jnp.sum(exps * live[...], axis=1, keepdims=True)
-    col_sum[...] = cols
-    pair = jnp.where(own_group[...] == groups[...], live_own * live[...], 0.0)
-    linear = pair * scores * (1.0 / same_own + 1.0 / same[...])
-    losses = live_own * jnp.log(cols) - jnp.sum(linear, axis=1, keepdims=True)
-    loss_part[...] = jnp.broadcast_to(jnp.sum(losses, axis=0, keepdims=True), loss_part.shape)
-
-
-def contrast(low, images, live, same, groups, own, own_group):
-    texts = low.shape[0]
-    pairs = images.shape[0]
-    shape = jax.ShapeDtypeStruct
-    return pl.pallas_call(
-        contrast_kernel,
-        name="contrast",
-        in_specs=[WHOLE] * 7,
-        out_specs=[WHOLE] * 4,
-        out_shape=[
-            shape((texts, pairs), F32),
-            shape((pairs // 128, 128), F32),
-            shape((texts, 1), F32),
-            shape((8, 128), F32),
-        ],
-        compiler_params=params(),
-    )(low, images, live, same, groups, own, own_group)
-
-
-def relative_kernel(where, h1, h2, att, h1_t, h2_t, att_t):
+    )(tokens, packed, vec, ub, images, live, same, groups, own, own_group)
+
+
+def relative_kernel(where, h1_i, h2_i, att_i, h1_o, h2_o, att_o, h1, h2, att, h1_t, h2_t, att_t, sem):
     width = h1.shape[1]
     block = width // PF
     my, mz, mc = where[1], where[2], where[3]
-    for src, dst in ((h2, h2_t), (h1, h1_t), (att, att_t)):
+    loads = move([(h2_i, h2), (h1_i, h1), (att_i, att)], sem)
+    saves = []
+    for n, (src, dst, out) in enumerate(((h2, h2_t, h2_o), (h1, h1_t, h1_o), (att, att_t, att_o))):
+        loads[n].wait()
         turned = src[...].T
         for z in range(4):
             for y in range(2):
@@ -482,6 +502,9 @@
                     dst[pl.ds(pl.multiple_of(place, block), block), :] = turned[
                         f * block : (f + 1) * block
                     ]
+        saves += move([(dst, out)], sem, 3 + n)
+    for copy in saves:
+        copy.wait()
 
 
 SMEM = pl.BlockSpec(memory_space=pltpu.SMEM)
@@ -492,9 +515,12 @@
     return pl.pallas_call(
         relative_kernel,
         name="relative_rows",
-        in_specs=[SMEM, WHOLE, WHOLE, WHOLE],
-        out_specs=[WHOLE] * 3,
+        in_specs=[SMEM, ANY, ANY, ANY],
+        out_specs=[ANY] * 3,
         out_shape=[jax.ShapeDtypeStruct((width, rows), BF)] * 3,
+        scratch_shapes=[pltpu.VMEM((rows, width), BF)] * 3
+        + [pltpu.VMEM((width, rows), BF)] * 3
+        + [pltpu.SemaphoreType.DMA((6,))],
         compiler_params=params(),
         cost_estimate=pl.CostEstimate(flops=0, bytes_accessed=12 * rows * width, transcendentals=0),
     )(where, h1, h2, att)
@@ -513,42 +539,69 @@
         for y in range(2):
             piece = low[(c * 2 + y) * 4 * block : (c * 2 + y + 1) * 4 * block].reshape(4, block, cols)
             if second:
-                outs[2 + c][y, x_rel, :, :, pl.ds(at, cols)] = piece
+                outs[2 + c, y, x_rel, :, :, pl.ds(at, cols)] = piece
             else:
-                outs[c][x_rel, y, :, :, pl.ds(at, cols)] = piece
-
-
-def back_first_kernel(
-    length,
-    where, power, row_all, col_sum, images, live, same, groups, own, own_group, factor, pooled, packed, slope,
-    h2_t, dy_out, dm_out, du, keep_a, send_a, keep_b, send_b, bias_up, down_bias, wd, dact, sem,
+                outs[c, x_rel, y, :, :, pl.ds(at, cols)] = piece
+
+
+def start_grads(parts, outs, sem, x):
+    return move(
+        [(parts.at[n, x], outs[n].at[x]) for n in range(2)]
+        + [(parts.at[n, :, x], outs[n].at[:, x]) for n in range(2, 4)],
+        sem,
+        4 * x,
+    )
+
+
+def back_one_kernel(
+    length, shard,
+    where, power, row_all, col_sum, images_i, live, same, groups, own, own_group, factor, pooled, packed, vec,
+    slope_i, h2_i, r1_i, acts,
+    factors_o, keep_a, send_a, keep_b, send_b, bias_up, down_bias, dr1_o, dz_o, da_o, sums, loss_rows,
+    factors, wd, wu, wo, dact, images, slope, h2_t, r1, du, dr1, dz_s, da_s, dy, parts, sem, in_sem, out_sem,
 ):
     rows, hidden = slope.shape
     texts = rows // length
     width = h2_t.shape[0]
-    loads = weight_copies(packed, "down", wd, sem, 0, width, hidden)
-    for copy in loads:
+    (gathered,) = move([(images_i, images)], in_sem)
+    down = weight_copies(packed, "down", wd, sem, 0, width, hidden)
+    up = weight_copies(packed, "up", wu, sem, len(down), width, hidden)
+    out = weight_copies(packed, "out", wo, sem, len(down) + len(up), width, hidden)
+    for copy in down:
         copy.start()
-    sums = row_all[...]
-    if sums.ndim == 3:
-        sums = jnp.sum(sums, axis=0)
-    row_sum = jnp.concatenate([sums[k : k + 1] for k in range(sums.shape[0])], axis=1)
+    saved = move([(slope_i, slope), (h2_i, h2_t)], in_sem, 1)
+    for copy in up + out:
+        copy.start()
+    saved += move([(r1_i, r1)], in_sem, 3)
+    totals = jnp.sum(row_all[...], axis=0)
+    row_sum = jnp.concatenate([totals[k : k + 1] for k in range(totals.shape[0])], axis=1)
     live_own, same_own = own[:, 0:1], own[:, 1:2]
     pair = factor[0:1, 0:1] * live_own * live[...]
     match = jnp.where(own_group[...] == groups[...], 1.0 / same_own + 1.0 / same[...], 0.0)
     grad_scores = pair * (power[...] * (1.0 / row_sum + 1.0 / col_sum[...]) - match)
+    gathered.wait()
     grad_low = LOGIT_SCALE * dot(grad_scores.astype(BF), images[...])
     pool = pooled[...]
     inverse = lax.rsqrt(jnp.sum(pool * pool, axis=-1, keepdims=True) + 1e-06)
     along = jnp.sum(pool * grad_low, axis=-1, keepdims=True)
-    dy = inverse * (grad_low - pool * (inverse * inverse * along)) * (1.0 / length)
-    dm = dy.astype(BF)
-    dy_out[...] = dy
-    dm_out[...] = dm
+    dy[...] = inverse * (grad_low - pool * (inverse * inverse * along)) * (1.0 / length)
+    dm = dy[...].astype(BF)
+    loss_rows[...] = jnp.broadcast_to(
+        jnp.sum(live[...] * jnp.log(row_sum), axis=1, keepdims=True), loss_rows.shape
+    )
+    parts_x, parts_f = shard
+    piece_x, piece_f = width // parts_x, hidden // parts_f
+    for f in range(parts_f):
+        left = acts[:, f * piece_f : (f + 1) * piece_f]
+        for x in range(parts_x):
+            factors[x * parts_f + f, :, piece_x:] = left
+            factors[x * parts_f + f, :, :piece_x] = dm[:, x * piece_x : (x + 1) * piece_x]
+    sent = move([(factors, factors_o)], out_sem, 11)
     down_bias[...] = length * jnp.sum(dm.astype(F32), axis=0, keepdims=True)
-    for copy in loads:
+    for copy in down:
         copy.wait()
     dact[...] = dot(dm, natural(wd), 1, 1)
+    saved[0].wait()
 
     def slopes(i):
         at = pl.ds(pl.multiple_of(i * 256, 256), 256)
@@ -558,74 +611,34 @@
         bias_up[:, at] = jnp.sum(part.astype(F32), axis=0, keepdims=True)
 
     repeat(hidden // 256, slopes, 3)
+    saved[1].wait()
     half = hidden // PX
-
-    def grads(i):
-        x, c = i // (width // 256), pl.multiple_of(i % (width // 256) * 256, 256)
-        first = (x ^ where[0]) * half + c
-        for second in range(2):
-            part = du[:, pl.ds(pl.multiple_of(first + second * width, 256), 256)]
-            put_grad(dot(h2_t[...], part), (keep_a, send_a, keep_b, send_b), x, c, second)
-
-    repeat(PX * width // 256, grads, 2)
-
-
-def back_first(
-    where, power, row_all, col_sum, images, live, same, groups, own, own_group, factor, pooled, packed, slope,
-    h2_t, length,
-):
-    rows, hidden = slope.shape
-    width = h2_t.shape[0]
-    texts = rows // length
-    shape = jax.ShapeDtypeStruct
-    return pl.pallas_call(
-        functools.partial(back_first_kernel, length),
-        name="back_first",
-        in_specs=[SMEM] + [WHOLE] * 11 + [ANY, WHOLE, WHOLE],
-        out_specs=[WHOLE] * 9,
-        out_shape=[
-            shape((texts, width), F32),
-            shape((texts, width), BF),
-            shape((rows, hidden), BF),
-            *grad_shapes(width),
-            shape((1, hidden), F32),
-            shape((1, width), F32),
-        ],
-        scratch_shapes=[
-            weight_scratch("down", width, hidden),
-            pltpu.VMEM((texts, hidden), F32),
-            pltpu.SemaphoreType.DMA((PX,)),
-        ],
-        compiler_params=params(),
-        cost_estimate=pl.CostEstimate(
-            flops=2 * rows * width * hidden, bytes_accessed=12 * width * hidden, transcendentals=0
-        ),
-    )(
-        where, power, row_all, col_sum, images, live, same, groups, own, own_group, factor, pooled, packed, slope,
-        h2_t,
-    )
-
-
-def back_norm_kernel(length, dy, du, r1, packed, vec, dr1, dz_s, da_s, sums, wu, wo, sem):
-    rows, width = r1.shape
-    hidden = du.shape[1]
-    up = weight_copies(packed, "up", wu, sem, 0, width, hidden)
-    out = weight_copies(packed, "out", wo, sem, len(up), width, hidden)
-    for copy in up + out:
-        copy.start()
+    outs = (keep_a, send_a, keep_b, send_b)
+    for x in range(PX):
+        first = (x ^ where[0]) * half
+
+        def grads(i):
+            c = pl.multiple_of(i * 256, 256)
+            for second in range(2):
+                part = du[:, pl.ds(pl.multiple_of(first + c + second * width, 256), 256)]
+                put_grad(dot(h2_t[...], part), parts, x, c, second)
+
+        repeat(width // 256, grads)
+        sent += start_grads(parts, outs, out_sem, x)
+
     v = vec[...].astype(F32)
     blk = 128
     for copy in up:
         copy.wait()
-    half = rows // 2
 
     def product(i):
-        at = pl.ds(pl.multiple_of(i * half, half), half)
+        at = pl.ds(pl.multiple_of(i * (rows // 2), rows // 2), rows // 2)
         dr1[at, :] = dot(du[at, :], natural(wu), 1, 1)
 
     repeat(2, product)
     sums[...] = jnp.zeros((8, width), F32)
     some = blk // length
+    saved[2].wait()
 
     def back(i):
         at = pl.ds(pl.multiple_of(i * blk, blk), blk)
@@ -643,41 +656,79 @@
         sums[0:1, :] += jnp.sum(low.astype(F32), axis=0, keepdims=True)
 
     repeat(rows // blk, back, 2)
+    sent += move([(dr1, dr1_o), (dz_s, dz_o)], out_sem, 8)
     for copy in out:
         copy.wait()
     da_s[...] = dot(dz_s[...], natural(wo), 1, 1).astype(BF)
-
-
-def back_norm(dy, du, r1, packed, vec, length):
-    rows, width = r1.shape
-    hidden = du.shape[1]
+    sent += move([(da_s, da_o)], out_sem, 10)
+    for copy in sent:
+        copy.wait()
+
+
+def back_one(
+    where, power, row_all, col_sum, images, live, same, groups, own, own_group, factor, pooled, packed, vec, slope,
+    h2_t, r1, acts, length, shard,
+):
+    rows, hidden = slope.shape
+    width = h2_t.shape[0]
+    texts = rows // length
+    payload = (shard[0] * shard[1], texts, width // shard[0] + hidden // shard[1])
     shape = jax.ShapeDtypeStruct
     return pl.pallas_call(
-        functools.partial(back_norm_kernel, length),
-        name="back_norm",
-        in_specs=[WHOLE] * 3 + [ANY, WHOLE],
-        out_specs=[WHOLE] * 4,
+        functools.partial(back_one_kernel, length, shard),
+        name="back_one",
+        in_specs=[SMEM] + [WHOLE] * 3 + [ANY] + [WHOLE] * 7 + [ANY, WHOLE, ANY, ANY, ANY, WHOLE],
+        out_specs=[ANY] * 5 + [WHOLE] * 2 + [ANY] * 3 + [WHOLE] * 2,
         out_shape=[
+            shape(payload, BF),
+            *grad_shapes(width),
+            shape((1, hidden), F32),
+            shape((1, width), F32),
             shape((rows, width), F32),
             shape((rows, width), BF),
             shape((rows, width), BF),
             shape((8, width), F32),
+            shape((8, 128), F32),
         ],
         scratch_shapes=[
+            pltpu.VMEM(payload, BF),
+            weight_scratch("down", width, hidden),
             weight_scratch("up", width, hidden),
             weight_scratch("out", width, hidden),
-            pltpu.SemaphoreType.DMA((PX * (1 + hidden // width),)),
+            pltpu.VMEM((texts, hidden), F32),
+            pltpu.VMEM(images.shape, BF),
+            pltpu.VMEM((rows, hidden), BF),
+            pltpu.VMEM((width, rows), BF),
+            pltpu.VMEM((rows, width), F32),
+            pltpu.VMEM((rows, hidden), BF),
+            pltpu.VMEM((rows, width), F32),
+            pltpu.VMEM((rows, width), BF),
+            pltpu.VMEM((rows, width), BF),
+            pltpu.VMEM((texts, width), F32),
+            pltpu.VMEM((4,) + grad_shapes(width)[0].shape, BF),
+            pltpu.SemaphoreType.DMA((PX * (2 + hidden // width),)),
+            pltpu.SemaphoreType.DMA((4,)),
+            pltpu.SemaphoreType.DMA((12,)),
         ],
         compiler_params=params(),
         cost_estimate=pl.CostEstimate(
-            flops=2 * rows * width * (hidden + width), bytes_accessed=6 * width * hidden, transcendentals=0
+            flops=2 * rows * width * (2 * hidden + width), bytes_accessed=16 * width * hidden, transcendentals=0
         ),
-    )(dy, du, r1, packed, vec)
-
-
-def back_attention_kernel(length, qkv, da_s, dqkv, sums):
+    )(
+        where, power, row_all, col_sum, images, live, same, groups, own, own_group, factor, pooled, packed, vec,
+        slope, h2_t, r1, acts,
+    )
+
+
+def back_two_kernel(
+    length, where, qkv_i, da_i, dz_i, h1_i, att_i, dqkv_o, keep_a, send_a, keep_b, send_b, sums,
+    qkv, da_s, dz, h1_t, att_t, dqkv, parts, sem, out_sem,
+):
     rows, width = da_s.shape
     blk = 128
+    loads = move([(qkv_i, qkv), (da_i, da_s), (att_i, att_t), (dz_i, dz), (h1_i, h1_t)], sem)
+    for copy in loads[:2]:
+        copy.wait()
     low_lane = lax.broadcasted_iota(jnp.int32, (blk, 128), 1) < HEAD_DIM
     bias = text_mask(blk, length)
     cols = range(0, width, 128)
@@ -718,67 +769,66 @@
     sums[0:1, :] = jnp.sum(dqkv[:, :width].astype(F32), axis=0, keepdims=True)
     sums[1:2, :] = jnp.sum(dqkv[:, 2 * width :].astype(F32), axis=0, keepdims=True)
     sums[2:8, :] = jnp.zeros((6, width), F32)
-
-
-def back_attention(qkv, da, length):
+    sent = move([(dqkv, dqkv_o)], out_sem, 8)
+    for copy in loads[2:]:
+        copy.wait()
+    piece = width // PX
+    outs = (keep_a, send_a, keep_b, send_b)
+    for x in range(PX):
+        other = x ^ where[0]
+        first = other * (3 * piece)
+
+        def chunk(i):
+            c = pl.multiple_of(i * 256, 256)
+            part = dqkv[:, pl.ds(pl.multiple_of(first + c, 128), 256)]
+            put_grad(dot(h1_t[...], part), parts, x, c, 0)
+
+        repeat(width // 256, chunk)
+        part = dqkv[:, pl.ds(pl.multiple_of(first + width, 128), piece)]
+        put_grad(dot(h1_t[...], part), parts, x, 0, 1)
+        part = dz[:, pl.ds(pl.multiple_of(other * piece, 128), piece)]
+        put_grad(dot(att_t[...], part), parts, x, piece, 1)
+        sent += start_grads(parts, outs, out_sem, x)
+    for copy in sent:
+        copy.wait()
+
+
+def back_two(where, qkv, da, dz, h1_t, att_t, length):
     rows, width = da.shape
     shape = jax.ShapeDtypeStruct
     return pl.pallas_call(
-        functools.partial(back_attention_kernel, length),
-        name="back_attention",
-        in_specs=[WHOLE] * 2,
-        out_specs=[WHOLE] * 2,
-        out_shape=[shape((rows, 3 * width), BF), shape((8, width), F32)],
+        functools.partial(back_two_kernel, length),
+        name="back_two",
+        in_specs=[SMEM] + [ANY] * 5,
+        out_specs=[ANY] * 5 + [WHOLE],
+        out_shape=[shape((rows, 3 * width), BF), *grad_shapes(width), shape((8, width), F32)],
+        scratch_shapes=[
+            pltpu.VMEM((rows, 3 * width), BF),
+            pltpu.VMEM((rows, width), BF),
+            pltpu.VMEM((rows, width), BF),
+            pltpu.VMEM((width, rows), BF),
+            pltpu.VMEM((width, rows), BF),
+            pltpu.VMEM((rows, 3 * width), BF),
+            pltpu.VMEM((4,) + grad_shapes(width)[0].shape, BF),
+            pltpu.SemaphoreType.DMA((5,)),
+            pltpu.SemaphoreType.DMA((9,)),
+        ],
         compiler_params=params(),
         cost_estimate=pl.CostEstimate(
-            flops=2 * rows * width * 1280, bytes_accessed=20 * rows * width, transcendentals=rows * width
+            flops=2 * rows * width * (1280 + 4 * width), bytes_accessed=20 * rows * width, transcendentals=rows * width
         ),
-    )(qkv, da)
-
-
-def attention_grads_kernel(where, h1_t, att_t, dqkv, dz, keep_a, send_a, keep_b, send_b):
-    width = h1_t.shape[0]
-    piece = width // PX
-    outs = (keep_a, send_a, keep_b, send_b)
-
-    def part_of(x):
-        other = x ^ where[0]
-        first = other * (3 * piece)
-
-        def chunk(i):
-            c = pl.multiple_of(i * 256, 256)
-            part = dqkv[:, pl.ds(pl.multiple_of(first + c, 128), 256)]
-            put_grad(dot(h1_t[...], part), outs, x, c, 0)
-
-        repeat(width // 256, chunk, 3)
-        part = dqkv[:, pl.ds(pl.multiple_of(first + width, 128), piece)]
-        put_grad(dot(h1_t[...], part), outs, x, 0, 1)
-        part = dz[:, pl.ds(pl.multiple_of(other * piece, 128), piece)]
-        put_grad(dot(att_t[...], part), outs, x, piece, 1)
-
-    repeat(PX, part_of)
-
-
-def attention_grads(where, h1_t, att_t, dqkv, dz):
-    width, rows = h1_t.shape
-    return pl.pallas_call(
-        attention_grads_kernel,
-        name="attention_grads",
-        in_specs=[SMEM] + [WHOLE] * 4,
-        out_specs=[WHOLE] * 4,
-        out_shape=grad_shapes(width),
-        compiler_params=params(),
-        cost_estimate=pl.CostEstimate(
-            flops=8 * rows * width * width, bytes_accessed=8 * width * width + 12 * rows * width, transcendentals=0
-        ),
-    )(where, h1_t, att_t, dqkv, dz)
-
-
-def back_third_kernel(dr1, dqkv, tok, packed, vec, sums, bias_sums, down_bias, dx, all_sums, wq, sem):
+    )(where, qkv, da, dz, h1_t, att_t)
+
+
+def back_third_kernel(
+    parts_f, dr1_i, dqkv_i, tok_i, packed, vec, sums, bias_sums, down_bias, bias_up, loss_part, dx_o, share, all_sums, wq, dr1, tok, dx, sem, dqkv, own_sem
+):
     rows, width = tok.shape
     loads = weight_copies(packed, "qkv", wq, sem, 0, width, width)
     for copy in loads:
         copy.start()
+    saved = move([(dqkv_i, dqkv), (dr1_i, dr1), (tok_i, tok)], own_sem)
+    saved[0].wait()
     v = vec[...].astype(F32)
     for copy in loads:
         copy.wait()
@@ -789,6 +839,8 @@
         dx[at, :] = dot(dqkv[at, :], natural(wq), 1, 1)
 
     repeat(2, product)
+    for copy in saved[1:]:
+        copy.wait()
     all_sums[0:2, :] = jnp.zeros((2, width), F32)
     blk = 128
 
@@ -801,29 +853,49 @@
         dx[at, :] = dr1[at, :] + norm_back(grad, hat, inverse, v[0:1])
 
     repeat(rows // blk, back, 2)
+    (save,) = move([(dx, dx_o)], own_sem, 3)
     all_sums[2:4, :] = bias_sums[0:2, :]
     all_sums[4:7, :] = sums[0:3, :]
     all_sums[7:8, :] = down_bias[...]
-
-
-def back_third(dr1, dqkv, tok, packed, vec, sums, bias_sums, down_bias):
+    every = all_sums[...]
+    piece, tall = width // parts_f, bias_up.shape[1] // parts_f
+    devices = share.shape[0]
+    used = piece + tall // 8
+    for f in range(parts_f):
+        bias = bias_up[:, f * tall : (f + 1) * tall]
+        bias = jnp.concatenate([bias[:, r * tall // 8 : (r + 1) * tall // 8] for r in range(8)], axis=0)
+        block = jnp.concatenate(
+            [every[:, f * piece : (f + 1) * piece], bias, loss_part[:, : 128 - used]], axis=1
+        )
+        for x in range(devices // parts_f):
+            share[x * parts_f + f] = block
+    save.wait()
+
+
+def back_third(dr1, dqkv, tok, packed, vec, sums, bias_sums, down_bias, bias_up, loss_part, shard):
     rows, width = tok.shape
     shape = jax.ShapeDtypeStruct
     return pl.pallas_call(
-        back_third_kernel,
+        functools.partial(back_third_kernel, shard[1]),
         name="back_third",
-        in_specs=[WHOLE, WHOLE, WHOLE, ANY, WHOLE, WHOLE, WHOLE, WHOLE],
-        out_specs=[WHOLE] * 2,
-        out_shape=[shape((rows, width), F32), shape((8, width), F32)],
+        in_specs=[ANY, ANY, ANY, ANY] + [WHOLE] * 6,
+        out_specs=[ANY, WHOLE],
+        out_shape=[shape((rows, width), F32), shape((shard[0] * shard[1], 8, 128), F32)],
         scratch_shapes=[
+            pltpu.VMEM((8, width), F32),
             weight_scratch("qkv", width, width),
+            pltpu.VMEM((rows, width), F32),
+            pltpu.VMEM((rows, width), BF),
+            pltpu.VMEM((rows, width), F32),
             pltpu.SemaphoreType.DMA((PX * 3,)),
+            pltpu.VMEM((rows, 3 * width), BF),
+            pltpu.SemaphoreType.DMA((4,)),
         ],
         compiler_params=params(),
         cost_estimate=pl.CostEstimate(
             flops=6 * rows * width * width, bytes_accessed=14 * width * width, transcendentals=0
         ),
-    )(dr1, dqkv, tok, packed, vec, sums, bias_sums, down_bias)
+    )(dr1, dqkv, tok, packed, vec, sums, bias_sums, down_bias, bias_up, loss_part)
 
 
 def fold_kernel(a_own, a_new, b_own, b_new, a_keep, a_send, b_keep, b_send):
@@ -850,7 +922,7 @@
         in_specs=[pair] * 4,
         out_specs=[one] * 4,
         out_shape=[jax.ShapeDtypeStruct((rest, rows, cols), BF)] * 4,
-        compiler_params=params(),
+        compiler_params=params(18),
         cost_estimate=pl.CostEstimate(
             flops=4 * rest * rows * cols, bytes_accessed=24 * rest * rows * cols, transcendentals=0
         ),
@@ -875,7 +947,7 @@
         in_specs=[WHOLE] * 4,
         out_specs=[WHOLE] * 4,
         out_shape=[shape((rows, 2 * cols), F32)] + [shape((rows, 2 * cols), BF)] * 3,
-        compiler_params=params(),
+        compiler_params=params(6),
         cost_estimate=pl.CostEstimate(
             flops=16 * rows * cols, bytes_accessed=40 * rows * cols, transcendentals=0
         ),
@@ -916,10 +988,24 @@
     return join(keep_a, new_a, keep_b, new_b)
 
 
-def third_step(parts):
+def total_kernel(stay, one, two, three, *outs):
+    total = stay[...] + one[...].astype(F32) + two[...].astype(F32) + three[...].astype(F32)
+    at = 0
+    for out in outs:
+        out[...] = total[:, at : at + out.shape[1]]
+        at += out.shape[1]
+
+
+def third_step(parts, splits):
     stay, one, two, three = parts
-    others = [hop(one, z=1), hop(two, z=2), hop(three, z=3)]
-    return stay + sum(o.astype(F32) for o in others)
+    return pl.pallas_call(
+        total_kernel,
+        name="total",
+        in_specs=[WHOLE] * 4,
+        out_specs=[WHOLE] * len(splits),
+        out_shape=[jax.ShapeDtypeStruct((stay.shape[0], n), F32) for n in splits],
+        compiler_params=params(4),
+    )(stay, hop(one, z=1), hop(two, z=2), hop(three, z=3))
 
 
 def natural_grad(keep_a, send_a, keep_b, send_b):
@@ -1047,73 +1133,53 @@
     factor = jnp.broadcast_to(LOSS_WEIGHT / (2.0 * live_total), (1, 128))
 
     tokens = text_tokens.reshape(cap * length, width)
-    h1, qkv, att, r1, h2, slope, acts, pooled, low = text_forward(tokens, packed, vec, ub, length, hidden)
-    power, row_part, col_sum, loss_part = contrast(
-        low, images, live_row, same_row, group_row, own, own_group
+    h1, qkv, att, r1, h2, slope, acts, pooled, power, row_part, col_sum, loss_part = text_forward(
+        tokens, packed, vec, ub, images, live_row, same_row, group_row, own, own_group, length, hidden,
+        devices if grid_mesh else 1,
     )
-    if devices <= 32:
-        row_all = lax.all_to_all(
-            jnp.broadcast_to(row_part[None], (devices,) + row_part.shape), AXES, 0, 0, tiled=True
-        )
-        row_sum = jnp.sum(row_all, axis=0)
+    if grid_mesh:
+        row_all = lax.all_to_all(row_part, AXES, 0, 0, tiled=True)
     else:
         row_all = lax.psum(row_part, AXES)
-        row_sum = row_all
     h1_t, h2_t, att_t = relative_rows(where, h1, h2, att)
-    dy, dm, du, *up_parts, bias_up, down_bias = back_first(
+    factors, *up_parts, bias_up, down_bias, dr1, dz, da, sums, loss_rows = back_one(
         where, power, row_all, col_sum, images, live_row, same_row, group_row, own, own_group, factor, pooled,
-        packed, slope, h2_t, length,
+        packed, vec, slope, h2_t, r1, acts, length, (dp, fsdp),
     )
-    dr1, dz, da, sums = back_norm(dy, du, r1, packed, vec, length)
+    dqkv, *att_parts, bias_sums = back_two(where, qkv, da, dz, h1_t, att_t, length)
+
+    both = lax.all_to_all(factors, AXES, 0, 0, tiled=True).reshape(pairs, width // dp + hidden // fsdp)
+    grad_down = dot(both[:, width // dp :], both[:, : width // dp], 0, 0)
+
     if grid_mesh:
-        up_parts = core_step(up_parts, da)
-        (da,) = after((da,), *up_parts)
-    dqkv, bias_sums = back_attention(qkv, da, length)
-    att_parts = attention_grads(where, h1_t, att_t, dqkv, dz)
-    if grid_mesh:
-        up_parts = first_step(up_parts, *att_parts)
-        dqkv, *att_parts = after((dqkv, *att_parts), *up_parts)
-    dx, vec_grads = back_third(dr1, dqkv, tokens, packed, vec, sums, bias_sums, down_bias)
-    rows_of = hidden // fsdp
-    cols_of = width // dp
-    left = jnp.swapaxes(acts.reshape(cap, fsdp, rows_of), 0, 1)
-    left = jnp.broadcast_to(left[None], (dp, fsdp, cap, rows_of)).reshape(devices, cap, rows_of)
-    right = jnp.swapaxes(dm.reshape(cap, dp, cols_of), 0, 1)
-    right = jnp.broadcast_to(right[:, None], (dp, fsdp, cap, cols_of)).reshape(devices, cap, cols_of)
-    both = lax.all_to_all(jnp.concatenate([left, right], axis=2), AXES, 0, 0, tiled=True)
-    both = both.reshape(pairs, rows_of + cols_of)
-    grad_down = dot(both[:, :rows_of], both[:, rows_of:], 0, 0)
-
-    if grid_mesh:
-        att_parts = core_step(att_parts, dx)
+        up_parts = core_step(up_parts, *att_parts)
+        (att_keep,) = after((att_parts[0],), *up_parts)
+        att_parts = core_step([att_keep] + att_parts[1:])
+        (dqkv,) = after((dqkv,), *att_parts)
+        dx, share = back_third(
+            dr1, dqkv, tokens, packed, vec, sums, bias_sums, down_bias, bias_up, loss_part, (dp, fsdp)
+        )
+        up_parts = first_step(up_parts, dx)
+        att_parts = first_step(att_parts, grad_down, *up_parts)
         up_parts = second_step(up_parts, *att_parts)
-        att_parts = first_step(att_parts, grad_down, *up_parts)
-        (vec_grads,) = after((vec_grads,), *att_parts)
-        grad_up = third_step(up_parts)
-        grad_attn = third_step(second_step(att_parts))
-        grad_qkv, grad_out = grad_attn[:, : 3 * width // dp], grad_attn[:, 3 * width // dp :]
+        (share,) = after((share,), *att_parts)
+        att_parts = second_step(att_parts, *up_parts)
+        (grad_up,) = third_step(up_parts, (hidden // dp,))
+        grad_qkv, grad_out = third_step(att_parts, (3 * width // dp, width // dp))
     else:
+        dx, share = back_third(
+            dr1, dqkv, tokens, packed, vec, sums, bias_sums, down_bias, bias_up, loss_part, (dp, fsdp)
+        )
         grad_attn = natural_grad(*att_parts)
         grad_up = scatter_columns(natural_grad(*up_parts), dp, fsdp)
         grad_qkv = scatter_columns(grad_attn[:, :, : 3 * width // PX], dp, fsdp)
         grad_out = scatter_columns(grad_attn[:, :, 3 * width // PX :], dp, fsdp)
 
-    share = jnp.concatenate(
-        [
-            jnp.swapaxes(vec_grads.reshape(8, fsdp, part), 0, 1).reshape(fsdp, 8 * part),
-            bias_up.reshape(fsdp, rows_of),
-            jnp.broadcast_to(loss_part[0, 0].reshape(1, 1), (fsdp, 1)),
-        ],
-        axis=1,
-    )
-    used = share.shape[1]
-    padded = -(-used // 128) * 128
-    share = jnp.pad(share, ((0, 0), (0, padded - used))).reshape(fsdp, padded // 128, 128)
-    share = jnp.broadcast_to(share[None], (dp,) + share.shape).reshape(devices, padded // 128, 128)
-    share = jnp.sum(lax.all_to_all(share, AXES, 0, 0, tiled=True), axis=0).reshape(padded)
-    grad_vec = share[: 8 * part].reshape(8, part)
-    grad_bias = share[8 * part : 8 * part + rows_of]
-    loss = (share[used - 1] + jnp.sum(live * jnp.log(row_sum.reshape(pairs)))) / (2.0 * live_total)
+    share = jnp.sum(lax.all_to_all(share, AXES, 0, 0, tiled=True), axis=0)
+    grad_vec = share[:, :part]
+    tall = hidden // fsdp // 8
+    grad_bias = share[:, part : part + tall].reshape(hidden // fsdp)
+    loss = (share[0, part + tall] + loss_rows[0, 0]) / (2.0 * live_total)
 
     return (
         loss,

time: 306 us -> 280 us (0.915)
  Pallas kernels: 147 us -> 129 us
  local copies, waits for them, and re-layouts: 26.2 us -> 17 us
  other arithmetic: 12.1 us -> 6.66 us
  waiting for transfers between devices: 57.4 us -> 60.9 us
    ppermute x23, waiting for transfers between devices: 47.3 us -> 58.2 us  [hop(): return lax.ppermute(array, AXES, shifted(x, y, z, core))]
    pallas_call x7 -> x6, Pallas kernels: 54.4 us -> 44.5 us  [the longest x1 17.7 us: back_one(): pl.pallas_call(functools.partial(back_one_kernel, length, shard), name='b...]
    all_gather x1, waiting for transfers between devices: 4.9 us -> 0.01 us  [gather_packed(): return lax.all_gather(pack_block(qkv, out, up, down), AXES, axis=0)]
    pallas_call x2, Pallas kernels: 4.29 us -> 0.26 us  [join(): pl.pallas_call(join_kernel, name='join', in_specs=[WHOLE] * 4, out_specs=...]
    pallas_call x4, Pallas kernels: 12.6 us -> 8.71 us  [fold(): pl.pallas_call(fold_kernel, name='fold', grid=(steps,), in_specs=[pair] *...]
  transfers between devices with their start and end apart: 28 -> 28, of which waited for: 10 -> 12; matrix products, arithmetic and copies ran while one was open for 11% -> 8% of each run, Pallas kernels for 33% -> 31%
where the time goes in v1:
time: 280 us; the launch traced here: 279 us
  Pallas kernels  129 us (46%)
  waiting for transfers between devices  60.9 us (22%)
  starting transfers between devices  45.8 us (16%)
  between operations  17.4 us (6%)
  local copies, waits for them, and re-layouts  17 us (6%)
  other arithmetic  6.66 us (2%)
    ppermute x23, waiting for transfers between devices, hop(): return lax.ppermute(array, AXES, shifted(x, y, z, core))  58.2 us
    pallas_call x1, Pallas kernels, image_forward(): pl.pallas_call(image_kernel, name='image_forward', grid=(pairs // group,)...  50.5 us
    ppermute x23, starting transfers between devices, hop(): return lax.ppermute(array, AXES, shifted(x, y, z, core))  26.8 us
    pallas_call x1, Pallas kernels, text_forward(): pl.pallas_call(functools.partial(text_forward_kernel, length), name='text...  22.9 us
    pallas_call x1, Pallas kernels, back_one(): pl.pallas_call(functools.partial(back_one_kernel, length, shard), name='b...  17.7 us
    pallas_call x1, Pallas kernels, back_two(): pl.pallas_call(functools.partial(back_two_kernel, length), name='back_two...  12.7 us
    pallas_call x1, Pallas kernels, back_third(): pl.pallas_call(functools.partial(back_third_kernel, shard[1]), name='back...  9.01 us
    pallas_call x4, Pallas kernels, fold(): pl.pallas_call(fold_kernel, name='fold', grid=(steps,), in_specs=[pair] *...  8.71 us
  transfers between devices with their start and end apart: 28, of which 12 were waited for; matrix products, arithmetic and copies ran while one was open for 8% of the time, Pallas kernels for 31%

profile of v1, /device:TPU:0, one launch (start us, length us, event | category | flops | bytes accessed | tf_op | source)
XLA Modules:
  0.0 278.9 jit_solution(7332310326677091701)
XLA Ops:
  7.2 1.9 pack_block.1
  9.1 0.7 reshape.221
  9.8 0.8 pad_maximum_fusion.3
  11.2 7.4 %all-to-all-start = ((bf16[16,8,72]{2,1,0:T(8,128)(2,1)}), bf16[16,8,72]{2,1,0:T(8,128)(2,1)S(1)}, u32[]{:S(2)}, u32[]{:S(2)}) async-start(bf16[16,8,72]{2,1,0:T(8,128)(2,1)} %broadcast_in_dim.42), calls=%async_computation | async-start | bytes 65536 | tf_op jit(solution)/shard_map/all_to_all | solution.py:1100
  18.6 1.3 reshape.224.ub
  19.9 50.5 %image_forward.1 = bf16[32,768]{1,0:T(8,128)(2,1)} custom-call(bf16[50,32,768]{2,1,0:T(8,128)(2,1)} %bitcast.63, bf16[768,2304]{1,0:T(8,128)(2,1)} %wq_h.1, bf16[768,768]{1,0:T(8,128)(2,1)} %wo_h.1, bf16[768,3072]{1,0:T(8,128)(2,1)} %wu_h.1, bf16[3072,768]{1,0:T(8,128)(2,1)} %wd_h.1, bf16[8,768]{1,0:T(8,128)(2,1)} %vec.1, bf16[1,3072]{1,0:T(2,128)(2,1)} %reshape.224.ub), custom_call_target="tpu_custom_call" | custom-call | flops 15099494400 | bytes 16613376 | tf_op jit(solution)/shard_map/image_forward/pallas_call | solution.py:229
  70.4 2.0 collective-permute-start
  73.1 6.2 %collective-permute-done = bf16[32,768]{1,0:T(8,128)(2,1)S(1)} collective-permute-done((bf16[32,768]{1,0:T(8,128)(2,1)}, bf16[32,768]{1,0:T(8,128)(2,1)S(1)}, u32[]{:S(2)}, u32[]{:S(2)}) %collective-permute-start) | collective-permute-done | bytes 49184 | tf_op jit(solution)/shard_map/ppermute | solution.py:963
  79.3 0.8 pad_maximum_fusion.2
  80.1 1.5 collective-permute-start.1
  81.7 1.4 constant_dynamic-update-slice_fusion.4
  83.1 11.0 %collective-permute-done.1 = bf16[64,768]{1,0:T(8,128)(2,1)S(1)} collective-permute-done((bf16[64,768]{1,0:T(8,128)(2,1)S(1)}, bf16[64,768]{1,0:T(8,128)(2,1)S(1)}, u32[]{:S(2)}, u32[]{:S(2)}) %collective-permute-start.1) | collective-permute-done | bytes 98336 | tf_op jit(solution)/shard_map/ppermute | solution.py:963
  94.1 0.8 pad_maximum_fusion.1
  94.9 1.5 collective-permute-start.2
  96.4 5.9 %collective-permute-done.2 = bf16[128,768]{1,0:T(8,128)(2,1)S(1)} collective-permute-done((bf16[128,768]{1,0:T(8,128)(2,1)S(1)}, bf16[128,768]{1,0:T(8,128)(2,1)S(1)}, u32[]{:S(2)}, u32[]{:S(2)}) %collective-permute-start.2) | collective-permute-done | bytes 196640 | tf_op jit(solution)/shard_map/ppermute | solution.py:963
  102.3 0.8 pad_maximum_fusion
  103.2 1.5 collective-permute-start.3
  105.3 0.7 constant_dynamic-update-slice_fusion.2
  106.0 0.7 constant_dynamic-update-slice_fusion.1
  106.7 7.2 %collective-permute-done.3 = bf16[256,768]{1,0:T(8,128)(2,1)S(1)} collective-permute-done((bf16[256,768]{1,0:T(8,128)(2,1)S(1)}, bf16[256,768]{1,0:T(8,128)(2,1)S(1)}, u32[]{:S(2)}, u32[]{:S(2)}) %collective-permute-start.3) | collective-permute-done | bytes 393248 | tf_op jit(solution)/shard_map/ppermute | solution.py:963
  113.8 0.8 constant_dynamic-update-slice_fusion
  114.8 0.7 reshape.246.live
  115.7 0.7 copy.36.own_group
  116.4 0.7 copy.35.own
  117.1 0.7 reshape.223.ub
  117.9 0.7 reshape.222.vec
  119.3 1.4 bitcast_select_fusion.images_i
  120.7 22.9 %text_forward.1 = (bf16[512,768]{1,0:T(8,128)(2,1)}, bf16[512,2304]{1,0:T(8,128)(2,1)}, bf16[512,768]{1,0:T(8,128)(2,1)}, f32[512,768]{1,0:T(8,128)}, bf16[512,7...) custom-call(bf16[512,768]{1,0:T(8,128)(2,1)} %bitcast.56, ...), custom_call_target="tpu_custom_call" | custom-call | flops 4831838208 | bytes 23592960 | tf_op jit(solution)/shard_map/text_forward/pallas_call | solution.py:446
  143.6 5.1 %all-to-all-start.1 = ((f32[32,8,128]{2,1,0:T(8,128)}), f32[32,8,128]{2,1,0:T(8,128)S(1)}, u32[]{:S(2)}, u32[]{:S(2)}) async-start(f32[32,8,128]{2,1,0:T(8,128)} %get-tuple-element.85), calls=%async_computation.1 | async-start | bytes 262144 | tf_op jit(solution)/shard_map/all_to_all | solution.py:1141
  150.1 0.7 pad_add_fusion.where
  150.7 3.5 %relative_rows.1 = (bf16[768,512]{1,0:T(8,128)(2,1)}, bf16[768,512]{1,0:T(8,128)(2,1)}, bf16[768,512]{1,0:T(8,128)(2,1)}) custom-call(s32[4]{0:T(128)} %pad_add_fusion.where, bf16[512,768]{1,0:T(8,128)(2,1)} %get-tuple-element.89.h1_i, bf16[512,768]{1,0:T(8,128)(2,1)} %get-tuple-element.90.h2_i, bf16[512,768]{1,0:T(8,128)(2,1)} %get-tuple-element.91.att_i), custom_call_target="tpu_custom_call" | custom-call | bytes 4718592 | tf_op jit(solution)/shard_map/relative_rows/pallas_call | solution.py:515
  154.3 2.7 all-to-all-done.1.row_all
  157.6 17.7 %back_one.1 = (bf16[32,32,576]{2,1,0:T(8,128)(2,1)}, bf16[2,2,4,48,768]{4,3,2,1,0:T(8,128)(2,1)}, bf16[2,2,4,48,768]{4,3,2,1,0:T(8,128)(2,1)}, bf16[2,2,4,48,768...) custom-call(s32[4]{0:T(128)} %pad_add_fusion.where, ...), custom_call_target="tpu_custom_call" | custom-call | flops 5435817984 | bytes 37748736 | tf_op jit(solution)/shard_map/back_one/pallas_call | solution.py:677
  175.4 3.6 %all-to-all-start.2 = ((bf16[32,32,576]{2,1,0:T(8,128)(2,1)}), bf16[32,32,576]{2,1,0:T(8,128)(2,1)}, u32[]{:S(2)}, u32[]{:S(2)}) async-start(bf16[32,32,576]{2,1,0:T(8,128)(2,1)} %get-tuple-element.130), calls=%async_computation.2 | async-start | bytes 2621440 | tf_op jit(solution)/shard_map/all_to_all | solution.py:1151
  179.6 12.7 %back_two.1 = (bf16[512,2304]{1,0:T(8,128)(2,1)}, bf16[2,2,4,48,768]{4,3,2,1,0:T(8,128)(2,1)}, bf16[2,2,4,48,768]{4,3,2,1,0:T(8,128)(2,1)}, bf16[2,2,4,48,768]{4...) custom-call(s32[4]{0:T(128)} %pad_add_fusion.where, ...), custom_call_target="tpu_custom_call" | custom-call | flops 3422552064 | bytes 7864320 | tf_op jit(solution)/shard_map/back_two/pallas_call | solution.py:799
  192.9 1.3 copy-done.1
  194.2 2.8 %fold.4 = (bf16[8,48,768]{2,1,0:T(8,128)(2,1)S(1)}, bf16[8,48,768]{2,1,0:T(8,128)(2,1)}, bf16[8,48,768]{2,1,0:T(8,128)(2,1)S(1)}, bf16[8,48,768]{2,1,0:T(8,128)(2,1)}) custom-call(bf16[2,8,48,768]{3,2,1,0:T(8,128)(2,1)S(1)} %bitcast.42, bf16[2,8,48,768]{3,2,1,0:T(8,128)(2,1)} %bitcast.17.a_new, bf16[2,8,48,768]{3,2,1,0:T(8,128)(2,1)S(1)} %bitcast.43, ...), custom_call_target="tpu_custom_call" | custom-call | flops 1179648 | bytes 7077888 | tf_op jit(solution)/shard_map/fold/pallas_call | solution.py:918
  197.0 1.4 collective-permute-start.9
  198.4 1.5 collective-permute-start.10
  199.9 1.7 fold.5
  202.2 0.7 collective-permute-start.12
  202.8 9.0 %back_third.1 = (f32[512,768]{1,0:T(8,128)}, f32[32,8,128]{2,1,0:T(8,128)}) custom-call(f32[512,768]{1,0:T(8,128)} %get-tuple-element.95.dr1_i, bf16[512,2304]{1,0:T(8,128)(2,1)} %get-tuple-element.123.dqkv_i, bf16[512,768]{1,0:T(8,128)(2,1)} %bitcast.57, bf16[32,576,384]{2,1,0:T(8,128)(2,1)} %bitcast.54, bf16[8,768]{1,0:T(8,128)(2,1)} %reshape.222.vec, ...), custom_call_target="tpu_custom_call" | custom-call | flops 1811939328 | bytes 8257536 | tf_op jit(solution)/shard_map/back_third/pallas_call | solution.py:878
  211.8 4.8 %collective-permute-done.9.a_new = bf16[2,4,48,768]{3,2,1,0:T(8,128)(2,1)} collective-permute-done((bf16[2,4,48,768]{3,2,1,0:T(8,128)(2,1)}, bf16[2,4,48,768]{3,2,1,0:T(8,128)(2,1)}, u32[]{:S(2)}, u32[]{:S(2)}) %collective-permute-start.9) | collective-permute-done | bytes 589856 | tf_op jit(solution)/shard_map/ppermute | solution.py:963
  217.1 1.1 copy-done.5
  218.2 2.0 fold.6
  220.2 1.5 collective-permute-start.13
  221.7 0.7 collective-permute-start.14
  222.4 2.4 fusion
  224.8 4.4 %collective-permute-done.11.a_new = bf16[2,4,48,768]{3,2,1,0:T(8,128)(2,1)} collective-permute-done((bf16[2,4,48,768]{3,2,1,0:T(8,128)(2,1)}, bf16[2,4,48,768]{3,2,1,0:T(8,128)(2,1)}, u32[]{:S(2)}, u32[]{:S(2)}) %collective-permute-start.11) | collective-permute-done | bytes 589856 | tf_op jit(solution)/shard_map/ppermute | solution.py:963
  229.8 2.1 fold.7
  231.9 1.5 collective-permute-start.15
  233.4 0.7 collective-permute-start.16
  234.1 1.9 collective-permute-done.13.a_new
  236.1 2.0 collective-permute-start.20
  238.1 2.9 %all-to-all-start.3 = ((f32[32,8,128]{2,1,0:T(8,128)}), f32[32,8,128]{2,1,0:T(8,128)S(1)}, u32[]{:S(2)}, u32[]{:S(2)}) async-start(f32[32,8,128]{2,1,0:T(8,128)} %get-tuple-element.144), calls=%async_computation.3 | async-start | bytes 262144 | tf_op jit(solution)/shard_map/all_to_all | solution.py:1178
  241.0 2.7 collective-permute-start.21
  243.8 1.5 collective-permute-start.22
  245.5 2.9 %collective-permute-start.18 = (bf16[48,1536]{1,0:T(8,128)(2,1)S(1)}, bf16[48,1536]{1,0:T(8,128)(2,1)S(1)}, u32[]{:S(2)}, u32[]{:S(2)}) collective-permute-start(bf16[48,1536]{1,0:T(8,128)(2,1)S(1)} %get-tuple-element.156), channel_id=1, source_target_pairs={{0,8},{1,9},{2,10},{3,11},{4,12},{5,13},{6,14},{7,15},{8,0},{9,1},... | collective-permute-start | bytes 442376 | tf_op jit(solution)/shard_map/ppermute | solution.py:963
  248.4 1.5 collective-permute-start.19
  249.8 1.2 slice.29
  251.0 12.9 %collective-permute-done.21.two = bf16[48,1536]{1,0:T(8,128)(2,1)S(1)} collective-permute-done((bf16[48,1536]{1,0:T(8,128)(2,1)S(1)}, bf16[48,1536]{1,0:T(8,128)(2,1)S(1)}, u32[]{:S(2)}, u32[]{:S(2)}) %collective-permute-start.21) | collective-permute-done | bytes 147488 | tf_op jit(solution)/shard_map/ppermute | solution.py:963
  263.9 0.8 total.3
  267.4 2.8 %collective-permute-done.18.two = bf16[48,1536]{1,0:T(8,128)(2,1)S(1)} collective-permute-done((bf16[48,1536]{1,0:T(8,128)(2,1)S(1)}, bf16[48,1536]{1,0:T(8,128)(2,1)S(1)}, u32[]{:S(2)}, u32[]{:S(2)}) %collective-permute-start.18) | collective-permute-done | bytes 147488 | tf_op jit(solution)/shard_map/ppermute | solution.py:963
  270.2 0.8 total.2
  (74 shorter events, 9.0 us)
Async XLA Ops:
  7.2 113.6 %all-gather.3.cloned.1.call-start = ((), (), s32[]{:S(2)}) async-start(), calls=%async_computation.4 | async-start | bytes 14598144 | tf_op jit(solution)/shard_map/all_gather | solution.py:1043
  11.2 105.8 %all-to-all-start = ((bf16[16,8,72]{2,1,0:T(8,128)(2,1)}), bf16[16,8,72]{2,1,0:T(8,128)(2,1)S(1)}, u32[]{:S(2)}, u32[]{:S(2)}) async-start(bf16[16,8,72]{2,1,0:T(8,128)(2,1)} %broadcast_in_dim.42), calls=%async_computation | async-start | bytes 65536 | tf_op jit(solution)/shard_map/all_to_all | solution.py:1100
  19.9 52.5 %copy-start.10 = (s32[32]{0:T(128)S(1)}, s32[32]{0:T(128)}, u32[]{:S(2)}) copy-start(s32[32]{0:T(128)} %param.30) | copy-start | bytes 388
  19.9 52.7 %copy-start.7 = (s32[1024]{0:T(1024)S(1)}, s32[1024]{0:T(1024)}, u32[]{:S(2)}) copy-start(s32[1024]{0:T(1024)} %param.31) | copy-start | bytes 12292
  70.4 8.9 %collective-permute-start = (bf16[32,768]{1,0:T(8,128)(2,1)}, bf16[32,768]{1,0:T(8,128)(2,1)S(1)}, u32[]{:S(2)}, u32[]{:S(2)}) collective-permute-start(bf16[32,768]{1,0:T(8,128)(2,1)} %image_forward.1), channel_id=1, source_target_pairs={{0,4},{1,5},{2,6},{3,7},{4,0},{5,1},{6,2},{7,3},{8,12},{9,13},{10,... | collective-permute-start | bytes 147464 | tf_op jit(solution)/shard_map/ppermute | solution.py:963
  80.1 13.9 %collective-permute-start.1 = (bf16[64,768]{1,0:T(8,128)(2,1)S(1)}, bf16[64,768]{1,0:T(8,128)(2,1)S(1)}, u32[]{:S(2)}, u32[]{:S(2)}) collective-permute-start(bf16[64,768]{1,0:T(8,128)(2,1)S(1)} %pad_maximum_fusion.2), channel_id=1, source_target_pairs={{0,8},{1,9},{2,10},{3,11},{4,12},{5,13},{6,14},{7,15},{8,0},{9,1},... | collective-permute-start | bytes 294920 | tf_op jit(solution)/shard_map/ppermute | solution.py:963
  94.9 7.4 %collective-permute-start.2 = (bf16[128,768]{1,0:T(8,128)(2,1)S(1)}, bf16[128,768]{1,0:T(8,128)(2,1)S(1)}, u32[]{:S(2)}, u32[]{:S(2)}) collective-permute-start(bf16[128,768]{1,0:T(8,128)(2,1)S(1)} %pad_maximum_fusion.1), channel_id=1, source_target_pairs={{0,16},{1,17},{2,18},{3,19},{4,20},{5,21},{6,22},{7,23},{8,24},{9,... | collective-permute-start | bytes 589832 | tf_op jit(solution)/shard_map/ppermute | solution.py:963
  96.4 20.7 %copy-start.8 = (f32[1024]{0:T(1024)}, f32[1024]{0:T(1024)S(1)}, u32[]{:S(2)}) copy-start(f32[1024]{0:T(1024)S(1)} %broadcast_maximum_fusion) | copy-start | bytes 12292
  103.2 10.7 %collective-permute-start.3 = (bf16[256,768]{1,0:T(8,128)(2,1)S(1)}, bf16[256,768]{1,0:T(8,128)(2,1)S(1)}, u32[]{:S(2)}, u32[]{:S(2)}) collective-permute-start(bf16[256,768]{1,0:T(8,128)(2,1)S(1)} %pad_maximum_fusion), channel_id=1, source_target_pairs={{0,2},{1,3},{2,0},{3,1},{4,6},{5,7},{6,4},{7,5},{8,10},{9,11},{10,... | collective-permute-start | bytes 1179656 | tf_op jit(solution)/shard_map/ppermute | solution.py:963
  114.6 3.9 %collective-permute-start.4 = (bf16[512,768]{1,0:T(8,128)(2,1)}, bf16[512,768]{1,0:T(8,128)(2,1)S(1)}, u32[]{:S(2)}, u32[]{:S(2)}) collective-permute-start(bf16[512,768]{1,0:T(8,128)(2,1)} %get-tuple-element.160), channel_id=1, source_target_pairs={{0,1},{1,0},{2,3},{3,2},{4,5},{5,4},{6,7},{7,6},{8,9},{9,8},{10,11... | collective-permute-start | bytes 2359304 | tf_op jit(solution)/shard_map/ppermute | solution.py:963
  143.6 13.3 %all-to-all-start.1 = ((f32[32,8,128]{2,1,0:T(8,128)}), f32[32,8,128]{2,1,0:T(8,128)S(1)}, u32[]{:S(2)}, u32[]{:S(2)}) async-start(f32[32,8,128]{2,1,0:T(8,128)} %get-tuple-element.85), calls=%async_computation.1 | async-start | bytes 262144 | tf_op jit(solution)/shard_map/all_to_all | solution.py:1141
  157.0 0.7 copy-start.6
  175.4 47.0 %all-to-all-start.2 = ((bf16[32,32,576]{2,1,0:T(8,128)(2,1)}), bf16[32,32,576]{2,1,0:T(8,128)(2,1)}, u32[]{:S(2)}, u32[]{:S(2)}) async-start(bf16[32,32,576]{2,1,0:T(8,128)(2,1)} %get-tuple-element.130), calls=%async_computation.2 | async-start | bytes 2621440 | tf_op jit(solution)/shard_map/all_to_all | solution.py:1151
  179.0 13.9 %collective-permute-start.5 = (bf16[2,2,4,48,768]{4,3,2,1,0:T(8,128)(2,1)}, bf16[2,2,4,48,768]{4,3,2,1,0:T(8,128)(2,1)}, u32[]{:S(2)}, u32[]{:S(2)}) collective-permute-start(bf16[2,2,4,48,768]{4,3,2,1,0:T(8,128)(2,1)} %get-tuple-element.109), channel_id=1, source_target_pairs={{0,1},{1,0},{2,3},{3,2},{4,5},{5,4},{6,7},{7,6},{8,9},{9,8},{10,11... | collective-permute-start | bytes 3538952 | tf_op jit(solution)/shard_map/ppermute | solution.py:963
  179.1 13.8 %collective-permute-start.6 = (bf16[2,2,4,48,768]{4,3,2,1,0:T(8,128)(2,1)}, bf16[2,2,4,48,768]{4,3,2,1,0:T(8,128)(2,1)}, u32[]{:S(2)}, u32[]{:S(2)}) collective-permute-start(bf16[2,2,4,48,768]{4,3,2,1,0:T(8,128)(2,1)} %get-tuple-element.111), channel_id=1, source_target_pairs={{0,1},{1,0},{2,3},{3,2},{4,5},{5,4},{6,7},{7,6},{8,9},{9,8},{10,11... | collective-permute-start | bytes 3538952 | tf_op jit(solution)/shard_map/ppermute | solution.py:963
  179.6 13.3 %copy-start = (bf16[2,2,4,48,768]{4,3,2,1,0:T(8,128)(2,1)S(1)}, bf16[2,2,4,48,768]{4,3,2,1,0:T(8,128)(2,1)}, u32[]{:S(2)}) copy-start(bf16[2,2,4,48,768]{4,3,2,1,0:T(8,128)(2,1)} %get-tuple-element.108) | copy-start | bytes 3538948
  192.3 7.6 %collective-permute-start.7 = (bf16[2,2,4,48,768]{4,3,2,1,0:T(8,128)(2,1)}, bf16[2,2,4,48,768]{4,3,2,1,0:T(8,128)(2,1)S(1)}, u32[]{:S(2)}, u32[]{:S(2)}) collective-permute-start(bf16[2,2,4,48,768]{4,3,2,1,0:T(8,128)(2,1)} %get-tuple-element.105), channel_id=1, source_target_pairs={{0,1},{1,0},{2,3},{3,2},{4,5},{5,4},{6,7},{7,6},{8,9},{9,8},{10,11... | collective-permute-start | bytes 3538952 | tf_op jit(solution)/shard_map/ppermute | solution.py:963
  192.5 7.4 %collective-permute-start.8 = (bf16[2,2,4,48,768]{4,3,2,1,0:T(8,128)(2,1)}, bf16[2,2,4,48,768]{4,3,2,1,0:T(8,128)(2,1)S(1)}, u32[]{:S(2)}, u32[]{:S(2)}) collective-permute-start(bf16[2,2,4,48,768]{4,3,2,1,0:T(8,128)(2,1)} %get-tuple-element.107), channel_id=1, source_target_pairs={{0,1},{1,0},{2,3},{3,2},{4,5},{5,4},{6,7},{7,6},{8,9},{9,8},{10,11... | collective-permute-start | bytes 3538952 | tf_op jit(solution)/shard_map/ppermute | solution.py:963
  192.9 1.3 copy-start.1
  194.2 5.7 %copy-start.2 = (bf16[2,2,4,48,768]{4,3,2,1,0:T(8,128)(2,1)S(1)}, bf16[2,2,4,48,768]{4,3,2,1,0:T(8,128)(2,1)}, u32[]{:S(2)}) copy-start(bf16[2,2,4,48,768]{4,3,2,1,0:T(8,128)(2,1)} %get-tuple-element.117) | copy-start | bytes 3538948
  194.2 5.7 %copy-start.3 = (bf16[2,2,4,48,768]{4,3,2,1,0:T(8,128)(2,1)S(1)}, bf16[2,2,4,48,768]{4,3,2,1,0:T(8,128)(2,1)}, u32[]{:S(2)}) copy-start(bf16[2,2,4,48,768]{4,3,2,1,0:T(8,128)(2,1)} %get-tuple-element.118) | copy-start | bytes 3538948
  197.0 4.6 %copy-start.4 = (bf16[8,48,768]{2,1,0:T(8,128)(2,1)}, bf16[8,48,768]{2,1,0:T(8,128)(2,1)S(1)}, u32[]{:S(2)}) copy-start(bf16[8,48,768]{2,1,0:T(8,128)(2,1)S(1)} %get-tuple-element.114) | copy-start | bytes 1769476
  197.0 19.6 %collective-permute-start.9 = (bf16[2,4,48,768]{3,2,1,0:T(8,128)(2,1)}, bf16[2,4,48,768]{3,2,1,0:T(8,128)(2,1)}, u32[]{:S(2)}, u32[]{:S(2)}) collective-permute-start(bf16[2,4,48,768]{3,2,1,0:T(8,128)(2,1)} %bitcast.21), channel_id=1, source_target_pairs={{0,16},{1,17},{2,18},{3,19},{4,20},{5,21},{6,22},{7,23},{8,24},{9,... | collective-permute-start | bytes 1769480 | tf_op jit(solution)/shard_map/ppermute | solution.py:963
  198.4 18.7 %collective-permute-start.10 = (bf16[2,4,48,768]{3,2,1,0:T(8,128)(2,1)}, bf16[2,4,48,768]{3,2,1,0:T(8,128)(2,1)}, u32[]{:S(2)}, u32[]{:S(2)}) collective-permute-start(bf16[2,4,48,768]{3,2,1,0:T(8,128)(2,1)} %bitcast.23), channel_id=1, source_target_pairs={{0,2},{1,3},{2,0},{3,1},{4,6},{5,7},{6,4},{7,5},{8,10},{9,11},{10,... | collective-permute-start | bytes 1769480 | tf_op jit(solution)/shard_map/ppermute | solution.py:963
  201.6 27.6 %collective-permute-start.11 = (bf16[2,4,48,768]{3,2,1,0:T(8,128)(2,1)}, bf16[2,4,48,768]{3,2,1,0:T(8,128)(2,1)}, u32[]{:S(2)}, u32[]{:S(2)}) collective-permute-start(bf16[2,4,48,768]{3,2,1,0:T(8,128)(2,1)} %bitcast.29), channel_id=1, source_target_pairs={{0,16},{1,17},{2,18},{3,19},{4,20},{5,21},{6,22},{7,23},{8,24},{9,... | collective-permute-start | bytes 1769480 | tf_op jit(solution)/shard_map/ppermute | solution.py:963
  202.2 27.6 %collective-permute-start.12 = (bf16[2,4,48,768]{3,2,1,0:T(8,128)(2,1)}, bf16[2,4,48,768]{3,2,1,0:T(8,128)(2,1)}, u32[]{:S(2)}, u32[]{:S(2)}) collective-permute-start(bf16[2,4,48,768]{3,2,1,0:T(8,128)(2,1)} %bitcast.31), channel_id=1, source_target_pairs={{0,2},{1,3},{2,0},{3,1},{4,6},{5,7},{6,4},{7,5},{8,10},{9,11},{10,... | collective-permute-start | bytes 1769480 | tf_op jit(solution)/shard_map/ppermute | solution.py:963
  217.1 1.1 copy-start.5
  220.2 15.8 %collective-permute-start.13 = (bf16[4,48,768]{2,1,0:T(8,128)(2,1)}, bf16[4,48,768]{2,1,0:T(8,128)(2,1)S(1)}, u32[]{:S(2)}, u32[]{:S(2)}) collective-permute-start(bf16[4,48,768]{2,1,0:T(8,128)(2,1)} %get-tuple-element.135), channel_id=1, source_target_pairs={{0,2},{1,3},{2,0},{3,1},{4,6},{5,7},{6,4},{7,5},{8,10},{9,11},{10,... | collective-permute-start | bytes 884744 | tf_op jit(solution)/shard_map/ppermute | solution.py:963
  221.7 14.3 %collective-permute-start.14 = (bf16[4,48,768]{2,1,0:T(8,128)(2,1)S(1)}, bf16[4,48,768]{2,1,0:T(8,128)(2,1)S(1)}, u32[]{:S(2)}, u32[]{:S(2)}) collective-permute-start(bf16[4,48,768]{2,1,0:T(8,128)(2,1)S(1)} %get-tuple-element.137), channel_id=1, source_target_pairs={{0,16},{1,17},{2,18},{3,19},{4,20},{5,21},{6,22},{7,23},{8,24},{9,... | collective-permute-start | bytes 884744 | tf_op jit(solution)/shard_map/ppermute | solution.py:963
  231.9 13.3 %collective-permute-start.15 = (bf16[4,48,768]{2,1,0:T(8,128)(2,1)}, bf16[4,48,768]{2,1,0:T(8,128)(2,1)S(1)}, u32[]{:S(2)}, u32[]{:S(2)}) collective-permute-start(bf16[4,48,768]{2,1,0:T(8,128)(2,1)} %get-tuple-element.141), channel_id=1, source_target_pairs={{0,2},{1,3},{2,0},{3,1},{4,6},{5,7},{6,4},{7,5},{8,10},{9,11},{10,... | collective-permute-start | bytes 884744 | tf_op jit(solution)/shard_map/ppermute | solution.py:963
  233.4 11.9 %collective-permute-start.16 = (bf16[4,48,768]{2,1,0:T(8,128)(2,1)}, bf16[4,48,768]{2,1,0:T(8,128)(2,1)S(1)}, u32[]{:S(2)}, u32[]{:S(2)}) collective-permute-start(bf16[4,48,768]{2,1,0:T(8,128)(2,1)} %get-tuple-element.143), channel_id=1, source_target_pairs={{0,16},{1,17},{2,18},{3,19},{4,20},{5,21},{6,22},{7,23},{8,24},{9,... | collective-permute-start | bytes 884744 | tf_op jit(solution)/shard_map/ppermute | solution.py:963
  236.1 12.3 %collective-permute-start.20 = (bf16[48,1536]{1,0:T(8,128)(2,1)S(1)}, bf16[48,1536]{1,0:T(8,128)(2,1)S(1)}, u32[]{:S(2)}, u32[]{:S(2)}) collective-permute-start(bf16[48,1536]{1,0:T(8,128)(2,1)S(1)} %get-tuple-element.149), channel_id=1, source_target_pairs={{0,4},{1,5},{2,6},{3,7},{4,0},{5,1},{6,2},{7,3},{8,12},{9,13},{10,... | collective-permute-start | bytes 442376 | tf_op jit(solution)/shard_map/ppermute | solution.py:963
  238.1 26.6 %all-to-all-start.3 = ((f32[32,8,128]{2,1,0:T(8,128)}), f32[32,8,128]{2,1,0:T(8,128)S(1)}, u32[]{:S(2)}, u32[]{:S(2)}) async-start(f32[32,8,128]{2,1,0:T(8,128)} %get-tuple-element.144), calls=%async_computation.3 | async-start | bytes 262144 | tf_op jit(solution)/shard_map/all_to_all | solution.py:1178
  241.0 22.8 %collective-permute-start.21 = (bf16[48,1536]{1,0:T(8,128)(2,1)S(1)}, bf16[48,1536]{1,0:T(8,128)(2,1)S(1)}, u32[]{:S(2)}, u32[]{:S(2)}) collective-permute-start(bf16[48,1536]{1,0:T(8,128)(2,1)S(1)} %get-tuple-element.150), channel_id=1, source_target_pairs={{0,8},{1,9},{2,10},{3,11},{4,12},{5,13},{6,14},{7,15},{8,0},{9,1},... | collective-permute-start | bytes 442376 | tf_op jit(solution)/shard_map/ppermute | solution.py:963
  243.8 20.1 %collective-permute-start.22 = (bf16[48,1536]{1,0:T(8,128)(2,1)S(1)}, bf16[48,1536]{1,0:T(8,128)(2,1)S(1)}, u32[]{:S(2)}, u32[]{:S(2)}) collective-permute-start(bf16[48,1536]{1,0:T(8,128)(2,1)S(1)} %get-tuple-element.151), channel_id=1, source_target_pairs={{0,12},{1,13},{2,14},{3,15},{4,8},{5,9},{6,10},{7,11},{8,4},{9,5},... | collective-permute-start | bytes 442376 | tf_op jit(solution)/shard_map/ppermute | solution.py:963
  245.4 22.0 %collective-permute-start.17 = (bf16[48,1536]{1,0:T(8,128)(2,1)S(1)}, bf16[48,1536]{1,0:T(8,128)(2,1)S(1)}, u32[]{:S(2)}, u32[]{:S(2)}) collective-permute-start(bf16[48,1536]{1,0:T(8,128)(2,1)S(1)} %get-tuple-element.155), channel_id=1, source_target_pairs={{0,4},{1,5},{2,6},{3,7},{4,0},{5,1},{6,2},{7,3},{8,12},{9,13},{10,... | collective-permute-start | bytes 442376 | tf_op jit(solution)/shard_map/ppermute | solution.py:963
  245.5 24.7 %collective-permute-start.18 = (bf16[48,1536]{1,0:T(8,128)(2,1)S(1)}, bf16[48,1536]{1,0:T(8,128)(2,1)S(1)}, u32[]{:S(2)}, u32[]{:S(2)}) collective-permute-start(bf16[48,1536]{1,0:T(8,128)(2,1)S(1)} %get-tuple-element.156), channel_id=1, source_target_pairs={{0,8},{1,9},{2,10},{3,11},{4,12},{5,13},{6,14},{7,15},{8,0},{9,1},... | collective-permute-start | bytes 442376 | tf_op jit(solution)/shard_map/ppermute | solution.py:963
  248.4 21.8 %collective-permute-start.19 = (bf16[48,1536]{1,0:T(8,128)(2,1)S(1)}, bf16[48,1536]{1,0:T(8,128)(2,1)S(1)}, u32[]{:S(2)}, u32[]{:S(2)}) collective-permute-start(bf16[48,1536]{1,0:T(8,128)(2,1)S(1)} %get-tuple-element.157), channel_id=1, source_target_pairs={{0,12},{1,13},{2,14},{3,15},{4,8},{5,9},{6,10},{7,11},{8,4},{9,5},... | collective-permute-start | bytes 442376 | tf_op jit(solution)/shard_map/ppermute | solution.py:963
  264.7 6.3 %copy-start.9 = (f32[8,128]{1,0:T(8,128)}, f32[8,128]{1,0:T(8,128)S(1)}, u32[]{:S(2)}) copy-start(f32[8,128]{1,0:T(8,128)S(1)} %reduce_sum.29) | copy-start | bytes 12292
Sparse Core Ops, SparseCore 0:
  10.9 108.3 all-gather.2

commit v2 on v1

--- a/solution.py
+++ b/solution.py
@@ -930,12 +930,13 @@
     return [o.reshape(shape[1:]) for o in outs]
 
 
-def join_kernel(a_own, a_new, b_own, b_new, stay, one, two, three):
+def join_kernel(a_own, a_new, b_own, b_new, keep, send):
     half = a_own.shape[-1]
     for at, own, new in ((0, a_own, a_new), (half, b_own, b_new)):
         total = own[...].astype(F32) + new[...].astype(F32)
-        for k, dst in enumerate((stay, one, two, three)):
-            dst[:, at : at + half] = total[k].astype(dst.dtype)
+        for k in range(2):
+            keep[k, :, at : at + half] = total[2 * k]
+            send[k, :, at : at + half] = total[2 * k + 1].astype(BF)
 
 
 def join(a_own, a_new, b_own, b_new):
@@ -945,8 +946,8 @@
         join_kernel,
         name="join",
         in_specs=[WHOLE] * 4,
-        out_specs=[WHOLE] * 4,
-        out_shape=[shape((rows, 2 * cols), F32)] + [shape((rows, 2 * cols), BF)] * 3,
+        out_specs=[WHOLE] * 2,
+        out_shape=[shape((2, rows, 2 * cols), F32), shape((2, rows, 2 * cols), BF)],
         compiler_params=params(6),
         cost_estimate=pl.CostEstimate(
             flops=16 * rows * cols, bytes_accessed=40 * rows * cols, transcendentals=0
@@ -954,6 +955,27 @@
     )(a_own, a_new, b_own, b_new)
 
 
+def turn_kernel(keep, new, stay, send):
+    stay[...] = keep[0] + new[0].astype(F32)
+    send[...] = (keep[1] + new[1].astype(F32)).astype(BF)
+
+
+def turn(keep, new):
+    blocks, rows, cols = keep.shape
+    shape = jax.ShapeDtypeStruct
+    return pl.pallas_call(
+        turn_kernel,
+        name="turn",
+        in_specs=[WHOLE] * 2,
+        out_specs=[WHOLE] * 2,
+        out_shape=[shape((rows, cols), F32), shape((rows, cols), BF)],
+        compiler_params=params(6),
+        cost_estimate=pl.CostEstimate(
+            flops=4 * rows * cols, bytes_accessed=18 * rows * cols, transcendentals=0
+        ),
+    )(keep, new)
+
+
 def shifted(x, y, z, core):
     change = x * 16 + z * 4 + y * 2 + core
     return [(i, i ^ change) for i in range(32)]
@@ -988,24 +1010,31 @@
     return join(keep_a, new_a, keep_b, new_b)
 
 
-def total_kernel(stay, one, two, three, *outs):
-    total = stay[...] + one[...].astype(F32) + two[...].astype(F32) + three[...].astype(F32)
+def total_kernel(stay, new, *outs):
+    total = stay[...] + new[...].astype(F32)
     at = 0
     for out in outs:
         out[...] = total[:, at : at + out.shape[1]]
         at += out.shape[1]
 
 
-def third_step(parts, splits):
-    stay, one, two, three = parts
+def third_step(parts, *wait):
+    keep, send = parts
+    new = hop(send, z=1)
+    (keep,) = after((keep,), *wait)
+    return turn(keep, new)
+
+
+def last_step(parts, splits):
+    stay, send = parts
     return pl.pallas_call(
         total_kernel,
         name="total",
-        in_specs=[WHOLE] * 4,
+        in_specs=[WHOLE] * 2,
         out_specs=[WHOLE] * len(splits),
         out_shape=[jax.ShapeDtypeStruct((stay.shape[0], n), F32) for n in splits],
         compiler_params=params(4),
-    )(stay, hop(one, z=1), hop(two, z=2), hop(three, z=3))
+    )(stay, hop(send, z=2))
 
 
 def natural_grad(keep_a, send_a, keep_b, send_b):
@@ -1164,8 +1193,10 @@
         up_parts = second_step(up_parts, *att_parts)
         (share,) = after((share,), *att_parts)
         att_parts = second_step(att_parts, *up_parts)
-        (grad_up,) = third_step(up_parts, (hidden // dp,))
-        grad_qkv, grad_out = third_step(att_parts, (3 * width // dp, width // dp))
+        up_parts = third_step(up_parts, *att_parts)
+        att_parts = third_step(att_parts, *up_parts)
+        (grad_up,) = last_step(up_parts, (hidden // dp,))
+        grad_qkv, grad_out = last_step(att_parts, (3 * width // dp, width // dp))
     else:
         dx, share = back_third(
             dr1, dqkv, tokens, packed, vec, sums, bias_sums, down_bias, bias_up, loss_part, (dp, fsdp)

time: 280 us -> 276 us (0.986)
    ppermute x23 -> x21, waiting for transfers between devices: 58.2 us -> 55.4 us  [hop(): return lax.ppermute(array, AXES, shifted(x, y, z, core))]
    ppermute x23 -> x21, starting transfers between devices: 26.8 us -> 25.8 us  [hop(): return lax.ppermute(array, AXES, shifted(x, y, z, core))]
  transfers between devices with their start and end apart: 28 -> 26, of which waited for: 12 -> 14; matrix products, arithmetic and copies ran while one was open for 8% -> 8% of each run, Pallas kernels for 31% -> 31%
where the time goes in v2:
time: 276 us; the launch traced here: 275 us
  Pallas kernels  128 us (46%)
  waiting for transfers between devices  58.1 us (21%)
  starting transfers between devices  45.4 us (16%)
  between operations  17.4 us (6%)
  local copies, waits for them, and re-layouts  17 us (6%)
  other arithmetic  6.66 us (2%)
    ppermute x21, waiting for transfers between devices, hop(): return lax.ppermute(array, AXES, shifted(x, y, z, core))  55.4 us
    pallas_call x1, Pallas kernels, image_forward(): pl.pallas_call(image_kernel, name='image_forward', grid=(pairs // group,)...  50.5 us
    ppermute x21, starting transfers between devices, hop(): return lax.ppermute(array, AXES, shifted(x, y, z, core))  25.8 us
    pallas_call x1, Pallas kernels, text_forward(): pl.pallas_call(functools.partial(text_forward_kernel, length), name='text...  22.9 us
    pallas_call x1, Pallas kernels, back_one(): pl.pallas_call(functools.partial(back_one_kernel, length, shard), name='b...  17.7 us
    pallas_call x1, Pallas kernels, back_two(): pl.pallas_call(functools.partial(back_two_kernel, length), name='back_two...  12.7 us
    pallas_call x1, Pallas kernels, back_third(): pl.pallas_call(functools.partial(back_third_kernel, shard[1]), name='back...  9 us
    pallas_call x4, Pallas kernels, fold(): pl.pallas_call(fold_kernel, name='fold', grid=(steps,), in_specs=[pair] *...  7.57 us
  transfers between devices with their start and end apart: 26, of which 14 were waited for; matrix products, arithmetic and copies ran while one was open for 8% of the time, Pallas kernels for 31%

profile of v2, /device:TPU:0, one launch (start us, length us, event | category | flops | bytes accessed | tf_op | source)
XLA Modules:
  0.0 274.7 jit_solution(15798842063957908489)
XLA Ops:
  7.2 1.9 pack_block.1
  9.1 0.7 reshape.221
  9.8 0.8 pad_maximum_fusion.3
  11.2 7.4 %all-to-all-start = ((bf16[16,8,72]{2,1,0:T(8,128)(2,1)}), bf16[16,8,72]{2,1,0:T(8,128)(2,1)S(1)}, u32[]{:S(2)}, u32[]{:S(2)}) async-start(bf16[16,8,72]{2,1,0:T(8,128)(2,1)} %broadcast_in_dim.42), calls=%async_computation | async-start | bytes 65536 | tf_op jit(solution)/shard_map/all_to_all | solution.py:1129
  18.6 1.3 reshape.224.ub
  19.9 50.5 %image_forward.1 = bf16[32,768]{1,0:T(8,128)(2,1)} custom-call(bf16[50,32,768]{2,1,0:T(8,128)(2,1)} %bitcast.63, bf16[768,2304]{1,0:T(8,128)(2,1)} %wq_h.1, bf16[768,768]{1,0:T(8,128)(2,1)} %wo_h.1, bf16[768,3072]{1,0:T(8,128)(2,1)} %wu_h.1, bf16[3072,768]{1,0:T(8,128)(2,1)} %wd_h.1, bf16[8,768]{1,0:T(8,128)(2,1)} %vec.1, bf16[1,3072]{1,0:T(2,128)(2,1)} %reshape.224.ub), custom_call_target="tpu_custom_call" | custom-call | flops 15099494400 | bytes 16613376 | tf_op jit(solution)/shard_map/image_forward/pallas_call | solution.py:229
  70.4 2.0 collective-permute-start
  73.1 6.2 %collective-permute-done = bf16[32,768]{1,0:T(8,128)(2,1)S(1)} collective-permute-done((bf16[32,768]{1,0:T(8,128)(2,1)}, bf16[32,768]{1,0:T(8,128)(2,1)S(1)}, u32[]{:S(2)}, u32[]{:S(2)}) %collective-permute-start) | collective-permute-done | bytes 49184 | tf_op jit(solution)/shard_map/ppermute | solution.py:985
  79.3 0.8 pad_maximum_fusion.2
  80.1 1.5 collective-permute-start.1
  81.7 1.4 constant_dynamic-update-slice_fusion.4
  83.1 11.0 %collective-permute-done.1 = bf16[64,768]{1,0:T(8,128)(2,1)S(1)} collective-permute-done((bf16[64,768]{1,0:T(8,128)(2,1)S(1)}, bf16[64,768]{1,0:T(8,128)(2,1)S(1)}, u32[]{:S(2)}, u32[]{:S(2)}) %collective-permute-start.1) | collective-permute-done | bytes 98336 | tf_op jit(solution)/shard_map/ppermute | solution.py:985
  94.1 0.8 pad_maximum_fusion.1
  94.9 1.5 collective-permute-start.2
  96.4 5.9 %collective-permute-done.2 = bf16[128,768]{1,0:T(8,128)(2,1)S(1)} collective-permute-done((bf16[128,768]{1,0:T(8,128)(2,1)S(1)}, bf16[128,768]{1,0:T(8,128)(2,1)S(1)}, u32[]{:S(2)}, u32[]{:S(2)}) %collective-permute-start.2) | collective-permute-done | bytes 196640 | tf_op jit(solution)/shard_map/ppermute | solution.py:985
  102.3 0.8 pad_maximum_fusion
  103.2 1.5 collective-permute-start.3
  105.3 0.7 constant_dynamic-update-slice_fusion.2
  106.0 0.7 constant_dynamic-update-slice_fusion.1
  106.7 7.2 %collective-permute-done.3 = bf16[256,768]{1,0:T(8,128)(2,1)S(1)} collective-permute-done((bf16[256,768]{1,0:T(8,128)(2,1)S(1)}, bf16[256,768]{1,0:T(8,128)(2,1)S(1)}, u32[]{:S(2)}, u32[]{:S(2)}) %collective-permute-start.3) | collective-permute-done | bytes 393248 | tf_op jit(solution)/shard_map/ppermute | solution.py:985
  113.8 0.8 constant_dynamic-update-slice_fusion
  114.8 0.7 reshape.246.live
  115.7 0.7 copy.36.own_group
  116.4 0.7 copy.35.own
  117.1 0.7 reshape.223.ub
  117.9 0.7 reshape.222.vec
  119.3 1.4 bitcast_select_fusion.images_i
  120.7 22.9 %text_forward.1 = (bf16[512,768]{1,0:T(8,128)(2,1)}, bf16[512,2304]{1,0:T(8,128)(2,1)}, bf16[512,768]{1,0:T(8,128)(2,1)}, f32[512,768]{1,0:T(8,128)}, bf16[512,7...) custom-call(bf16[512,768]{1,0:T(8,128)(2,1)} %bitcast.56, ...), custom_call_target="tpu_custom_call" | custom-call | flops 4831838208 | bytes 23592960 | tf_op jit(solution)/shard_map/text_forward/pallas_call | solution.py:446
  143.6 5.1 %all-to-all-start.1 = ((f32[32,8,128]{2,1,0:T(8,128)}), f32[32,8,128]{2,1,0:T(8,128)S(1)}, u32[]{:S(2)}, u32[]{:S(2)}) async-start(f32[32,8,128]{2,1,0:T(8,128)} %get-tuple-element.87), calls=%async_computation.1 | async-start | bytes 262144 | tf_op jit(solution)/shard_map/all_to_all | solution.py:1170
  150.1 0.7 pad_add_fusion.where
  150.7 3.5 %relative_rows.1 = (bf16[768,512]{1,0:T(8,128)(2,1)}, bf16[768,512]{1,0:T(8,128)(2,1)}, bf16[768,512]{1,0:T(8,128)(2,1)}) custom-call(s32[4]{0:T(128)} %pad_add_fusion.where, bf16[512,768]{1,0:T(8,128)(2,1)} %get-tuple-element.91.h1_i, bf16[512,768]{1,0:T(8,128)(2,1)} %get-tuple-element.92.h2_i, bf16[512,768]{1,0:T(8,128)(2,1)} %get-tuple-element.93.att_i), custom_call_target="tpu_custom_call" | custom-call | bytes 4718592 | tf_op jit(solution)/shard_map/relative_rows/pallas_call | solution.py:515
  154.3 2.7 all-to-all-done.1.row_all
  157.6 17.7 %back_one.1 = (bf16[32,32,576]{2,1,0:T(8,128)(2,1)}, bf16[2,2,4,48,768]{4,3,2,1,0:T(8,128)(2,1)}, bf16[2,2,4,48,768]{4,3,2,1,0:T(8,128)(2,1)}, bf16[2,2,4,48,768...) custom-call(s32[4]{0:T(128)} %pad_add_fusion.where, ...), custom_call_target="tpu_custom_call" | custom-call | flops 5435817984 | bytes 37748736 | tf_op jit(solution)/shard_map/back_one/pallas_call | solution.py:677
  175.4 3.6 %all-to-all-start.2 = ((bf16[32,32,576]{2,1,0:T(8,128)(2,1)}), bf16[32,32,576]{2,1,0:T(8,128)(2,1)}, u32[]{:S(2)}, u32[]{:S(2)}) async-start(bf16[32,32,576]{2,1,0:T(8,128)(2,1)} %get-tuple-element.132), calls=%async_computation.2 | async-start | bytes 2621440 | tf_op jit(solution)/shard_map/all_to_all | solution.py:1180
  179.6 12.7 %back_two.1 = (bf16[512,2304]{1,0:T(8,128)(2,1)}, bf16[2,2,4,48,768]{4,3,2,1,0:T(8,128)(2,1)}, bf16[2,2,4,48,768]{4,3,2,1,0:T(8,128)(2,1)}, bf16[2,2,4,48,768]{4...) custom-call(s32[4]{0:T(128)} %pad_add_fusion.where, ...), custom_call_target="tpu_custom_call" | custom-call | flops 3422552064 | bytes 7864320 | tf_op jit(solution)/shard_map/back_two/pallas_call | solution.py:799
  192.9 1.3 copy-done.1
  194.2 2.8 %fold.4 = (bf16[8,48,768]{2,1,0:T(8,128)(2,1)S(1)}, bf16[8,48,768]{2,1,0:T(8,128)(2,1)}, bf16[8,48,768]{2,1,0:T(8,128)(2,1)S(1)}, bf16[8,48,768]{2,1,0:T(8,128)(2,1)}) custom-call(bf16[2,8,48,768]{3,2,1,0:T(8,128)(2,1)S(1)} %bitcast.42, bf16[2,8,48,768]{3,2,1,0:T(8,128)(2,1)} %bitcast.17.a_new, bf16[2,8,48,768]{3,2,1,0:T(8,128)(2,1)S(1)} %bitcast.43, ...), custom_call_target="tpu_custom_call" | custom-call | flops 1179648 | bytes 7077888 | tf_op jit(solution)/shard_map/fold/pallas_call | solution.py:918
  197.0 1.4 collective-permute-start.9
  198.4 1.5 collective-permute-start.10
  199.9 1.7 fold.5
  202.8 9.0 %back_third.1 = (f32[512,768]{1,0:T(8,128)}, f32[32,8,128]{2,1,0:T(8,128)}) custom-call(f32[512,768]{1,0:T(8,128)} %get-tuple-element.97.dr1_i, bf16[512,2304]{1,0:T(8,128)(2,1)} %get-tuple-element.125.dqkv_i, bf16[512,768]{1,0:T(8,128)(2,1)} %bitcast.57, bf16[32,576,384]{2,1,0:T(8,128)(2,1)} %bitcast.54, bf16[8,768]{1,0:T(8,128)(2,1)} %reshape.222.vec, ...), custom_call_target="tpu_custom_call" | custom-call | flops 1811939328 | bytes 8257536 | tf_op jit(solution)/shard_map/back_third/pallas_call | solution.py:878
  211.8 4.8 %collective-permute-done.9.a_new = bf16[2,4,48,768]{3,2,1,0:T(8,128)(2,1)} collective-permute-done((bf16[2,4,48,768]{3,2,1,0:T(8,128)(2,1)}, bf16[2,4,48,768]{3,2,1,0:T(8,128)(2,1)}, u32[]{:S(2)}, u32[]{:S(2)}) %collective-permute-start.9) | collective-permute-done | bytes 589856 | tf_op jit(solution)/shard_map/ppermute | solution.py:985
  217.1 1.1 copy-done.5
  218.2 1.5 fold.6
  219.7 1.5 collective-permute-start.13
  221.2 0.7 collective-permute-start.14
  221.9 2.4 fusion
  224.3 4.9 %collective-permute-done.11.a_new = bf16[2,4,48,768]{3,2,1,0:T(8,128)(2,1)} collective-permute-done((bf16[2,4,48,768]{3,2,1,0:T(8,128)(2,1)}, bf16[2,4,48,768]{3,2,1,0:T(8,128)(2,1)}, u32[]{:S(2)}, u32[]{:S(2)}) %collective-permute-start.11) | collective-permute-done | bytes 589856 | tf_op jit(solution)/shard_map/ppermute | solution.py:985
  229.8 1.5 fold.7
  231.3 1.5 collective-permute-start.15
  232.8 0.7 collective-permute-start.16
  233.5 2.5 collective-permute-done.13.a_new
  236.1 2.0 collective-permute-start.17
  238.1 3.6 %collective-permute-done.15.a_new = bf16[4,48,768]{2,1,0:T(8,128)(2,1)S(1)} collective-permute-done((bf16[4,48,768]{2,1,0:T(8,128)(2,1)S(1)}, bf16[4,48,768]{2,1,0:T(8,128)(2,1)S(1)}, u32[]{:S(2)}, u32[]{:S(2)}) %collective-permute-start.15) | collective-permute-done | bytes 294944 | tf_op jit(solution)/shard_map/ppermute | solution.py:985
  241.9 1.5 collective-permute-start.18
  243.3 3.5 %all-to-all-start.3 = ((f32[32,8,128]{2,1,0:T(8,128)}), f32[32,8,128]{2,1,0:T(8,128)S(1)}, u32[]{:S(2)}, u32[]{:S(2)}) async-start(f32[32,8,128]{2,1,0:T(8,128)} %get-tuple-element.146), calls=%async_computation.3 | async-start | bytes 262144 | tf_op jit(solution)/shard_map/all_to_all | solution.py:1209
  246.9 2.7 collective-permute-start.20
  249.6 1.1 collective-permute-done.18.new
  250.8 3.4 %collective-permute-start.19 = (bf16[48,1536]{1,0:T(8,128)(2,1)S(1)}, bf16[48,1536]{1,0:T(8,128)(2,1)S(1)}, u32[]{:S(2)}, u32[]{:S(2)}) collective-permute-start(bf16[48,1536]{1,0:T(8,128)(2,1)S(1)} %get-tuple-element.161), channel_id=1, source_target_pairs={{0,8},{1,9},{2,10},{3,11},{4,12},{5,13},{6,14},{7,15},{8,0},{9,1},... | collective-permute-start | bytes 442376 | tf_op jit(solution)/shard_map/ppermute | solution.py:985
  254.2 1.2 slice.29
  258.0 5.3 %collective-permute-done.20.new = bf16[48,1536]{1,0:T(8,128)(2,1)S(1)} collective-permute-done((bf16[48,1536]{1,0:T(8,128)(2,1)S(1)}, bf16[48,1536]{1,0:T(8,128)(2,1)S(1)}, u32[]{:S(2)}, u32[]{:S(2)}) %collective-permute-start.20) | collective-permute-done | bytes 147488 | tf_op jit(solution)/shard_map/ppermute | solution.py:985
  263.4 0.7 total.3
  264.1 1.9 collective-permute-done.19.new
  266.0 0.7 total.2
  (72 shorter events, 9.6 us)
Async XLA Ops:
  7.2 113.6 %all-gather.3.cloned.1.call-start = ((), (), s32[]{:S(2)}) async-start(), calls=%async_computation.4 | async-start | bytes 14598144 | tf_op jit(solution)/shard_map/all_gather | solution.py:1072
  11.2 105.8 %all-to-all-start = ((bf16[16,8,72]{2,1,0:T(8,128)(2,1)}), bf16[16,8,72]{2,1,0:T(8,128)(2,1)S(1)}, u32[]{:S(2)}, u32[]{:S(2)}) async-start(bf16[16,8,72]{2,1,0:T(8,128)(2,1)} %broadcast_in_dim.42), calls=%async_computation | async-start | bytes 65536 | tf_op jit(solution)/shard_map/all_to_all | solution.py:1129
  19.9 52.5 %copy-start.10 = (s32[32]{0:T(128)S(1)}, s32[32]{0:T(128)}, u32[]{:S(2)}) copy-start(s32[32]{0:T(128)} %param.30) | copy-start | bytes 388
  19.9 52.7 %copy-start.7 = (s32[1024]{0:T(1024)S(1)}, s32[1024]{0:T(1024)}, u32[]{:S(2)}) copy-start(s32[1024]{0:T(1024)} %param.31) | copy-start | bytes 12292
  70.4 8.9 %collective-permute-start = (bf16[32,768]{1,0:T(8,128)(2,1)}, bf16[32,768]{1,0:T(8,128)(2,1)S(1)}, u32[]{:S(2)}, u32[]{:S(2)}) collective-permute-start(bf16[32,768]{1,0:T(8,128)(2,1)} %image_forward.1), channel_id=1, source_target_pairs={{0,4},{1,5},{2,6},{3,7},{4,0},{5,1},{6,2},{7,3},{8,12},{9,13},{10,... | collective-permute-start | bytes 147464 | tf_op jit(solution)/shard_map/ppermute | solution.py:985
  80.1 13.9 %collective-permute-start.1 = (bf16[64,768]{1,0:T(8,128)(2,1)S(1)}, bf16[64,768]{1,0:T(8,128)(2,1)S(1)}, u32[]{:S(2)}, u32[]{:S(2)}) collective-permute-start(bf16[64,768]{1,0:T(8,128)(2,1)S(1)} %pad_maximum_fusion.2), channel_id=1, source_target_pairs={{0,8},{1,9},{2,10},{3,11},{4,12},{5,13},{6,14},{7,15},{8,0},{9,1},... | collective-permute-start | bytes 294920 | tf_op jit(solution)/shard_map/ppermute | solution.py:985
  94.9 7.4 %collective-permute-start.2 = (bf16[128,768]{1,0:T(8,128)(2,1)S(1)}, bf16[128,768]{1,0:T(8,128)(2,1)S(1)}, u32[]{:S(2)}, u32[]{:S(2)}) collective-permute-start(bf16[128,768]{1,0:T(8,128)(2,1)S(1)} %pad_maximum_fusion.1), channel_id=1, source_target_pairs={{0,16},{1,17},{2,18},{3,19},{4,20},{5,21},{6,22},{7,23},{8,24},{9,... | collective-permute-start | bytes 589832 | tf_op jit(solution)/shard_map/ppermute | solution.py:985
  96.4 20.7 %copy-start.8 = (f32[1024]{0:T(1024)}, f32[1024]{0:T(1024)S(1)}, u32[]{:S(2)}) copy-start(f32[1024]{0:T(1024)S(1)} %broadcast_maximum_fusion) | copy-start | bytes 12292
  103.2 10.7 %collective-permute-start.3 = (bf16[256,768]{1,0:T(8,128)(2,1)S(1)}, bf16[256,768]{1,0:T(8,128)(2,1)S(1)}, u32[]{:S(2)}, u32[]{:S(2)}) collective-permute-start(bf16[256,768]{1,0:T(8,128)(2,1)S(1)} %pad_maximum_fusion), channel_id=1, source_target_pairs={{0,2},{1,3},{2,0},{3,1},{4,6},{5,7},{6,4},{7,5},{8,10},{9,11},{10,... | collective-permute-start | bytes 1179656 | tf_op jit(solution)/shard_map/ppermute | solution.py:985
  114.6 3.9 %collective-permute-start.4 = (bf16[512,768]{1,0:T(8,128)(2,1)}, bf16[512,768]{1,0:T(8,128)(2,1)S(1)}, u32[]{:S(2)}, u32[]{:S(2)}) collective-permute-start(bf16[512,768]{1,0:T(8,128)(2,1)} %get-tuple-element.164), channel_id=1, source_target_pairs={{0,1},{1,0},{2,3},{3,2},{4,5},{5,4},{6,7},{7,6},{8,9},{9,8},{10,11... | collective-permute-start | bytes 2359304 | tf_op jit(solution)/shard_map/ppermute | solution.py:985
  143.6 13.3 %all-to-all-start.1 = ((f32[32,8,128]{2,1,0:T(8,128)}), f32[32,8,128]{2,1,0:T(8,128)S(1)}, u32[]{:S(2)}, u32[]{:S(2)}) async-start(f32[32,8,128]{2,1,0:T(8,128)} %get-tuple-element.87), calls=%async_computation.1 | async-start | bytes 262144 | tf_op jit(solution)/shard_map/all_to_all | solution.py:1170
  157.0 0.7 copy-start.6
  175.4 46.6 %all-to-all-start.2 = ((bf16[32,32,576]{2,1,0:T(8,128)(2,1)}), bf16[32,32,576]{2,1,0:T(8,128)(2,1)}, u32[]{:S(2)}, u32[]{:S(2)}) async-start(bf16[32,32,576]{2,1,0:T(8,128)(2,1)} %get-tuple-element.132), calls=%async_computation.2 | async-start | bytes 2621440 | tf_op jit(solution)/shard_map/all_to_all | solution.py:1180
  179.0 13.9 %collective-permute-start.5 = (bf16[2,2,4,48,768]{4,3,2,1,0:T(8,128)(2,1)}, bf16[2,2,4,48,768]{4,3,2,1,0:T(8,128)(2,1)}, u32[]{:S(2)}, u32[]{:S(2)}) collective-permute-start(bf16[2,2,4,48,768]{4,3,2,1,0:T(8,128)(2,1)} %get-tuple-element.111), channel_id=1, source_target_pairs={{0,1},{1,0},{2,3},{3,2},{4,5},{5,4},{6,7},{7,6},{8,9},{9,8},{10,11... | collective-permute-start | bytes 3538952 | tf_op jit(solution)/shard_map/ppermute | solution.py:985
  179.1 13.8 %collective-permute-start.6 = (bf16[2,2,4,48,768]{4,3,2,1,0:T(8,128)(2,1)}, bf16[2,2,4,48,768]{4,3,2,1,0:T(8,128)(2,1)}, u32[]{:S(2)}, u32[]{:S(2)}) collective-permute-start(bf16[2,2,4,48,768]{4,3,2,1,0:T(8,128)(2,1)} %get-tuple-element.113), channel_id=1, source_target_pairs={{0,1},{1,0},{2,3},{3,2},{4,5},{5,4},{6,7},{7,6},{8,9},{9,8},{10,11... | collective-permute-start | bytes 3538952 | tf_op jit(solution)/shard_map/ppermute | solution.py:985
  179.6 13.3 %copy-start = (bf16[2,2,4,48,768]{4,3,2,1,0:T(8,128)(2,1)S(1)}, bf16[2,2,4,48,768]{4,3,2,1,0:T(8,128)(2,1)}, u32[]{:S(2)}) copy-start(bf16[2,2,4,48,768]{4,3,2,1,0:T(8,128)(2,1)} %get-tuple-element.110) | copy-start | bytes 3538948
  192.3 7.6 %collective-permute-start.7 = (bf16[2,2,4,48,768]{4,3,2,1,0:T(8,128)(2,1)}, bf16[2,2,4,48,768]{4,3,2,1,0:T(8,128)(2,1)S(1)}, u32[]{:S(2)}, u32[]{:S(2)}) collective-permute-start(bf16[2,2,4,48,768]{4,3,2,1,0:T(8,128)(2,1)} %get-tuple-element.107), channel_id=1, source_target_pairs={{0,1},{1,0},{2,3},{3,2},{4,5},{5,4},{6,7},{7,6},{8,9},{9,8},{10,11... | collective-permute-start | bytes 3538952 | tf_op jit(solution)/shard_map/ppermute | solution.py:985
  192.5 7.4 %collective-permute-start.8 = (bf16[2,2,4,48,768]{4,3,2,1,0:T(8,128)(2,1)}, bf16[2,2,4,48,768]{4,3,2,1,0:T(8,128)(2,1)S(1)}, u32[]{:S(2)}, u32[]{:S(2)}) collective-permute-start(bf16[2,2,4,48,768]{4,3,2,1,0:T(8,128)(2,1)} %get-tuple-element.109), channel_id=1, source_target_pairs={{0,1},{1,0},{2,3},{3,2},{4,5},{5,4},{6,7},{7,6},{8,9},{9,8},{10,11... | collective-permute-start | bytes 3538952 | tf_op jit(solution)/shard_map/ppermute | solution.py:985
  192.9 1.3 copy-start.1
  194.2 5.7 %copy-start.2 = (bf16[2,2,4,48,768]{4,3,2,1,0:T(8,128)(2,1)S(1)}, bf16[2,2,4,48,768]{4,3,2,1,0:T(8,128)(2,1)}, u32[]{:S(2)}) copy-start(bf16[2,2,4,48,768]{4,3,2,1,0:T(8,128)(2,1)} %get-tuple-element.119) | copy-start | bytes 3538948
  194.2 5.7 %copy-start.3 = (bf16[2,2,4,48,768]{4,3,2,1,0:T(8,128)(2,1)S(1)}, bf16[2,2,4,48,768]{4,3,2,1,0:T(8,128)(2,1)}, u32[]{:S(2)}) copy-start(bf16[2,2,4,48,768]{4,3,2,1,0:T(8,128)(2,1)} %get-tuple-element.120) | copy-start | bytes 3538948
  197.0 4.6 %copy-start.4 = (bf16[8,48,768]{2,1,0:T(8,128)(2,1)}, bf16[8,48,768]{2,1,0:T(8,128)(2,1)S(1)}, u32[]{:S(2)}) copy-start(bf16[8,48,768]{2,1,0:T(8,128)(2,1)S(1)} %get-tuple-element.116) | copy-start | bytes 1769476
  197.0 19.6 %collective-permute-start.9 = (bf16[2,4,48,768]{3,2,1,0:T(8,128)(2,1)}, bf16[2,4,48,768]{3,2,1,0:T(8,128)(2,1)}, u32[]{:S(2)}, u32[]{:S(2)}) collective-permute-start(bf16[2,4,48,768]{3,2,1,0:T(8,128)(2,1)} %bitcast.21), channel_id=1, source_target_pairs={{0,16},{1,17},{2,18},{3,19},{4,20},{5,21},{6,22},{7,23},{8,24},{9,... | collective-permute-start | bytes 1769480 | tf_op jit(solution)/shard_map/ppermute | solution.py:985
  198.4 18.7 %collective-permute-start.10 = (bf16[2,4,48,768]{3,2,1,0:T(8,128)(2,1)}, bf16[2,4,48,768]{3,2,1,0:T(8,128)(2,1)}, u32[]{:S(2)}, u32[]{:S(2)}) collective-permute-start(bf16[2,4,48,768]{3,2,1,0:T(8,128)(2,1)} %bitcast.23), channel_id=1, source_target_pairs={{0,2},{1,3},{2,0},{3,1},{4,6},{5,7},{6,4},{7,5},{8,10},{9,11},{10,... | collective-permute-start | bytes 1769480 | tf_op jit(solution)/shard_map/ppermute | solution.py:985
  201.6 27.6 %collective-permute-start.11 = (bf16[2,4,48,768]{3,2,1,0:T(8,128)(2,1)}, bf16[2,4,48,768]{3,2,1,0:T(8,128)(2,1)}, u32[]{:S(2)}, u32[]{:S(2)}) collective-permute-start(bf16[2,4,48,768]{3,2,1,0:T(8,128)(2,1)} %bitcast.29), channel_id=1, source_target_pairs={{0,16},{1,17},{2,18},{3,19},{4,20},{5,21},{6,22},{7,23},{8,24},{9,... | collective-permute-start | bytes 1769480 | tf_op jit(solution)/shard_map/ppermute | solution.py:985
  202.2 27.6 %collective-permute-start.12 = (bf16[2,4,48,768]{3,2,1,0:T(8,128)(2,1)}, bf16[2,4,48,768]{3,2,1,0:T(8,128)(2,1)}, u32[]{:S(2)}, u32[]{:S(2)}) collective-permute-start(bf16[2,4,48,768]{3,2,1,0:T(8,128)(2,1)} %bitcast.31), channel_id=1, source_target_pairs={{0,2},{1,3},{2,0},{3,1},{4,6},{5,7},{6,4},{7,5},{8,10},{9,11},{10,... | collective-permute-start | bytes 1769480 | tf_op jit(solution)/shard_map/ppermute | solution.py:985
  217.1 1.1 copy-start.5
  219.7 16.3 %collective-permute-start.13 = (bf16[4,48,768]{2,1,0:T(8,128)(2,1)S(1)}, bf16[4,48,768]{2,1,0:T(8,128)(2,1)S(1)}, u32[]{:S(2)}, u32[]{:S(2)}) collective-permute-start(bf16[4,48,768]{2,1,0:T(8,128)(2,1)S(1)} %get-tuple-element.137), channel_id=1, source_target_pairs={{0,2},{1,3},{2,0},{3,1},{4,6},{5,7},{6,4},{7,5},{8,10},{9,11},{10,... | collective-permute-start | bytes 884744 | tf_op jit(solution)/shard_map/ppermute | solution.py:985
  221.2 14.7 %collective-permute-start.14 = (bf16[4,48,768]{2,1,0:T(8,128)(2,1)S(1)}, bf16[4,48,768]{2,1,0:T(8,128)(2,1)S(1)}, u32[]{:S(2)}, u32[]{:S(2)}) collective-permute-start(bf16[4,48,768]{2,1,0:T(8,128)(2,1)S(1)} %get-tuple-element.139), channel_id=1, source_target_pairs={{0,16},{1,17},{2,18},{3,19},{4,20},{5,21},{6,22},{7,23},{8,24},{9,... | collective-permute-start | bytes 884744 | tf_op jit(solution)/shard_map/ppermute | solution.py:985
  231.3 10.5 %collective-permute-start.15 = (bf16[4,48,768]{2,1,0:T(8,128)(2,1)S(1)}, bf16[4,48,768]{2,1,0:T(8,128)(2,1)S(1)}, u32[]{:S(2)}, u32[]{:S(2)}) collective-permute-start(bf16[4,48,768]{2,1,0:T(8,128)(2,1)S(1)} %get-tuple-element.143), channel_id=1, source_target_pairs={{0,2},{1,3},{2,0},{3,1},{4,6},{5,7},{6,4},{7,5},{8,10},{9,11},{10,... | collective-permute-start | bytes 884744 | tf_op jit(solution)/shard_map/ppermute | solution.py:985
  232.8 8.9 %collective-permute-start.16 = (bf16[4,48,768]{2,1,0:T(8,128)(2,1)S(1)}, bf16[4,48,768]{2,1,0:T(8,128)(2,1)S(1)}, u32[]{:S(2)}, u32[]{:S(2)}) collective-permute-start(bf16[4,48,768]{2,1,0:T(8,128)(2,1)S(1)} %get-tuple-element.145), channel_id=1, source_target_pairs={{0,16},{1,17},{2,18},{3,19},{4,20},{5,21},{6,22},{7,23},{8,24},{9,... | collective-permute-start | bytes 884744 | tf_op jit(solution)/shard_map/ppermute | solution.py:985
  236.1 10.7 %collective-permute-start.17 = (bf16[2,48,1536]{2,1,0:T(8,128)(2,1)S(1)}, bf16[2,48,1536]{2,1,0:T(8,128)(2,1)S(1)}, u32[]{:S(2)}, u32[]{:S(2)}) collective-permute-start(bf16[2,48,1536]{2,1,0:T(8,128)(2,1)S(1)} %get-tuple-element.151), channel_id=1, source_target_pairs={{0,4},{1,5},{2,6},{3,7},{4,0},{5,1},{6,2},{7,3},{8,12},{9,13},{10,... | collective-permute-start | bytes 884744 | tf_op jit(solution)/shard_map/ppermute | solution.py:985
  241.9 8.9 %collective-permute-start.18 = (bf16[2,48,1536]{2,1,0:T(8,128)(2,1)S(1)}, bf16[2,48,1536]{2,1,0:T(8,128)(2,1)S(1)}, u32[]{:S(2)}, u32[]{:S(2)}) collective-permute-start(bf16[2,48,1536]{2,1,0:T(8,128)(2,1)S(1)} %get-tuple-element.155), channel_id=1, source_target_pairs={{0,4},{1,5},{2,6},{3,7},{4,0},{5,1},{6,2},{7,3},{8,12},{9,13},{10,... | collective-permute-start | bytes 884744 | tf_op jit(solution)/shard_map/ppermute | solution.py:985
  243.3 12.0 %all-to-all-start.3 = ((f32[32,8,128]{2,1,0:T(8,128)}), f32[32,8,128]{2,1,0:T(8,128)S(1)}, u32[]{:S(2)}, u32[]{:S(2)}) async-start(f32[32,8,128]{2,1,0:T(8,128)} %get-tuple-element.146), calls=%async_computation.3 | async-start | bytes 262144 | tf_op jit(solution)/shard_map/all_to_all | solution.py:1209
  246.9 16.5 %collective-permute-start.20 = (bf16[48,1536]{1,0:T(8,128)(2,1)S(1)}, bf16[48,1536]{1,0:T(8,128)(2,1)S(1)}, u32[]{:S(2)}, u32[]{:S(2)}) collective-permute-start(bf16[48,1536]{1,0:T(8,128)(2,1)S(1)} %get-tuple-element.158), channel_id=1, source_target_pairs={{0,8},{1,9},{2,10},{3,11},{4,12},{5,13},{6,14},{7,15},{8,0},{9,1},... | collective-permute-start | bytes 442376 | tf_op jit(solution)/shard_map/ppermute | solution.py:985
  250.8 15.2 %collective-permute-start.19 = (bf16[48,1536]{1,0:T(8,128)(2,1)S(1)}, bf16[48,1536]{1,0:T(8,128)(2,1)S(1)}, u32[]{:S(2)}, u32[]{:S(2)}) collective-permute-start(bf16[48,1536]{1,0:T(8,128)(2,1)S(1)} %get-tuple-element.161), channel_id=1, source_target_pairs={{0,8},{1,9},{2,10},{3,11},{4,12},{5,13},{6,14},{7,15},{8,0},{9,1},... | collective-permute-start | bytes 442376 | tf_op jit(solution)/shard_map/ppermute | solution.py:985
  255.4 11.4 %copy-start.9 = (f32[8,128]{1,0:T(8,128)}, f32[8,128]{1,0:T(8,128)S(1)}, u32[]{:S(2)}) copy-start(f32[8,128]{1,0:T(8,128)S(1)} %reduce_sum.29) | copy-start | bytes 12292
Sparse Core Ops, SparseCore 0:
  10.9 108.3 all-gather.2

commit v3 on v2

--- a/solution.py
+++ b/solution.py
@@ -65,7 +65,7 @@
 def gauss_tail(u):
     size = jnp.abs(u)
     t = 1.0 / (1.0 + (0.3275911 * 0.7071067811865476) * size)
-    bell = jnp.exp(-0.5 * (u * u))
+    bell = jnp.exp2(-0.7213475204444817 * (u * u))
     poly = 0.5 * 1.061405429 * t - 0.5 * 1.453152027
     poly = poly * t + 0.5 * 1.421413741
     poly = poly * t - 0.5 * 0.284496736
@@ -412,9 +412,9 @@
     def expand(i):
         at = pl.ds(pl.multiple_of(i * 256, 256), 256)
         u = dot(h2[...], wu[:, :, at].reshape(width, 256)) + ub[:, at].astype(F32)
-        tail, bell, size = gauss_tail(u)
-        act = jnp.maximum(u, 0.0) - size * tail
+        tail, bell, _ = gauss_tail(u)
         phi = jnp.where(u >= 0.0, 1.0 - tail, tail)
+        act = u * phi
         slope[:, at] = (phi + u * (bell * 0.3989422804014327)).astype(BF)
         sums = jnp.sum(act.reshape(texts, length, 256), axis=1)
         total[:, at] = sums
@@ -603,14 +603,6 @@
     dact[...] = dot(dm, natural(wd), 1, 1)
     saved[0].wait()
 
-    def slopes(i):
-        at = pl.ds(pl.multiple_of(i * 256, 256), 256)
-        spread = jnp.broadcast_to(dact[:, at].reshape(texts, 1, 256), (texts, length, 256))
-        part = (spread.reshape(rows, 256) * slope[:, at].astype(F32)).astype(BF)
-        du[:, at] = part
-        bias_up[:, at] = jnp.sum(part.astype(F32), axis=0, keepdims=True)
-
-    repeat(hidden // 256, slopes, 3)
     saved[1].wait()
     half = hidden // PX
     outs = (keep_a, send_a, keep_b, send_b)
@@ -620,10 +612,14 @@
         def grads(i):
             c = pl.multiple_of(i * 256, 256)
             for second in range(2):
-                part = du[:, pl.ds(pl.multiple_of(first + c + second * width, 256), 256)]
+                at = pl.ds(pl.multiple_of(first + c + second * width, 256), 256)
+                spread = jnp.broadcast_to(dact[:, at].reshape(texts, 1, 256), (texts, length, 256))
+                part = (spread.reshape(rows, 256) * slope[:, at].astype(F32)).astype(BF)
+                du[:, at] = part
+                bias_up[:, at] = jnp.sum(part.astype(F32), axis=0, keepdims=True)
                 put_grad(dot(h2_t[...], part), parts, x, c, second)
 
-        repeat(width // 256, grads)
+        repeat(width // 256, grads, 3)
         sent += start_grads(parts, outs, out_sem, x)
 
     v = vec[...].astype(F32)
@@ -783,7 +779,7 @@
             part = dqkv[:, pl.ds(pl.multiple_of(first + c, 128), 256)]
             put_grad(dot(h1_t[...], part), parts, x, c, 0)
 
-        repeat(width // 256, chunk)
+        repeat(width // 256, chunk, 3)
         part = dqkv[:, pl.ds(pl.multiple_of(first + width, 128), piece)]
         put_grad(dot(h1_t[...], part), parts, x, 0, 1)
         part = dz[:, pl.ds(pl.multiple_of(other * piece, 128), piece)]

time: 276 us -> 272 us (0.986)
  Pallas kernels: 128 us -> 123 us
    all_to_all x1, waiting for transfers between devices: 0.01 us -> 5.82 us  [body(): share = jnp.sum(lax.all_to_all(share, AXES, 0, 0, tiled=True), axis=0)]
    ppermute x21, waiting for transfers between devices: 55.4 us -> 50.6 us  [hop(): return lax.ppermute(array, AXES, shifted(x, y, z, core))]
  transfers between devices with their start and end apart: 26 -> 26, of which waited for: 14 -> 14; matrix products, arithmetic and copies ran while one was open for 8% -> 9% of each run, Pallas kernels for 31% -> 31%
where the time goes in v3:
time: 272 us; the launch traced here: 271 us
  Pallas kernels  123 us (45%)
  waiting for transfers between devices  59.2 us (22%)
  starting transfers between devices  45.1 us (17%)
  between operations  17.4 us (6%)
  local copies, waits for them, and re-layouts  17 us (6%)
  other arithmetic  6.66 us (2%)
    ppermute x21, waiting for transfers between devices, hop(): return lax.ppermute(array, AXES, shifted(x, y, z, core))  50.6 us
    pallas_call x1, Pallas kernels, image_forward(): pl.pallas_call(image_kernel, name='image_forward', grid=(pairs // group,)...  49.9 us
    ppermute x21, starting transfers between devices, hop(): return lax.ppermute(array, AXES, shifted(x, y, z, core))  25.2 us
    pallas_call x1, Pallas kernels, text_forward(): pl.pallas_call(functools.partial(text_forward_kernel, length), name='text...  22.3 us
    pallas_call x1, Pallas kernels, back_one(): pl.pallas_call(functools.partial(back_one_kernel, length, shard), name='b...  15.6 us
    pallas_call x1, Pallas kernels, back_two(): pl.pallas_call(functools.partial(back_two_kernel, length), name='back_two...  11.7 us
    pallas_call x1, Pallas kernels, back_third(): pl.pallas_call(functools.partial(back_third_kernel, shard[1]), name='back...  9 us
    pallas_call x4, Pallas kernels, fold(): pl.pallas_call(fold_kernel, name='fold', grid=(steps,), in_specs=[pair] *...  7.57 us
  transfers between devices with their start and end apart: 26, of which 14 were waited for; matrix products, arithmetic and copies ran while one was open for 9% of the time, Pallas kernels for 31%

profile of v3, /device:TPU:0, one launch (start us, length us, event | category | flops | bytes accessed | tf_op | source)
XLA Modules:
  0.0 271.0 jit_solution(5542684710065022896)
XLA Ops:
  7.2 1.9 pack_block.1
  9.1 0.7 reshape.221
  9.8 0.8 pad_maximum_fusion.3
  11.2 7.4 %all-to-all-start = ((bf16[16,8,72]{2,1,0:T(8,128)(2,1)}), bf16[16,8,72]{2,1,0:T(8,128)(2,1)S(1)}, u32[]{:S(2)}, u32[]{:S(2)}) async-start(bf16[16,8,72]{2,1,0:T(8,128)(2,1)} %broadcast_in_dim.42), calls=%async_computation | async-start | bytes 65536 | tf_op jit(solution)/shard_map/all_to_all | solution.py:1125
  18.6 1.3 reshape.224.ub
  19.9 49.9 %image_forward.1 = bf16[32,768]{1,0:T(8,128)(2,1)} custom-call(bf16[50,32,768]{2,1,0:T(8,128)(2,1)} %bitcast.63, bf16[768,2304]{1,0:T(8,128)(2,1)} %wq_h.1, bf16[768,768]{1,0:T(8,128)(2,1)} %wo_h.1, bf16[768,3072]{1,0:T(8,128)(2,1)} %wu_h.1, bf16[3072,768]{1,0:T(8,128)(2,1)} %wd_h.1, bf16[8,768]{1,0:T(8,128)(2,1)} %vec.1, bf16[1,3072]{1,0:T(2,128)(2,1)} %reshape.224.ub), custom_call_target="tpu_custom_call" | custom-call | flops 15099494400 | bytes 16613376 | tf_op jit(solution)/shard_map/image_forward/pallas_call | solution.py:229
  69.8 2.0 collective-permute-start
  72.5 4.6 %collective-permute-done = bf16[32,768]{1,0:T(8,128)(2,1)S(1)} collective-permute-done((bf16[32,768]{1,0:T(8,128)(2,1)}, bf16[32,768]{1,0:T(8,128)(2,1)S(1)}, u32[]{:S(2)}, u32[]{:S(2)}) %collective-permute-start) | collective-permute-done | bytes 49184 | tf_op jit(solution)/shard_map/ppermute | solution.py:981
  77.1 0.8 pad_maximum_fusion.2
  77.9 2.1 collective-permute-start.1
  80.0 1.4 constant_dynamic-update-slice_fusion.4
  81.4 11.6 %collective-permute-done.1 = bf16[64,768]{1,0:T(8,128)(2,1)S(1)} collective-permute-done((bf16[64,768]{1,0:T(8,128)(2,1)S(1)}, bf16[64,768]{1,0:T(8,128)(2,1)S(1)}, u32[]{:S(2)}, u32[]{:S(2)}) %collective-permute-start.1) | collective-permute-done | bytes 98336 | tf_op jit(solution)/shard_map/ppermute | solution.py:981
  93.0 0.8 pad_maximum_fusion.1
  93.8 1.5 collective-permute-start.2
  95.3 7.0 %collective-permute-done.2 = bf16[128,768]{1,0:T(8,128)(2,1)S(1)} collective-permute-done((bf16[128,768]{1,0:T(8,128)(2,1)S(1)}, bf16[128,768]{1,0:T(8,128)(2,1)S(1)}, u32[]{:S(2)}, u32[]{:S(2)}) %collective-permute-start.2) | collective-permute-done | bytes 196640 | tf_op jit(solution)/shard_map/ppermute | solution.py:981
  102.3 0.8 pad_maximum_fusion
  103.1 1.5 collective-permute-start.3
  105.9 0.7 constant_dynamic-update-slice_fusion.1
  106.6 6.7 %collective-permute-done.3 = bf16[256,768]{1,0:T(8,128)(2,1)S(1)} collective-permute-done((bf16[256,768]{1,0:T(8,128)(2,1)S(1)}, bf16[256,768]{1,0:T(8,128)(2,1)S(1)}, u32[]{:S(2)}, u32[]{:S(2)}) %collective-permute-start.3) | collective-permute-done | bytes 393248 | tf_op jit(solution)/shard_map/ppermute | solution.py:981
  113.3 0.8 constant_dynamic-update-slice_fusion
  114.3 0.7 reshape.246.live
  115.1 0.7 copy.36.own_group
  115.8 0.7 copy.35.own
  116.6 0.7 reshape.223.ub
  117.3 0.7 reshape.222.vec
  118.7 1.4 bitcast_select_fusion.images_i
  120.2 22.3 %text_forward.1 = (bf16[512,768]{1,0:T(8,128)(2,1)}, bf16[512,2304]{1,0:T(8,128)(2,1)}, bf16[512,768]{1,0:T(8,128)(2,1)}, f32[512,768]{1,0:T(8,128)}, bf16[512,7...) custom-call(bf16[512,768]{1,0:T(8,128)(2,1)} %bitcast.56, ...), custom_call_target="tpu_custom_call" | custom-call | flops 4831838208 | bytes 23592960 | tf_op jit(solution)/shard_map/text_forward/pallas_call | solution.py:446
  142.5 5.2 %all-to-all-start.1 = ((f32[32,8,128]{2,1,0:T(8,128)}), f32[32,8,128]{2,1,0:T(8,128)S(1)}, u32[]{:S(2)}, u32[]{:S(2)}) async-start(f32[32,8,128]{2,1,0:T(8,128)} %get-tuple-element.87), calls=%async_computation.1 | async-start | bytes 262144 | tf_op jit(solution)/shard_map/all_to_all | solution.py:1166
  149.0 0.7 pad_add_fusion.where
  149.7 3.5 %relative_rows.1 = (bf16[768,512]{1,0:T(8,128)(2,1)}, bf16[768,512]{1,0:T(8,128)(2,1)}, bf16[768,512]{1,0:T(8,128)(2,1)}) custom-call(s32[4]{0:T(128)} %pad_add_fusion.where, bf16[512,768]{1,0:T(8,128)(2,1)} %get-tuple-element.91.h1_i, bf16[512,768]{1,0:T(8,128)(2,1)} %get-tuple-element.92.h2_i, bf16[512,768]{1,0:T(8,128)(2,1)} %get-tuple-element.93.att_i), custom_call_target="tpu_custom_call" | custom-call | bytes 4718592 | tf_op jit(solution)/shard_map/relative_rows/pallas_call | solution.py:515
  153.3 2.7 all-to-all-done.1.row_all
  156.6 15.6 %back_one.1 = (bf16[32,32,576]{2,1,0:T(8,128)(2,1)}, bf16[2,2,4,48,768]{4,3,2,1,0:T(8,128)(2,1)}, bf16[2,2,4,48,768]{4,3,2,1,0:T(8,128)(2,1)}, bf16[2,2,4,48,768...) custom-call(s32[4]{0:T(128)} %pad_add_fusion.where, ...), custom_call_target="tpu_custom_call" | custom-call | flops 5435817984 | bytes 37748736 | tf_op jit(solution)/shard_map/back_one/pallas_call | solution.py:673
  172.2 3.6 %all-to-all-start.2 = ((bf16[32,32,576]{2,1,0:T(8,128)(2,1)}), bf16[32,32,576]{2,1,0:T(8,128)(2,1)}, u32[]{:S(2)}, u32[]{:S(2)}) async-start(bf16[32,32,576]{2,1,0:T(8,128)(2,1)} %get-tuple-element.132), calls=%async_computation.2 | async-start | bytes 2621440 | tf_op jit(solution)/shard_map/all_to_all | solution.py:1176
  176.4 11.7 %back_two.1 = (bf16[512,2304]{1,0:T(8,128)(2,1)}, bf16[2,2,4,48,768]{4,3,2,1,0:T(8,128)(2,1)}, bf16[2,2,4,48,768]{4,3,2,1,0:T(8,128)(2,1)}, bf16[2,2,4,48,768]{4...) custom-call(s32[4]{0:T(128)} %pad_add_fusion.where, ...), custom_call_target="tpu_custom_call" | custom-call | flops 3422552064 | bytes 7864320 | tf_op jit(solution)/shard_map/back_two/pallas_call | solution.py:795
  188.7 1.3 copy-done.1
  190.0 2.8 %fold.4 = (bf16[8,48,768]{2,1,0:T(8,128)(2,1)S(1)}, bf16[8,48,768]{2,1,0:T(8,128)(2,1)}, bf16[8,48,768]{2,1,0:T(8,128)(2,1)S(1)}, bf16[8,48,768]{2,1,0:T(8,128)(2,1)}) custom-call(bf16[2,8,48,768]{3,2,1,0:T(8,128)(2,1)S(1)} %bitcast.42, bf16[2,8,48,768]{3,2,1,0:T(8,128)(2,1)} %bitcast.17.a_new, bf16[2,8,48,768]{3,2,1,0:T(8,128)(2,1)S(1)} %bitcast.43, ...), custom_call_target="tpu_custom_call" | custom-call | flops 1179648 | bytes 7077888 | tf_op jit(solution)/shard_map/fold/pallas_call | solution.py:914
  192.8 1.4 collective-permute-start.9
  194.2 1.5 collective-permute-start.10
  195.7 1.7 fold.5
  198.6 9.0 %back_third.1 = (f32[512,768]{1,0:T(8,128)}, f32[32,8,128]{2,1,0:T(8,128)}) custom-call(f32[512,768]{1,0:T(8,128)} %get-tuple-element.97.dr1_i, bf16[512,2304]{1,0:T(8,128)(2,1)} %get-tuple-element.125.dqkv_i, bf16[512,768]{1,0:T(8,128)(2,1)} %bitcast.57, bf16[32,576,384]{2,1,0:T(8,128)(2,1)} %bitcast.54, bf16[8,768]{1,0:T(8,128)(2,1)} %reshape.222.vec, ...), custom_call_target="tpu_custom_call" | custom-call | flops 1811939328 | bytes 8257536 | tf_op jit(solution)/shard_map/back_third/pallas_call | solution.py:874
  207.6 5.2 %collective-permute-done.9.a_new = bf16[2,4,48,768]{3,2,1,0:T(8,128)(2,1)} collective-permute-done((bf16[2,4,48,768]{3,2,1,0:T(8,128)(2,1)}, bf16[2,4,48,768]{3,2,1,0:T(8,128)(2,1)}, u32[]{:S(2)}, u32[]{:S(2)}) %collective-permute-start.9) | collective-permute-done | bytes 589856 | tf_op jit(solution)/shard_map/ppermute | solution.py:981
  212.8 0.7 collective-permute-done.10.b_new
  213.5 1.1 copy-done.5
  214.6 1.5 fold.6
  216.1 1.0 collective-permute-start.13
  217.0 0.8 collective-permute-start.14
  217.8 2.4 fusion
  220.2 5.2 %collective-permute-done.11.a_new = bf16[2,4,48,768]{3,2,1,0:T(8,128)(2,1)} collective-permute-done((bf16[2,4,48,768]{3,2,1,0:T(8,128)(2,1)}, bf16[2,4,48,768]{3,2,1,0:T(8,128)(2,1)}, u32[]{:S(2)}, u32[]{:S(2)}) %collective-permute-start.11) | collective-permute-done | bytes 589856 | tf_op jit(solution)/shard_map/ppermute | solution.py:981
  225.5 0.7 collective-permute-done.12.b_new
  226.1 1.5 fold.7
  227.6 1.0 collective-permute-start.15
  228.6 0.8 collective-permute-start.16
  229.4 3.0 %collective-permute-done.13.a_new = bf16[4,48,768]{2,1,0:T(8,128)(2,1)S(1)} collective-permute-done((bf16[4,48,768]{2,1,0:T(8,128)(2,1)S(1)}, bf16[4,48,768]{2,1,0:T(8,128)(2,1)S(1)}, u32[]{:S(2)}, u32[]{:S(2)}) %collective-permute-start.13) | collective-permute-done | bytes 294944 | tf_op jit(solution)/shard_map/ppermute | solution.py:981
  232.5 1.4 collective-permute-start.17
  233.9 3.9 %collective-permute-done.15.a_new = bf16[4,48,768]{2,1,0:T(8,128)(2,1)S(1)} collective-permute-done((bf16[4,48,768]{2,1,0:T(8,128)(2,1)S(1)}, bf16[4,48,768]{2,1,0:T(8,128)(2,1)S(1)}, u32[]{:S(2)}, u32[]{:S(2)}) %collective-permute-start.15) | collective-permute-done | bytes 294944 | tf_op jit(solution)/shard_map/ppermute | solution.py:981
  238.0 1.5 collective-permute-start.18
  239.4 3.6 %all-to-all-start.3 = ((f32[32,8,128]{2,1,0:T(8,128)}), f32[32,8,128]{2,1,0:T(8,128)S(1)}, u32[]{:S(2)}, u32[]{:S(2)}) async-start(f32[32,8,128]{2,1,0:T(8,128)} %get-tuple-element.146), calls=%async_computation.3 | async-start | bytes 262144 | tf_op jit(solution)/shard_map/all_to_all | solution.py:1205
  243.1 2.7 %collective-permute-start.20 = (bf16[48,1536]{1,0:T(8,128)(2,1)S(1)}, bf16[48,1536]{1,0:T(8,128)(2,1)S(1)}, u32[]{:S(2)}, u32[]{:S(2)}) collective-permute-start(bf16[48,1536]{1,0:T(8,128)(2,1)S(1)} %get-tuple-element.158), channel_id=1, source_target_pairs={{0,8},{1,9},{2,10},{3,11},{4,12},{5,13},{6,14},{7,15},{8,0},{9,1},... | collective-permute-start | bytes 442376 | tf_op jit(solution)/shard_map/ppermute | solution.py:981
  246.5 3.8 %collective-permute-start.19 = (bf16[48,1536]{1,0:T(8,128)(2,1)S(1)}, bf16[48,1536]{1,0:T(8,128)(2,1)S(1)}, u32[]{:S(2)}, u32[]{:S(2)}) collective-permute-start(bf16[48,1536]{1,0:T(8,128)(2,1)S(1)} %get-tuple-element.161), channel_id=1, source_target_pairs={{0,8},{1,9},{2,10},{3,11},{4,12},{5,13},{6,14},{7,15},{8,0},{9,1},... | collective-permute-start | bytes 442376 | tf_op jit(solution)/shard_map/ppermute | solution.py:981
  250.3 1.2 slice.29
  251.5 5.8 %all-to-all-done.3 = f32[32,8,128]{2,1,0:T(8,128)S(1)} async-done(((f32[32,8,128]{2,1,0:T(8,128)}), f32[32,8,128]{2,1,0:T(8,128)S(1)}, u32[]{:S(2)}, u32[]{:S(2)}) %all-to-all-start.3) | async-done | bytes 131104 | tf_op jit(solution)/shard_map/all_to_all | solution.py:1205
  260.0 0.7 total.3
  260.7 1.5 collective-permute-done.19.new
  262.3 0.7 total.2
  (72 shorter events, 9.8 us)
Async XLA Ops:
  7.2 113.0 %all-gather.3.cloned.1.call-start = ((), (), s32[]{:S(2)}) async-start(), calls=%async_computation.4 | async-start | bytes 14598144 | tf_op jit(solution)/shard_map/all_gather | solution.py:1068
  11.2 105.3 %all-to-all-start = ((bf16[16,8,72]{2,1,0:T(8,128)(2,1)}), bf16[16,8,72]{2,1,0:T(8,128)(2,1)S(1)}, u32[]{:S(2)}, u32[]{:S(2)}) async-start(bf16[16,8,72]{2,1,0:T(8,128)(2,1)} %broadcast_in_dim.42), calls=%async_computation | async-start | bytes 65536 | tf_op jit(solution)/shard_map/all_to_all | solution.py:1125
  19.9 51.9 %copy-start.10 = (s32[32]{0:T(128)S(1)}, s32[32]{0:T(128)}, u32[]{:S(2)}) copy-start(s32[32]{0:T(128)} %param.30) | copy-start | bytes 388
  19.9 52.0 %copy-start.7 = (s32[1024]{0:T(1024)S(1)}, s32[1024]{0:T(1024)}, u32[]{:S(2)}) copy-start(s32[1024]{0:T(1024)} %param.31) | copy-start | bytes 12292
  69.8 7.3 %collective-permute-start = (bf16[32,768]{1,0:T(8,128)(2,1)}, bf16[32,768]{1,0:T(8,128)(2,1)S(1)}, u32[]{:S(2)}, u32[]{:S(2)}) collective-permute-start(bf16[32,768]{1,0:T(8,128)(2,1)} %image_forward.1), channel_id=1, source_target_pairs={{0,4},{1,5},{2,6},{3,7},{4,0},{5,1},{6,2},{7,3},{8,12},{9,13},{10,... | collective-permute-start | bytes 147464 | tf_op jit(solution)/shard_map/ppermute | solution.py:981
  77.9 15.1 %collective-permute-start.1 = (bf16[64,768]{1,0:T(8,128)(2,1)S(1)}, bf16[64,768]{1,0:T(8,128)(2,1)S(1)}, u32[]{:S(2)}, u32[]{:S(2)}) collective-permute-start(bf16[64,768]{1,0:T(8,128)(2,1)S(1)} %pad_maximum_fusion.2), channel_id=1, source_target_pairs={{0,8},{1,9},{2,10},{3,11},{4,12},{5,13},{6,14},{7,15},{8,0},{9,1},... | collective-permute-start | bytes 294920 | tf_op jit(solution)/shard_map/ppermute | solution.py:981
  93.8 8.5 %collective-permute-start.2 = (bf16[128,768]{1,0:T(8,128)(2,1)S(1)}, bf16[128,768]{1,0:T(8,128)(2,1)S(1)}, u32[]{:S(2)}, u32[]{:S(2)}) collective-permute-start(bf16[128,768]{1,0:T(8,128)(2,1)S(1)} %pad_maximum_fusion.1), channel_id=1, source_target_pairs={{0,16},{1,17},{2,18},{3,19},{4,20},{5,21},{6,22},{7,23},{8,24},{9,... | collective-permute-start | bytes 589832 | tf_op jit(solution)/shard_map/ppermute | solution.py:981
  95.3 21.3 %copy-start.8 = (f32[1024]{0:T(1024)}, f32[1024]{0:T(1024)S(1)}, u32[]{:S(2)}) copy-start(f32[1024]{0:T(1024)S(1)} %broadcast_maximum_fusion) | copy-start | bytes 12292
  103.1 10.2 %collective-permute-start.3 = (bf16[256,768]{1,0:T(8,128)(2,1)S(1)}, bf16[256,768]{1,0:T(8,128)(2,1)S(1)}, u32[]{:S(2)}, u32[]{:S(2)}) collective-permute-start(bf16[256,768]{1,0:T(8,128)(2,1)S(1)} %pad_maximum_fusion), channel_id=1, source_target_pairs={{0,2},{1,3},{2,0},{3,1},{4,6},{5,7},{6,4},{7,5},{8,10},{9,11},{10,... | collective-permute-start | bytes 1179656 | tf_op jit(solution)/shard_map/ppermute | solution.py:981
  114.1 3.9 %collective-permute-start.4 = (bf16[512,768]{1,0:T(8,128)(2,1)}, bf16[512,768]{1,0:T(8,128)(2,1)S(1)}, u32[]{:S(2)}, u32[]{:S(2)}) collective-permute-start(bf16[512,768]{1,0:T(8,128)(2,1)} %get-tuple-element.164), channel_id=1, source_target_pairs={{0,1},{1,0},{2,3},{3,2},{4,5},{5,4},{6,7},{7,6},{8,9},{9,8},{10,11... | collective-permute-start | bytes 2359304 | tf_op jit(solution)/shard_map/ppermute | solution.py:981
  142.5 13.5 %all-to-all-start.1 = ((f32[32,8,128]{2,1,0:T(8,128)}), f32[32,8,128]{2,1,0:T(8,128)S(1)}, u32[]{:S(2)}, u32[]{:S(2)}) async-start(f32[32,8,128]{2,1,0:T(8,128)} %get-tuple-element.87), calls=%async_computation.1 | async-start | bytes 262144 | tf_op jit(solution)/shard_map/all_to_all | solution.py:1166
  155.9 0.7 copy-start.6
  172.2 45.6 %all-to-all-start.2 = ((bf16[32,32,576]{2,1,0:T(8,128)(2,1)}), bf16[32,32,576]{2,1,0:T(8,128)(2,1)}, u32[]{:S(2)}, u32[]{:S(2)}) async-start(bf16[32,32,576]{2,1,0:T(8,128)(2,1)} %get-tuple-element.132), calls=%async_computation.2 | async-start | bytes 2621440 | tf_op jit(solution)/shard_map/all_to_all | solution.py:1176
  175.8 12.8 %collective-permute-start.5 = (bf16[2,2,4,48,768]{4,3,2,1,0:T(8,128)(2,1)}, bf16[2,2,4,48,768]{4,3,2,1,0:T(8,128)(2,1)}, u32[]{:S(2)}, u32[]{:S(2)}) collective-permute-start(bf16[2,2,4,48,768]{4,3,2,1,0:T(8,128)(2,1)} %get-tuple-element.111), channel_id=1, source_target_pairs={{0,1},{1,0},{2,3},{3,2},{4,5},{5,4},{6,7},{7,6},{8,9},{9,8},{10,11... | collective-permute-start | bytes 3538952 | tf_op jit(solution)/shard_map/ppermute | solution.py:981
  175.9 12.8 %collective-permute-start.6 = (bf16[2,2,4,48,768]{4,3,2,1,0:T(8,128)(2,1)}, bf16[2,2,4,48,768]{4,3,2,1,0:T(8,128)(2,1)}, u32[]{:S(2)}, u32[]{:S(2)}) collective-permute-start(bf16[2,2,4,48,768]{4,3,2,1,0:T(8,128)(2,1)} %get-tuple-element.113), channel_id=1, source_target_pairs={{0,1},{1,0},{2,3},{3,2},{4,5},{5,4},{6,7},{7,6},{8,9},{9,8},{10,11... | collective-permute-start | bytes 3538952 | tf_op jit(solution)/shard_map/ppermute | solution.py:981
  176.4 12.3 %copy-start = (bf16[2,2,4,48,768]{4,3,2,1,0:T(8,128)(2,1)S(1)}, bf16[2,2,4,48,768]{4,3,2,1,0:T(8,128)(2,1)}, u32[]{:S(2)}) copy-start(bf16[2,2,4,48,768]{4,3,2,1,0:T(8,128)(2,1)} %get-tuple-element.110) | copy-start | bytes 3538948
  188.1 7.6 %collective-permute-start.7 = (bf16[2,2,4,48,768]{4,3,2,1,0:T(8,128)(2,1)}, bf16[2,2,4,48,768]{4,3,2,1,0:T(8,128)(2,1)S(1)}, u32[]{:S(2)}, u32[]{:S(2)}) collective-permute-start(bf16[2,2,4,48,768]{4,3,2,1,0:T(8,128)(2,1)} %get-tuple-element.107), channel_id=1, source_target_pairs={{0,1},{1,0},{2,3},{3,2},{4,5},{5,4},{6,7},{7,6},{8,9},{9,8},{10,11... | collective-permute-start | bytes 3538952 | tf_op jit(solution)/shard_map/ppermute | solution.py:981
  188.2 7.4 %collective-permute-start.8 = (bf16[2,2,4,48,768]{4,3,2,1,0:T(8,128)(2,1)}, bf16[2,2,4,48,768]{4,3,2,1,0:T(8,128)(2,1)S(1)}, u32[]{:S(2)}, u32[]{:S(2)}) collective-permute-start(bf16[2,2,4,48,768]{4,3,2,1,0:T(8,128)(2,1)} %get-tuple-element.109), channel_id=1, source_target_pairs={{0,1},{1,0},{2,3},{3,2},{4,5},{5,4},{6,7},{7,6},{8,9},{9,8},{10,11... | collective-permute-start | bytes 3538952 | tf_op jit(solution)/shard_map/ppermute | solution.py:981
  188.7 1.3 copy-start.1
  189.9 5.7 %copy-start.2 = (bf16[2,2,4,48,768]{4,3,2,1,0:T(8,128)(2,1)S(1)}, bf16[2,2,4,48,768]{4,3,2,1,0:T(8,128)(2,1)}, u32[]{:S(2)}) copy-start(bf16[2,2,4,48,768]{4,3,2,1,0:T(8,128)(2,1)} %get-tuple-element.119) | copy-start | bytes 3538948
  189.9 5.7 %copy-start.3 = (bf16[2,2,4,48,768]{4,3,2,1,0:T(8,128)(2,1)S(1)}, bf16[2,2,4,48,768]{4,3,2,1,0:T(8,128)(2,1)}, u32[]{:S(2)}) copy-start(bf16[2,2,4,48,768]{4,3,2,1,0:T(8,128)(2,1)} %get-tuple-element.120) | copy-start | bytes 3538948
  192.8 4.6 %copy-start.4 = (bf16[8,48,768]{2,1,0:T(8,128)(2,1)}, bf16[8,48,768]{2,1,0:T(8,128)(2,1)S(1)}, u32[]{:S(2)}) copy-start(bf16[8,48,768]{2,1,0:T(8,128)(2,1)S(1)} %get-tuple-element.116) | copy-start | bytes 1769476
  192.8 20.0 %collective-permute-start.9 = (bf16[2,4,48,768]{3,2,1,0:T(8,128)(2,1)}, bf16[2,4,48,768]{3,2,1,0:T(8,128)(2,1)}, u32[]{:S(2)}, u32[]{:S(2)}) collective-permute-start(bf16[2,4,48,768]{3,2,1,0:T(8,128)(2,1)} %bitcast.21), channel_id=1, source_target_pairs={{0,16},{1,17},{2,18},{3,19},{4,20},{5,21},{6,22},{7,23},{8,24},{9,... | collective-permute-start | bytes 1769480 | tf_op jit(solution)/shard_map/ppermute | solution.py:981
  194.2 19.3 %collective-permute-start.10 = (bf16[2,4,48,768]{3,2,1,0:T(8,128)(2,1)}, bf16[2,4,48,768]{3,2,1,0:T(8,128)(2,1)}, u32[]{:S(2)}, u32[]{:S(2)}) collective-permute-start(bf16[2,4,48,768]{3,2,1,0:T(8,128)(2,1)} %bitcast.23), channel_id=1, source_target_pairs={{0,2},{1,3},{2,0},{3,1},{4,6},{5,7},{6,4},{7,5},{8,10},{9,11},{10,... | collective-permute-start | bytes 1769480 | tf_op jit(solution)/shard_map/ppermute | solution.py:981
  197.4 28.1 %collective-permute-start.11 = (bf16[2,4,48,768]{3,2,1,0:T(8,128)(2,1)}, bf16[2,4,48,768]{3,2,1,0:T(8,128)(2,1)}, u32[]{:S(2)}, u32[]{:S(2)}) collective-permute-start(bf16[2,4,48,768]{3,2,1,0:T(8,128)(2,1)} %bitcast.29), channel_id=1, source_target_pairs={{0,16},{1,17},{2,18},{3,19},{4,20},{5,21},{6,22},{7,23},{8,24},{9,... | collective-permute-start | bytes 1769480 | tf_op jit(solution)/shard_map/ppermute | solution.py:981
  197.9 28.2 %collective-permute-start.12 = (bf16[2,4,48,768]{3,2,1,0:T(8,128)(2,1)}, bf16[2,4,48,768]{3,2,1,0:T(8,128)(2,1)}, u32[]{:S(2)}, u32[]{:S(2)}) collective-permute-start(bf16[2,4,48,768]{3,2,1,0:T(8,128)(2,1)} %bitcast.31), channel_id=1, source_target_pairs={{0,2},{1,3},{2,0},{3,1},{4,6},{5,7},{6,4},{7,5},{8,10},{9,11},{10,... | collective-permute-start | bytes 1769480 | tf_op jit(solution)/shard_map/ppermute | solution.py:981
  213.5 1.1 copy-start.5
  216.1 16.3 %collective-permute-start.13 = (bf16[4,48,768]{2,1,0:T(8,128)(2,1)S(1)}, bf16[4,48,768]{2,1,0:T(8,128)(2,1)S(1)}, u32[]{:S(2)}, u32[]{:S(2)}) collective-permute-start(bf16[4,48,768]{2,1,0:T(8,128)(2,1)S(1)} %get-tuple-element.137), channel_id=1, source_target_pairs={{0,2},{1,3},{2,0},{3,1},{4,6},{5,7},{6,4},{7,5},{8,10},{9,11},{10,... | collective-permute-start | bytes 884744 | tf_op jit(solution)/shard_map/ppermute | solution.py:981
  217.0 15.3 %collective-permute-start.14 = (bf16[4,48,768]{2,1,0:T(8,128)(2,1)S(1)}, bf16[4,48,768]{2,1,0:T(8,128)(2,1)S(1)}, u32[]{:S(2)}, u32[]{:S(2)}) collective-permute-start(bf16[4,48,768]{2,1,0:T(8,128)(2,1)S(1)} %get-tuple-element.139), channel_id=1, source_target_pairs={{0,16},{1,17},{2,18},{3,19},{4,20},{5,21},{6,22},{7,23},{8,24},{9,... | collective-permute-start | bytes 884744 | tf_op jit(solution)/shard_map/ppermute | solution.py:981
  227.6 10.2 %collective-permute-start.15 = (bf16[4,48,768]{2,1,0:T(8,128)(2,1)S(1)}, bf16[4,48,768]{2,1,0:T(8,128)(2,1)S(1)}, u32[]{:S(2)}, u32[]{:S(2)}) collective-permute-start(bf16[4,48,768]{2,1,0:T(8,128)(2,1)S(1)} %get-tuple-element.143), channel_id=1, source_target_pairs={{0,2},{1,3},{2,0},{3,1},{4,6},{5,7},{6,4},{7,5},{8,10},{9,11},{10,... | collective-permute-start | bytes 884744 | tf_op jit(solution)/shard_map/ppermute | solution.py:981
  228.6 9.2 %collective-permute-start.16 = (bf16[4,48,768]{2,1,0:T(8,128)(2,1)S(1)}, bf16[4,48,768]{2,1,0:T(8,128)(2,1)S(1)}, u32[]{:S(2)}, u32[]{:S(2)}) collective-permute-start(bf16[4,48,768]{2,1,0:T(8,128)(2,1)S(1)} %get-tuple-element.145), channel_id=1, source_target_pairs={{0,16},{1,17},{2,18},{3,19},{4,20},{5,21},{6,22},{7,23},{8,24},{9,... | collective-permute-start | bytes 884744 | tf_op jit(solution)/shard_map/ppermute | solution.py:981
  232.5 10.6 %collective-permute-start.17 = (bf16[2,48,1536]{2,1,0:T(8,128)(2,1)S(1)}, bf16[2,48,1536]{2,1,0:T(8,128)(2,1)S(1)}, u32[]{:S(2)}, u32[]{:S(2)}) collective-permute-start(bf16[2,48,1536]{2,1,0:T(8,128)(2,1)S(1)} %get-tuple-element.151), channel_id=1, source_target_pairs={{0,4},{1,5},{2,6},{3,7},{4,0},{5,1},{6,2},{7,3},{8,12},{9,13},{10,... | collective-permute-start | bytes 884744 | tf_op jit(solution)/shard_map/ppermute | solution.py:981
  238.0 8.5 %collective-permute-start.18 = (bf16[2,48,1536]{2,1,0:T(8,128)(2,1)S(1)}, bf16[2,48,1536]{2,1,0:T(8,128)(2,1)S(1)}, u32[]{:S(2)}, u32[]{:S(2)}) collective-permute-start(bf16[2,48,1536]{2,1,0:T(8,128)(2,1)S(1)} %get-tuple-element.155), channel_id=1, source_target_pairs={{0,4},{1,5},{2,6},{3,7},{4,0},{5,1},{6,2},{7,3},{8,12},{9,13},{10,... | collective-permute-start | bytes 884744 | tf_op jit(solution)/shard_map/ppermute | solution.py:981
  239.4 17.9 %all-to-all-start.3 = ((f32[32,8,128]{2,1,0:T(8,128)}), f32[32,8,128]{2,1,0:T(8,128)S(1)}, u32[]{:S(2)}, u32[]{:S(2)}) async-start(f32[32,8,128]{2,1,0:T(8,128)} %get-tuple-element.146), calls=%async_computation.3 | async-start | bytes 262144 | tf_op jit(solution)/shard_map/all_to_all | solution.py:1205
  243.1 16.9 %collective-permute-start.20 = (bf16[48,1536]{1,0:T(8,128)(2,1)S(1)}, bf16[48,1536]{1,0:T(8,128)(2,1)S(1)}, u32[]{:S(2)}, u32[]{:S(2)}) collective-permute-start(bf16[48,1536]{1,0:T(8,128)(2,1)S(1)} %get-tuple-element.158), channel_id=1, source_target_pairs={{0,8},{1,9},{2,10},{3,11},{4,12},{5,13},{6,14},{7,15},{8,0},{9,1},... | collective-permute-start | bytes 442376 | tf_op jit(solution)/shard_map/ppermute | solution.py:981
  246.5 15.7 %collective-permute-start.19 = (bf16[48,1536]{1,0:T(8,128)(2,1)S(1)}, bf16[48,1536]{1,0:T(8,128)(2,1)S(1)}, u32[]{:S(2)}, u32[]{:S(2)}) collective-permute-start(bf16[48,1536]{1,0:T(8,128)(2,1)S(1)} %get-tuple-element.161), channel_id=1, source_target_pairs={{0,8},{1,9},{2,10},{3,11},{4,12},{5,13},{6,14},{7,15},{8,0},{9,1},... | collective-permute-start | bytes 442376 | tf_op jit(solution)/shard_map/ppermute | solution.py:981
  257.3 5.6 %copy-start.9 = (f32[8,128]{1,0:T(8,128)}, f32[8,128]{1,0:T(8,128)S(1)}, u32[]{:S(2)}) copy-start(f32[8,128]{1,0:T(8,128)S(1)} %reduce_sum.29) | copy-start | bytes 12292
Sparse Core Ops, SparseCore 0:
  10.9 108.2 all-gather.2
